TPU v7x, 32 devices: a whole 2x2x4 slice. The times are simulated.
32 devices in a mesh: dp: 4 (over x, core), mp: 8 (over z, y).
Axes of the slice: x: 2, y: 2, z: 4, core: 2. Of those that a mesh axis runs over, the one named last changes fastest.
Arguments:
- layer_input: bfloat16 [8192, 2048], P(('dp', 'mp')), may hold values from -6 to 6
- cotangent: bfloat16 [8192, 2048], P(('dp', 'mp')), may hold values from -6 to 6
- segment_ids: int32 [8192], P('dp'), may hold values from 0 to 11, as said below
- token_valid: int32 [8192], P('dp'), may hold values from 0 to 1, as said below
- norm_attn: bfloat16 [2048], replicated, may hold values from 0.099609375 to 1.8984375
- norm_mlp: bfloat16 [2048], replicated, may hold values from 0.099609375 to 1.8984375
- base_qkv: bfloat16 [3, 2048, 2048], P(None, None, 'mp'), may hold values from -0.125 to 0.125
- base_attn_out: bfloat16 [2048, 2048], P('mp'), may hold values from -0.125 to 0.125
- base_gate_up: bfloat16 [2, 2048, 5632], P(None, None, 'mp'), may hold values from -0.125 to 0.125
- base_down: bfloat16 [5632, 2048], P('mp'), may hold values from -0.078125 to 0.078125
- rank_in_attn: float32 [4, 2048, 16], P(None, ('dp', 'mp')), may hold values from -0.125 to 0.125
- rank_out_attn: float32 [4, 16, 2048], P(None, None, ('dp', 'mp')), may hold values from -0.36 to 0.36
- magnitude_qkv: float32 [3, 2048], P(None, ('dp', 'mp')), may hold values from 0.7 to 1.4
- magnitude_out: float32 [2048], P(('dp', 'mp')), may hold values from 3 to 12
- rank_in_mlp: float32 [2, 2048, 16], P(None, ('dp', 'mp')), may hold values from -0.125 to 0.125
- rank_out_mlp: float32 [2, 16, 5632], P(None, None, ('dp', 'mp')), may hold values from -0.36 to 0.36
- magnitude_mlp: float32 [2, 5632], P(None, ('dp', 'mp')), may hold values from 0.7 to 1.4
- rank_in_down: float32 [5632, 16], P(('dp', 'mp')), may hold values from -0.078125 to 0.078125
- rank_out_down: float32 [16, 2048], P(None, ('dp', 'mp')), may hold values from -0.36 to 0.36
- magnitude_down: float32 [2048], P(('dp', 'mp')), may hold values from 1 to 3
Outputs:
- layer_output: bfloat16 [8192, 2048], P(('dp', 'mp'))
- input_grad: float32 [8192, 2048], P(('dp', 'mp'))
- grad_rank_in_attn: float32 [4, 2048, 16], P(None, ('dp', 'mp'))
- grad_rank_out_attn: float32 [4, 16, 2048], P(None, None, ('dp', 'mp'))
- grad_magnitude_qkv: float32 [3, 2048], P(None, ('dp', 'mp'))
- grad_magnitude_out: float32 [2048], P(('dp', 'mp'))
- grad_rank_in_mlp: float32 [2, 2048, 16], P(None, ('dp', 'mp'))
- grad_rank_out_mlp: float32 [2, 16, 5632], P(None, None, ('dp', 'mp'))
- grad_magnitude_mlp: float32 [2, 5632], P(None, ('dp', 'mp'))
- grad_rank_in_down: float32 [5632, 16], P(('dp', 'mp'))
- grad_rank_out_down: float32 [16, 2048], P(None, ('dp', 'mp'))
- grad_magnitude_down: float32 [2048], P(('dp', 'mp'))
Inputs may be any that keep to these rules, and one draw needn't show every extreme that they name: `segment_ids`: ids never decrease along a row of 2048 tokens (each segment is one contiguous run), and no two rows share an id. `token_valid`: padding forms a tail of each row of 2048 tokens.
All inputs are finite; a program needn't handle non-finite values.
Results may differ from a plain program's by a relative error of at most 0.024.
Values may be sent and summed in bfloat16 or wider, within the bound.
No kernel may reach another device: no remote copies, remote signals or barrier semaphores. Data moves between devices by JAX's collectives and lax.ppermute only.
A program may use at most 320 MiB of HBM per device.

v0:
```python
import jax
import jax.numpy as jnp
from jax import lax
from jax.sharding import PartitionSpec as P

HD = 128
R = 16
ALPHA = 32
S = 2048


EXACT = lax.Precision.HIGHEST
EPSILON = 1e-05
ROPE_BASE = 10000.0


def product(left, right):
    return jnp.dot(left, right, preferred_element_type=jnp.float32)


def contract_rows(left, right):
    return lax.dot_general(
        left, right, (((0,), (0,)), ((), ())), preferred_element_type=jnp.float32
    )


def contract_cols(left, right):
    return lax.dot_general(
        left, right, (((1,), (1,)), ((), ())), preferred_element_type=jnp.float32
    )


def positions_of(segments):
    total_len = segments.shape[0]
    steps_idx = jnp.arange(total_len, dtype=jnp.int32)
    earlier = jnp.concatenate([segments[:1] - 1, segments[:-1]])
    begins = (steps_idx % S == 0) | (segments != earlier)
    first_idx = lax.cummax(jnp.where(begins, steps_idx, 0), axis=0)
    return steps_idx - first_idx


def rotary_tables(positions):
    half_width = HD // 2
    inverse_freq = ROPE_BASE ** (-(2.0 * jnp.arange(half_width, dtype=jnp.float32)) / HD)
    angle = positions.astype(jnp.float32)[:, None] * inverse_freq[None, :]
    return (jnp.cos(angle)[:, None, :], jnp.sin(angle)[:, None, :])


def rotate(values, cosine, sine):
    half_width = values.shape[-1] // 2
    first_half = values[..., :half_width]
    second_half = values[..., half_width:]
    return jnp.concatenate(
        [first_half * cosine - second_half * sine, second_half * cosine + first_half * sine],
        axis=-1,
    )


def norm_forward(values):
    inverse = lax.rsqrt(jnp.mean(values * values, axis=-1, keepdims=True) + EPSILON)
    return (values * inverse, inverse)


def norm_backward(grad_normed, unit_vals, inverse, gain):
    scaled = grad_normed * gain
    return inverse * (scaled - unit_vals * jnp.mean(scaled * unit_vals, axis=-1, keepdims=True))


def merge_adapter(base, rank_in, rank_out):
    return base.astype(jnp.float32) + ALPHA / R * product(rank_in, rank_out)


def norms_of(merged):
    return jnp.sqrt(jnp.sum(merged * merged, axis=0))


def adapter_grads(grad_merged, merged, col_grad, norms, magnitude, rank_in, rank_out):
    corrected = grad_merged - merged * (col_grad * magnitude / (norms * norms * norms))[None, :]
    factor = ALPHA / R
    grad_in = factor * jnp.dot(corrected, rank_out.astype(jnp.float32).T, precision=EXACT)
    grad_out = factor * jnp.dot(rank_in.astype(jnp.float32).T, corrected, precision=EXACT)
    return (grad_in, grad_out)


def block_scores(queries, key_heads, segments, valid, number, block_len):
    first_row = number * block_len
    row_start = first_row // S * S
    query_blk = lax.dynamic_slice_in_dim(queries, first_row, block_len, 0)
    query_pos = first_row - row_start + jnp.arange(block_len, dtype=jnp.int32)
    key_pos = jnp.arange(S, dtype=jnp.int32)
    seg_query = lax.dynamic_slice_in_dim(segments, first_row, block_len, 0)
    allowed = (
        (seg_query[:, None] == segments[None, :])
        & (key_pos[None, :] <= query_pos[:, None])
        & ((valid[None, :] == 1) | (key_pos[None, :] == query_pos[:, None]))
    )
    scores = jnp.einsum("qhd,khd->hqk", query_blk, key_heads, preferred_element_type=jnp.float32)
    return (jnp.where(allowed[None], scores, -1e30), query_blk, key_heads, row_start, first_row)


def attention_forward(queries, key_heads, value_heads, segments, valid):
    block_len = min(512, S)
    blocks = queries.shape[0] // block_len

    def one_block(number):
        scores, query_blk, key_row, row_start, first_row = block_scores(
            queries, key_heads, segments, valid, number, block_len
        )
        row_max = jnp.max(scores, axis=-1, keepdims=True)
        exponent = jnp.exp(scores - row_max)
        row_total = jnp.sum(exponent, axis=-1, keepdims=True)
        attn_weights = exponent / row_total
        mixed = jnp.einsum(
            "hqk,khd->qhd",
            attn_weights.astype(jnp.bfloat16),
            value_heads,
            preferred_element_type=jnp.float32,
        )
        return (mixed, (row_max + jnp.log(row_total))[:, :, 0])

    mixed, log_norm = lax.map(one_block, jnp.arange(blocks, dtype=jnp.int32))
    return (mixed.reshape(queries.shape), log_norm)


def attention_backward(queries, key_heads, value_heads, grad_mixed, log_norm, segments, valid):
    block_len = min(512, S)
    blocks = queries.shape[0] // block_len
    zeros_like_keys = jnp.zeros(key_heads.shape, jnp.float32)

    def one_block(carry, number):
        grad_keys, grad_values = carry
        scores, query_blk, key_row, row_start, first_row = block_scores(
            queries, key_heads, segments, valid, number, block_len
        )
        attn_weights = jnp.exp(scores - log_norm[number][:, :, None])
        grad_blk = lax.dynamic_slice_in_dim(grad_mixed, first_row, block_len, 0)
        grad_weights = jnp.einsum(
            "qhd,khd->hqk", grad_blk, value_heads, preferred_element_type=jnp.float32
        )
        inner_sum = jnp.sum(attn_weights * grad_weights, axis=-1, keepdims=True)
        grad_scores = (attn_weights * (grad_weights - inner_sum)).astype(jnp.bfloat16)
        grad_query = jnp.einsum(
            "hqk,khd->qhd", grad_scores, key_row, preferred_element_type=jnp.float32
        )
        key_part = jnp.einsum(
            "hqk,qhd->khd", grad_scores, query_blk, preferred_element_type=jnp.float32
        )
        value_part = jnp.einsum(
            "hqk,qhd->khd",
            attn_weights.astype(jnp.bfloat16),
            grad_blk,
            preferred_element_type=jnp.float32,
        )
        grad_keys = grad_keys + key_part
        grad_values = grad_values + value_part
        return ((grad_keys, grad_values), grad_query)

    (grad_keys, grad_values), grad_query = lax.scan(
        one_block, (zeros_like_keys, zeros_like_keys), jnp.arange(blocks, dtype=jnp.int32)
    )
    return (grad_query.reshape(queries.shape), grad_keys, grad_values)


def on_device(
    layer_input,
    cotangent,
    segment_ids,
    token_valid,
    norm_attn,
    norm_mlp,
    base_qkv,
    base_attn_out,
    base_gate_up,
    base_down,
    rank_in_attn,
    rank_out_attn,
    magnitude_qkv,
    magnitude_out,
    rank_in_mlp,
    rank_out_mlp,
    magnitude_mlp,
    rank_in_down,
    rank_out_down,
    magnitude_down,
):
    my_index = lax.axis_index("mp")
    local_width = base_qkv.shape[2]
    local_hidden = base_gate_up.shape[2]
    model_width = layer_input.shape[1]
    hidden_width = rank_in_down.shape[0] * lax.axis_size(("dp", "mp"))
    group_tokens = segment_ids.shape[0]
    local_heads = local_width // HD
    query_scale = HD ** (-0.5)

    def local_part(array, width, axis):
        return lax.dynamic_slice_in_dim(array, my_index * width, width, axis)

    def place_local(shape, part, width, axis):
        return lax.dynamic_update_slice_in_dim(
            jnp.zeros(shape, jnp.float32), part, my_index * width, axis
        )

    (
        whole_in_attn,
        whole_out_attn,
        whole_mag_qkv,
        whole_mag_out,
        whole_in_mlp,
        whole_out_mlp,
        whole_mag_mlp,
        whole_in_down,
        whole_out_down,
        whole_mag_down,
    ) = (
        lax.all_gather(rank_in_attn.astype(jnp.bfloat16), ("dp", "mp"), axis=1, tiled=True),
        lax.all_gather(rank_out_attn.astype(jnp.bfloat16), ("dp", "mp"), axis=2, tiled=True),
        lax.all_gather(magnitude_qkv.astype(jnp.bfloat16), ("dp", "mp"), axis=1, tiled=True),
        lax.all_gather(magnitude_out.astype(jnp.bfloat16), ("dp", "mp"), axis=0, tiled=True),
        lax.all_gather(rank_in_mlp.astype(jnp.bfloat16), ("dp", "mp"), axis=1, tiled=True),
        lax.all_gather(rank_out_mlp.astype(jnp.bfloat16), ("dp", "mp"), axis=2, tiled=True),
        lax.all_gather(magnitude_mlp.astype(jnp.bfloat16), ("dp", "mp"), axis=1, tiled=True),
        lax.all_gather(rank_in_down.astype(jnp.bfloat16), ("dp", "mp"), axis=0, tiled=True),
        lax.all_gather(rank_out_down.astype(jnp.bfloat16), ("dp", "mp"), axis=1, tiled=True),
        lax.all_gather(magnitude_down.astype(jnp.bfloat16), ("dp", "mp"), axis=0, tiled=True),
    )
    qkv_out_cols = [local_part(whole_out_attn[member], local_width, 1) for member in range(3)]
    qkv_merged = [
        merge_adapter(base_qkv[member], whole_in_attn[member], qkv_out_cols[member])
        for member in range(3)
    ]
    qkv_norms = [norms_of(matrix) for matrix in qkv_merged]
    qkv_mags = [
        local_part(whole_mag_qkv[member], local_width, 0).astype(jnp.float32) for member in range(3)
    ]
    qkv_scales = [qkv_mags[member] / qkv_norms[member] for member in range(3)]
    qkv_lowered = jnp.concatenate([matrix.astype(jnp.bfloat16) for matrix in qkv_merged], axis=1)
    out_in_rows = local_part(whole_in_attn[3], local_width, 0)
    gu_out_cols = [local_part(whole_out_mlp[member], local_hidden, 1) for member in range(2)]
    gu_merged = [
        merge_adapter(base_gate_up[member], whole_in_mlp[member], gu_out_cols[member])
        for member in range(2)
    ]
    gu_norms = [norms_of(matrix) for matrix in gu_merged]
    gu_mags = [
        local_part(whole_mag_mlp[member], local_hidden, 0).astype(jnp.float32)
        for member in range(2)
    ]
    gu_scales = [gu_mags[member] / gu_norms[member] for member in range(2)]
    gu_lowered = jnp.concatenate([matrix.astype(jnp.bfloat16) for matrix in gu_merged], axis=1)
    down_in_rows = local_part(whole_in_down, local_hidden, 0)
    merged_down = merge_adapter(base_down, down_in_rows, whole_out_down)
    merged_out = merge_adapter(base_attn_out, out_in_rows, whole_out_attn[3])
    square_out, square_down = lax.psum(
        (jnp.sum(merged_out * merged_out, axis=0), jnp.sum(merged_down * merged_down, axis=0)), "mp"
    )
    norms_out = jnp.sqrt(square_out)
    lowered_out = merged_out.astype(jnp.bfloat16)
    norms_down = jnp.sqrt(square_down)
    mag_out_full = whole_mag_out.astype(jnp.float32)
    mag_down_full = whole_mag_down.astype(jnp.float32)
    scale_out = mag_out_full / norms_out
    scale_down = mag_down_full / norms_down
    lowered_down = merged_down.astype(jnp.bfloat16)
    gain_one = norm_attn.astype(jnp.float32)
    gain_two = norm_mlp.astype(jnp.float32)
    input_full = layer_input.astype(jnp.float32)
    unit_one, inverse_one = norm_forward(input_full)
    normed_one = (unit_one * gain_one).astype(jnp.bfloat16)
    gathered_one = lax.all_gather(normed_one, "mp", axis=0, tiled=True)
    projected = product(gathered_one, qkv_lowered)
    proj_query = projected[:, :local_width]
    proj_key = projected[:, local_width : 2 * local_width]
    proj_value = projected[:, 2 * local_width :]
    positions = positions_of(segment_ids)
    cosine, sine = rotary_tables(positions)
    heads_shape = (group_tokens, local_heads, HD)
    queries = (
        rotate((proj_query * qkv_scales[0]).reshape(heads_shape), cosine, sine) * query_scale
    ).astype(jnp.bfloat16)
    key_heads = rotate((proj_key * qkv_scales[1]).reshape(heads_shape), cosine, sine).astype(
        jnp.bfloat16
    )
    value_heads = (proj_value * qkv_scales[2]).reshape(heads_shape).astype(jnp.bfloat16)
    attended, log_norm = attention_forward(
        queries, key_heads, value_heads, segment_ids, token_valid
    )
    attended_low = attended.reshape(group_tokens, local_width).astype(jnp.bfloat16)
    summed_out = lax.psum_scatter(
        product(attended_low, lowered_out).astype(jnp.bfloat16),
        "mp",
        scatter_dimension=0,
        tiled=True,
    ).astype(jnp.float32)
    residual = input_full + summed_out * scale_out
    unit_two, inverse_two = norm_forward(residual)
    normed_two = (unit_two * gain_two).astype(jnp.bfloat16)
    gathered_two = lax.all_gather(normed_two, "mp", axis=0, tiled=True)
    gate_up = product(gathered_two, gu_lowered)
    proj_gate = gate_up[:, :local_hidden]
    proj_up = gate_up[:, local_hidden:]
    gate = proj_gate * gu_scales[0]
    upward = proj_up * gu_scales[1]
    hidden = (jax.nn.silu(gate) * upward).astype(jnp.bfloat16)
    summed_down = lax.psum_scatter(
        product(hidden, lowered_down).astype(jnp.bfloat16), "mp", scatter_dimension=0, tiled=True
    ).astype(jnp.float32)
    layer_output = (residual + summed_down * scale_down).astype(jnp.bfloat16)
    grad_output = cotangent.astype(jnp.float32)
    colgrad_down = jnp.sum(grad_output * summed_down, axis=0)
    low_down = (grad_output * scale_down).astype(jnp.bfloat16)
    gathered_grad_down = lax.all_gather(low_down, "mp", axis=0, tiled=True)
    grad_hidden = contract_cols(gathered_grad_down, lowered_down)
    grad_merged_down = contract_rows(hidden, gathered_grad_down)
    sigmoid_gate = jax.nn.sigmoid(gate)
    grad_gate = grad_hidden * upward * sigmoid_gate * (1.0 + gate * (1.0 - sigmoid_gate))
    grad_up = grad_hidden * gate * sigmoid_gate
    colgrad_gate = jnp.sum(grad_gate * proj_gate, axis=0)
    colgrad_up = jnp.sum(grad_up * proj_up, axis=0)
    low_gate_up = jnp.concatenate(
        [grad_gate * gu_scales[0], grad_up * gu_scales[1]], axis=1
    ).astype(jnp.bfloat16)
    grad_merged_gu = contract_rows(
        lax.all_gather(normed_two, "mp", axis=0, tiled=True), low_gate_up
    )
    grad_normed_two = lax.psum_scatter(
        contract_cols(low_gate_up, gu_lowered).astype(jnp.bfloat16),
        "mp",
        scatter_dimension=0,
        tiled=True,
    ).astype(jnp.float32)
    grad_residual = grad_output + norm_backward(grad_normed_two, unit_two, inverse_two, gain_two)
    colgrad_out = jnp.sum(grad_residual * summed_out, axis=0)
    low_out = (grad_residual * scale_out).astype(jnp.bfloat16)
    gathered_grad_out = lax.all_gather(low_out, "mp", axis=0, tiled=True)
    grad_attended = (
        contract_cols(gathered_grad_out, lowered_out).astype(jnp.bfloat16).reshape(heads_shape)
    )
    grad_merged_out = contract_rows(attended_low, gathered_grad_out)
    grad_query, grad_key, grad_value = attention_backward(
        queries, key_heads, value_heads, grad_attended, log_norm, segment_ids, token_valid
    )
    delta_query = rotate(grad_query * query_scale, cosine, -sine).reshape(group_tokens, local_width)
    delta_key = rotate(grad_key, cosine, -sine).reshape(group_tokens, local_width)
    delta_value = grad_value.reshape(group_tokens, local_width)
    qkv_colgrads = [
        jnp.sum(delta_query * proj_query, axis=0),
        jnp.sum(delta_key * proj_key, axis=0),
        jnp.sum(delta_value * proj_value, axis=0),
    ]
    low_qkv = jnp.concatenate(
        [delta_query * qkv_scales[0], delta_key * qkv_scales[1], delta_value * qkv_scales[2]],
        axis=1,
    ).astype(jnp.bfloat16)
    grad_merged_qkv = contract_rows(lax.all_gather(normed_one, "mp", axis=0, tiled=True), low_qkv)
    grad_normed_one = lax.psum_scatter(
        contract_cols(low_qkv, qkv_lowered).astype(jnp.bfloat16),
        "mp",
        scatter_dimension=0,
        tiled=True,
    ).astype(jnp.float32)
    input_grad = grad_residual + norm_backward(grad_normed_one, unit_one, inverse_one, gain_one)
    total_out, total_down = lax.psum((colgrad_out, colgrad_down), "mp")
    attn_in = []
    attn_out = []
    qkv_mag_grads = []
    for member in range(3):
        grad_in, grad_out_local = adapter_grads(
            grad_merged_qkv[:, member * local_width : (member + 1) * local_width],
            qkv_merged[member],
            qkv_colgrads[member],
            qkv_norms[member],
            qkv_mags[member],
            whole_in_attn[member],
            qkv_out_cols[member],
        )
        attn_in.append(grad_in)
        attn_out.append(place_local((R, model_width), grad_out_local, local_width, 1))
        qkv_mag_grads.append(
            place_local((model_width,), qkv_colgrads[member] / qkv_norms[member], local_width, 0)
        )
    grad_in_rows, grad_out_full = adapter_grads(
        grad_merged_out,
        merged_out,
        total_out,
        norms_out,
        mag_out_full,
        out_in_rows,
        whole_out_attn[3],
    )
    attn_in.append(place_local((model_width, R), grad_in_rows, local_width, 0))
    attn_out.append(grad_out_full)
    mag_out_grad = colgrad_out / norms_out
    mlp_in = []
    mlp_out = []
    gu_mag_grads = []
    gu_colgrads = [colgrad_gate, colgrad_up]
    for member in range(2):
        grad_in, grad_out_local = adapter_grads(
            grad_merged_gu[:, member * local_hidden : (member + 1) * local_hidden],
            gu_merged[member],
            gu_colgrads[member],
            gu_norms[member],
            gu_mags[member],
            whole_in_mlp[member],
            gu_out_cols[member],
        )
        mlp_in.append(grad_in)
        mlp_out.append(place_local((R, hidden_width), grad_out_local, local_hidden, 1))
        gu_mag_grads.append(
            place_local((hidden_width,), gu_colgrads[member] / gu_norms[member], local_hidden, 0)
        )
    down_in_rows_grad, down_out_grad = adapter_grads(
        grad_merged_down,
        merged_down,
        total_down,
        norms_down,
        mag_down_full,
        down_in_rows,
        whole_out_down,
    )
    down_in_grad = place_local((hidden_width, R), down_in_rows_grad, local_hidden, 0)
    mag_down_grad = colgrad_down / norms_down
    (
        grad_in_attn,
        grad_out_attn,
        grad_mag_qkv,
        grad_mag_out,
        grad_in_mlp,
        grad_out_mlp,
        grad_mag_mlp,
        grad_in_down,
        grad_out_down,
        grad_mag_down,
    ) = (
        lax.psum_scatter(jnp.stack(attn_in), ("dp", "mp"), scatter_dimension=1, tiled=True),
        lax.psum_scatter(jnp.stack(attn_out), ("dp", "mp"), scatter_dimension=2, tiled=True),
        lax.psum_scatter(jnp.stack(qkv_mag_grads), ("dp", "mp"), scatter_dimension=1, tiled=True),
        lax.psum_scatter(mag_out_grad, ("dp", "mp"), scatter_dimension=0, tiled=True),
        lax.psum_scatter(jnp.stack(mlp_in), ("dp", "mp"), scatter_dimension=1, tiled=True),
        lax.psum_scatter(jnp.stack(mlp_out), ("dp", "mp"), scatter_dimension=2, tiled=True),
        lax.psum_scatter(jnp.stack(gu_mag_grads), ("dp", "mp"), scatter_dimension=1, tiled=True),
        lax.psum_scatter(down_in_grad, ("dp", "mp"), scatter_dimension=0, tiled=True),
        lax.psum_scatter(down_out_grad, ("dp", "mp"), scatter_dimension=1, tiled=True),
        lax.psum_scatter(mag_down_grad, ("dp", "mp"), scatter_dimension=0, tiled=True),
    )
    return (
        layer_output,
        input_grad,
        grad_in_attn,
        grad_out_attn,
        grad_mag_qkv,
        grad_mag_out,
        grad_in_mlp,
        grad_out_mlp,
        grad_mag_mlp,
        grad_in_down,
        grad_out_down,
        grad_mag_down,
    )


def solution(mesh):
    return jax.shard_map(
        on_device,
        mesh=mesh,
        in_specs=(
            P(("dp", "mp"), None),
            P(("dp", "mp"), None),
            P("dp"),
            P("dp"),
            P(),
            P(),
            P(None, None, "mp"),
            P("mp", None),
            P(None, None, "mp"),
            P("mp", None),
            P(None, ("dp", "mp"), None),
            P(None, None, ("dp", "mp")),
            P(None, ("dp", "mp")),
            P(("dp", "mp")),
            P(None, ("dp", "mp"), None),
            P(None, None, ("dp", "mp")),
            P(None, ("dp", "mp")),
            P(("dp", "mp"), None),
            P(None, ("dp", "mp")),
            P(("dp", "mp")),
        ),
        out_specs=(
            P(("dp", "mp"), None),
            P(("dp", "mp"), None),
            P(None, ("dp", "mp"), None),
            P(None, None, ("dp", "mp")),
            P(None, ("dp", "mp")),
            P(("dp", "mp")),
            P(None, ("dp", "mp"), None),
            P(None, None, ("dp", "mp")),
            P(None, ("dp", "mp")),
            P(("dp", "mp"), None),
            P(None, ("dp", "mp")),
            P(("dp", "mp")),
        ),
        check_vma=False,
    )
```

profile of v0, /device:TPU:0, one launch (start us, length us, event | category | flops | bytes accessed | tf_op | source)
XLA Modules:
  0.0 2656.5 jit_solution(223321264474529078)
XLA Ops:
  14.4 70.8 %all-gather = bf16[32,64,3]{1,2,0:T(4,128)(2,1)S(1)} all-gather(bf16[1,64,3]{1,2,0:T(4,128)(2,1)S(1)} %convert_bitcast_fusion.3), channel_id=1, replica_groups=mesh['dp'=4,'mp'=8] {'dp','mp'}, dimensions={0}, use_global_device_ids=true | all-gather | bytes 12672 | tf_op jit(solution)/shard_map/all_gather | solution.py:217
  85.6 97.9 %all_gather.45 = bf16[4,16,2048]{1,0,2:T(4,128)(2,1)S(1)} all-gather(bf16[4,16,64]{1,0,2:T(4,128)(2,1)S(1)} %copy.145), channel_id=1, replica_groups=mesh['dp'=4,'mp'=8] {'dp','mp'}, dimensions={2}, use_global_device_ids=true | all-gather | bytes 270336 | tf_op jit(solution)/shard_map/all_gather | solution.py:216
  189.3 80.0 %all_gather.46 = bf16[4,2048,16]{2,0,1:T(4,128)(2,1)S(1)} all-gather(bf16[4,64,16]{2,0,1:T(4,128)(2,1)S(1)} %copy.147), channel_id=1, replica_groups=mesh['dp'=4,'mp'=8] {'dp','mp'}, dimensions={1}, use_global_device_ids=true | all-gather | bytes 270336 | tf_op jit(solution)/shard_map/all_gather | solution.py:215
  337.7 51.1 %while.31 = (s32[]{:T(128)}, bf16[4,512,2,128]{3,1,2,0:T(8,128)(2,1)}, f32[4,2,512]{2,1,0:T(2,128)S(1)}, s32[4]{0:T(128)S(1)}, s32[2048]{0:T(1024)S(1)}, /*index...) while((s32[]{:T(128)}, ...), condition=%wide.region_9.0_spmd, body=%wide.region_6.9_spmd.sunk | while | flops 1098909184 | bytes 40696264 | solution.py:121
  399.3 69.3 %all-gather.3 = bf16[32,64,16]{1,2,0:T(8,128)(2,1)S(1)} all-gather(bf16[1,64,16]{1,2,0:T(8,128)(2,1)S(1)} %convert_bitcast_fusion.1), channel_id=1, replica_groups=mesh['dp'=4,'mp'=8] {'dp','mp'}, dimensions={0}, use_global_device_ids=true | all-gather | bytes 67584 | tf_op jit(solution)/shard_map/all_gather | solution.py:223
  468.9 67.8 %all-gather.2 = bf16[32,176,16]{1,2,0:T(8,128)(2,1)S(1)} all-gather(bf16[1,176,16]{1,2,0:T(8,128)(2,1)S(1)} %convert_bitcast_fusion), channel_id=1, replica_groups=mesh['dp'=4,'mp'=8] {'dp','mp'}, dimensions={0}, use_global_device_ids=true | all-gather | bytes 185856 | tf_op jit(solution)/shard_map/all_gather | solution.py:222
  537.6 37.1 %all-reduce.7 = (bf16[2048]{0:T(1024)(128)(2,1)S(1)}, bf16[2048]{0:T(1024)(128)(2,1)S(1)}) all-reduce(bf16[2048]{0:T(1024)(128)(2,1)S(1)} %dynamic-update-slice, bf16[2048]{0:T(1024)(128)(2,1)S(1)} %dynamic-update-slice.1), channel_id=1, replica_groups=mesh['dp'=4,'mp'=8] {'dp','mp'}, use_global_device_ids=true, to_apply=%add | all-reduce | flops 4096 | bytes 16384
  580.3 36.9 %all-reduce.6 = (f32[2048]{0:T(1024)S(1)}, f32[2048]{0:T(1024)S(1)}) all-reduce(f32[2048]{0:T(1024)S(1)} %get-tuple-element.576, f32[2048]{0:T(1024)S(1)} %get-tuple-element.578), channel_id=1, replica_groups=mesh['dp'=4,'mp'=8] {'mp'}, use_global_device_ids=true, to_apply=%region_12.13 | all-reduce | flops 4096 | bytes 32768 | tf_op jit(solution)/shard_map/psum | solution.py:253
  623.3 64.3 %all-gather.1 = bf16[32,176,2]{1,2,0:T(2,128)(2,1)S(1)} all-gather(bf16[1,176,2]{1,2,0:T(2,128)(2,1)S(1)} %convert_bitcast_fusion.2), channel_id=1, replica_groups=mesh['dp'=4,'mp'=8] {'dp','mp'}, dimensions={0}, use_global_device_ids=true | all-gather | bytes 23232 | tf_op jit(solution)/shard_map/all_gather | solution.py:221
  687.9 82.8 %all_gather.51 = bf16[2,2048,16]{2,0,1:T(2,128)(2,1)S(1)} all-gather(bf16[2,64,16]{2,0,1:T(2,128)(2,1)S(1)} %copy.166), channel_id=1, replica_groups=mesh['dp'=4,'mp'=8] {'dp','mp'}, dimensions={1}, use_global_device_ids=true | all-gather | bytes 135168 | tf_op jit(solution)/shard_map/all_gather | solution.py:219
  775.7 122.1 %all_gather.50 = bf16[2,16,5632]{1,0,2:T(2,128)(2,1)S(1)} all-gather(bf16[2,16,176]{1,0,2:T(2,128)(2,1)S(1)} %copy.164), channel_id=1, replica_groups=mesh['dp'=4,'mp'=8] {'dp','mp'}, dimensions={2}, use_global_device_ids=true | all-gather | bytes 371712 | tf_op jit(solution)/shard_map/all_gather | solution.py:220
  917.7 18.8 fusion.40
  936.6 19.1 multiply_reduce_fusion.2
  963.3 17.3 convolution_convert_fusion.1
  980.7 147.5 %reduce-scatter.33.cloned.1.call-done = bf16[256,2048]{1,0:T(8,128)(2,1)} async-done(((bf16[2048,2048]{1,0:T(8,128)(2,1)}), bf16[256,2048]{1,0:T(8,128)(2,1)}) %reduce-scatter.33.cloned.1.call-update) | async-done | bytes 1048592 | tf_op jit(solution)/shard_map/reduce_scatter | solution.py:325
  1132.6 11.7 convolution_convert_fusion.2
  1144.4 112.2 %all-gather.15.cloned.1.call-done = bf16[2048,2048]{1,0:T(8,128)(2,1)} async-done(((bf16[256,2048]{1,0:T(8,128)(2,1)}), bf16[2048,2048]{1,0:T(8,128)(2,1)}) %all-gather.15.cloned.1.call-update) | async-done | bytes 8388624 | tf_op jit(solution)/shard_map/all_gather | solution.py:334
  1263.9 98.8 %while.32 = (s32[]{:T(128)}, f32[2048,2,128]{0,2,1:T(8,128)S(1)}, f32[2048,2,128]{0,2,1:T(8,128)}, f32[4,512,2,128]{3,1,0,2:T(8,128)}, s32[4]{0:T(128)S(1)}, /*i...) while((s32[]{:T(128)}, f32[2048,2,128]{0,2,1:T(8,128)S(1)}, ...), condition=%wide.region_23.24_spmd.clone, body=%wide.region_21.23_spmd.clone.sunk | while | flops 2717910528 | bytes 88664616 | solution.py:158
  1401.9 17.2 fusion.39
  1449.8 11.6 fusion.78
  1475.0 84.5 %reduce-scatter.35.cloned.1.call-done = bf16[256,2048]{1,0:T(8,128)(2,1)} async-done(((bf16[2048,2048]{1,0:T(8,128)(2,1)}), bf16[256,2048]{1,0:T(8,128)(2,1)}) %reduce-scatter.35.cloned.1.call-update) | async-done | bytes 1048592 | tf_op jit(solution)/shard_map/reduce_scatter | solution.py:355
  1565.2 35.4 %all-reduce.5 = (f32[2048]{0:T(1024)}, f32[2048]{0:T(1024)S(1)}) all-reduce(f32[2048]{0:T(1024)S(1)} %get-tuple-element.434, f32[2048]{0:T(1024)S(1)} %get-tuple-element.433), channel_id=1, replica_groups=mesh['dp'=4,'mp'=8] {'mp'}, use_global_device_ids=true, to_apply=%region_30.31 | all-reduce | flops 4096 | bytes 32768 | tf_op jit(solution)/shard_map/psum | solution.py:362
  1601.3 10.3 multiply_subtract_fusion
  1665.3 35.6 %reduce-scatter.47.cloned.1.call-done = f32[176,2]{1,0:T(8,128)} async-done(((f32[5632,2]{1,0:T(8,128)}), f32[176,2]{1,0:T(8,128)}) %reduce-scatter.47.cloned.1.call-update) | async-done | bytes 1424
  1702.5 132.4 %reduce-scatter.43.cloned.1.call-done = f32[64,32]{1,0:T(8,128)} async-done(((f32[2048,32]{1,0:T(8,128)}), f32[64,32]{1,0:T(8,128)}) %reduce-scatter.43.cloned.1.call-update) | async-done | bytes 8208
  1836.5 137.2 %reduce-scatter.45.cloned.1.call-done = f32[176,32]{1,0:T(8,128)} async-done(((f32[5632,32]{1,0:T(8,128)}), f32[176,32]{1,0:T(8,128)}) %reduce-scatter.45.cloned.1.call-update) | async-done | bytes 22544
  1975.5 132.9 %reduce-scatter.41.cloned.1.call-done = f32[64,3]{1,0:T(8,128)} async-done(((f32[2048,3]{1,0:T(8,128)}), f32[64,3]{1,0:T(8,128)}) %reduce-scatter.41.cloned.1.call-update) | async-done | bytes 784
  2109.8 37.2 %all-reduce.4 = (f32[2048]{0:T(1024)S(1)}, f32[2048]{0:T(1024)S(1)}) all-reduce(f32[2048]{0:T(1024)S(1)} %get-tuple-element.551, f32[2048]{0:T(1024)S(1)} %copy-done.98), channel_id=9, replica_groups=mesh['dp'=4,'mp'=8] {'dp','mp'}, use_global_device_ids=true, to_apply=%region_34.35.clone | all-reduce | flops 4096 | bytes 32768
  2152.8 89.3 %reduce-scatter.51.cloned.1.call-done = f32[64,16]{1,0:T(8,128)} async-done(((f32[2048,16]{1,0:T(8,128)}), f32[64,16]{1,0:T(8,128)}) %reduce-scatter.51.cloned.1.call-update) | async-done | bytes 4112
  2243.5 137.4 %reduce-scatter.49.cloned.1.call-done = f32[176,16]{1,0:T(8,128)} async-done(((f32[5632,16]{1,0:T(8,128)}), f32[176,16]{1,0:T(8,128)}) %reduce-scatter.49.cloned.1.call-update) | async-done | bytes 11280
  2382.5 132.0 %reduce-scatter.37.cloned.1.call-done = f32[64,64]{1,0:T(8,128)} async-done(((f32[2048,64]{1,0:T(8,128)}), f32[64,64]{1,0:T(8,128)}) %reduce-scatter.37.cloned.1.call-update) | async-done | bytes 16400
  2516.1 131.8 %reduce-scatter.39.cloned.1.call-done = f32[64,64]{1,0:T(8,128)} async-done(((f32[2048,64]{1,0:T(8,128)}), f32[64,64]{1,0:T(8,128)}) %reduce-scatter.39.cloned.1.call-update) | async-done | bytes 16400
  (642 shorter events, 444.9 us)
Async XLA Ops:
  7.2 289.3 %all-gather.9.cloned.1.call-start = ((), (), s32[]{:S(2)}) async-start(), calls=%async_computation.12 | async-start | bytes 9437184 | tf_op jit(solution)/shard_map/all_gather | solution.py:269
  12.6 604.6 %reduce-scatter.29.cloned.1.call-start = ((), (), s32[]{:S(2)}) async-start(), calls=%async_computation.13 | async-start | bytes 9437184 | tf_op jit(solution)/shard_map/reduce_scatter | solution.py:288
  187.7 101.5 %copy-start.55 = (bf16[1,16,2048]{2,1,0:T(8,128)(2,1)}, bf16[1,16,2048]{2,1,0:T(8,128)(2,1)S(1)}, u32[]{:S(2)}) copy-start(bf16[1,16,2048]{2,1,0:T(8,128)(2,1)S(1)} %copy.223) | copy-start | bytes 196612
  188.9 97.0 %copy-start.75 = (bf16[1,16,256]{2,1,0:T(8,128)(2,1)}, bf16[1,16,256]{2,1,0:T(8,128)(2,1)S(1)}, u32[]{:S(2)}) copy-start(bf16[1,16,256]{2,1,0:T(8,128)(2,1)S(1)} %copy.207) | copy-start | bytes 24580
  189.3 93.7 %copy-start.77 = (bf16[1,16,256]{2,1,0:T(8,128)(2,1)}, bf16[1,16,256]{2,1,0:T(8,128)(2,1)S(1)}, u32[]{:S(2)}) copy-start(bf16[1,16,256]{2,1,0:T(8,128)(2,1)S(1)} %copy.211) | copy-start | bytes 24580
  398.6 519.1 %all-gather.11.cloned.1.call-start = ((), (), s32[]{:S(2)}) async-start(), calls=%async_computation.14 | async-start | bytes 9437184 | tf_op jit(solution)/shard_map/all_gather | solution.py:297
  399.3 731.0 %copy-start.64 = (f32[2048]{0:T(1024)}, f32[2048]{0:T(1024)S(1)}, u32[]{:S(2)}) copy-start(f32[2048]{0:T(1024)S(1)} %convert_element_type.262) | copy-start | bytes 24580
  468.9 111.4 %copy-start.49 = (bf16[2048,16]{0,1:T(8,128)(2,1)}, bf16[2048,16]{0,1:T(8,128)(2,1)S(1)}, u32[]{:S(2)}) copy-start(bf16[2048,16]{0,1:T(8,128)(2,1)S(1)} %reshape.642) | copy-start | bytes 196612
  617.2 513.1 %copy-start.62 = (f32[2048]{0:T(1024)}, f32[2048]{0:T(1024)S(1)}, u32[]{:S(2)}) copy-start(f32[2048]{0:T(1024)S(1)} %convert_divide_fusion.1) | copy-start | bytes 24580
  619.1 511.2 %copy-start.87 = (f32[256]{0:T(256)}, f32[256]{0:T(256)S(1)}, u32[]{:S(2)}) copy-start(f32[256]{0:T(256)S(1)} %add_rsqrt_fusion) | copy-start | bytes 3076
  621.8 314.8 %all-gather.13.cloned.1.call-start = ((), (), s32[]{:S(2)}) async-start(), calls=%async_computation.16 | async-start | bytes 9437184 | tf_op jit(solution)/shard_map/all_gather | solution.py:311
  623.1 505.1 %reduce-scatter.33.cloned.1.call-start = ((), (), s32[]{:S(2)}) async-start(), calls=%async_computation.17 | async-start | bytes 9437184 | tf_op jit(solution)/shard_map/reduce_scatter | solution.py:325
  775.2 127.9 %copy-start.51 = (bf16[1,2048,16]{1,2,0:T(8,128)(2,1)}, bf16[1,2048,16]{1,2,0:T(8,128)(2,1)S(1)}, u32[]{:S(2)}) copy-start(bf16[1,2048,16]{1,2,0:T(8,128)(2,1)S(1)} %copy.226) | copy-start | bytes 196612
  775.7 134.8 %copy-start.53 = (bf16[1,2048,16]{1,2,0:T(8,128)(2,1)}, bf16[1,2048,16]{1,2,0:T(8,128)(2,1)S(1)}, u32[]{:S(2)}) copy-start(bf16[1,2048,16]{1,2,0:T(8,128)(2,1)S(1)} %copy.229) | copy-start | bytes 196612
  980.6 147.6 %copy-start.4 = (bf16[256,2048]{1,0:T(8,128)(2,1)S(1)}, bf16[256,2048]{1,0:T(8,128)(2,1)}, u32[]{:S(2)}) copy-start(bf16[256,2048]{1,0:T(8,128)(2,1)} %reduce-scatter.29.cloned.1.call-done) | copy-start | bytes 3145732
  980.6 275.9 %all-gather.15.cloned.1.call-start = ((), (), s32[]{:S(2)}) async-start(), calls=%async_computation.18 | async-start | bytes 9437184 | tf_op jit(solution)/shard_map/all_gather | solution.py:334
  1132.5 342.5 %reduce-scatter.31.cloned.1.call-start = ((), (), s32[]{:S(2)}) async-start(), calls=%async_computation.15 | async-start | bytes 9437184 | tf_op jit(solution)/shard_map/reduce_scatter | solution.py:304
  1144.3 415.1 %reduce-scatter.35.cloned.1.call-start = ((), (), s32[]{:S(2)}) async-start(), calls=%async_computation.19 | async-start | bytes 9437184 | tf_op jit(solution)/shard_map/reduce_scatter | solution.py:355
  1396.8 304.2 %reduce-scatter.47.cloned.1.call-start = ((), (), s32[]{:S(2)}) async-start(), calls=%async_computation.25 | async-start | bytes 2973696
  1430.7 404.2 %reduce-scatter.43.cloned.1.call-start = ((), (), s32[]{:S(2)}) async-start(), calls=%async_computation.23 | async-start | bytes 1081344
  1435.5 538.3 %reduce-scatter.45.cloned.1.call-start = ((), (), s32[]{:S(2)}) async-start(), calls=%async_computation.24 | async-start | bytes 2973696
  1447.7 660.7 %reduce-scatter.41.cloned.1.call-start = ((), (), s32[]{:S(2)}) async-start(), calls=%async_computation.22 | async-start | bytes 1081344
  1474.7 126.0 %copy-start.97 = (f32[2048]{0:T(1024)S(1)}, f32[2048]{0:T(1024)}, u32[]{:S(2)}) copy-start(f32[2048]{0:T(1024)} %copy-done.96) | copy-start | bytes 24580
  1474.7 126.0 %copy-start.106 = (bf16[2048]{0:T(1024)(128)(2,1)S(1)}, bf16[2048]{0:T(1024)(128)(2,1)}, u32[]{:S(2)}) copy-start(bf16[2048]{0:T(1024)(128)(2,1)} %copy-done.105) | copy-start | bytes 12292
  1474.7 767.4 %reduce-scatter.51.cloned.1.call-start = ((), (), s32[]{:S(2)}) async-start(), calls=%async_computation.27 | async-start | bytes 1081344
  1618.3 762.6 %reduce-scatter.49.cloned.1.call-start = ((), (), s32[]{:S(2)}) async-start(), calls=%async_computation.26 | async-start | bytes 2973696
  1628.3 886.2 %reduce-scatter.37.cloned.1.call-start = ((), (), s32[]{:S(2)}) async-start(), calls=%async_computation.20 | async-start | bytes 1081344
  1647.7 1000.2 %reduce-scatter.39.cloned.1.call-start = ((), (), s32[]{:S(2)}) async-start(), calls=%async_computation.21 | async-start | bytes 1081344
  1660.7 449.1 %copy-start.98 = (f32[2048]{0:T(1024)S(1)}, f32[2048]{0:T(1024)}, u32[]{:S(2)}) copy-start(f32[2048]{0:T(1024)} %get-tuple-element.550) | copy-start | bytes 24580
  1660.7 487.5 %copy-start.133 = (f32[256]{0:T(256)S(1)}, f32[256]{0:T(256)}, u32[]{:S(2)}) copy-start(f32[256]{0:T(256)} %get-tuple-element.435) | copy-start | bytes 3076
  1660.7 487.5 %copy-start.109 = (f32[256]{0:T(256)S(1)}, f32[256]{0:T(256)}, u32[]{:S(2)}) copy-start(f32[256]{0:T(256)} %copy-done.107) | copy-start | bytes 3076
  1660.7 487.5 %copy-start.112 = (f32[256]{0:T(256)S(1)}, f32[256]{0:T(256)}, u32[]{:S(2)}) copy-start(f32[256]{0:T(256)} %copy-done.110) | copy-start | bytes 3076
  (144 other events, 1885.7 us)
Sparse Core Ops, SparseCore 0:
  12.7 158.0 all-gather.8
  398.7 149.0 reduce-scatter.28
  621.9 136.3 all-gather.10
  760.5 167.5 all-gather.12
  980.8 147.3 reduce-scatter.32
  1132.6 123.9 all-gather.14
  1260.2 147.0 reduce-scatter.30
  1411.4 147.9 reduce-scatter.34
  1561.7 139.2 reduce-scatter.46
  1703.1 131.8 reduce-scatter.42
  1837.3 136.3 reduce-scatter.44
  1975.9 132.4 reduce-scatter.40
  2110.7 131.3 reduce-scatter.50
  2244.3 136.5 reduce-scatter.48
  2383.1 131.3 reduce-scatter.36
  2516.6 131.2 reduce-scatter.38
where the time goes:
time: 2660 us
  waiting for transfers between devices  1270 us (48%)
  blocking collectives  802 us (30%)
  matrix products  290 us (11%)
  local copies, waits for them, and re-layouts  147 us (6%)
  other arithmetic  112 us (4%)
    unnamed x24, waiting for transfers between devices  929 us
    reduce_scatter x1, waiting for transfers between devices, on_device(): lax.psum_scatter(contract_cols(low_gate_up, gu_lowered).astype(jnp.bfloat...  148 us
    all_gather x1, blocking collectives, on_device(): lax.all_gather(rank_out_mlp.astype(jnp.bfloat16), ('dp', 'mp'), axis=2, t...  122 us
    all_gather x1, waiting for transfers between devices, on_device(): gathered_grad_out = lax.all_gather(low_out, 'mp', axis=0, tiled=True)  112 us
    all_gather x1, blocking collectives, on_device(): lax.all_gather(rank_out_attn.astype(jnp.bfloat16), ('dp', 'mp'), axis=2,...  97.9 us
    unnamed x341, local copies, waits for them, and re-layouts  92.9 us
    reduce_scatter x1, waiting for transfers between devices, on_device(): lax.psum_scatter(contract_cols(low_qkv, qkv_lowered).astype(jnp.bfloat16)...  84.5 us
    all_gather x1, blocking collectives, on_device(): lax.all_gather(rank_in_mlp.astype(jnp.bfloat16), ('dp', 'mp'), axis=1, ti...  82.8 us
  transfers between devices with their start and end apart: 16, of which 11 were waited for; matrix products, arithmetic and copies ran while one was open for 14% of the time, Pallas kernels for 0%

commit v1 on v0

v1 whole, which is shorter than its diff:
```python
import functools

import jax
import jax.numpy as jnp
import numpy as np
from jax import lax
from jax.experimental import pallas as pl
from jax.experimental.pallas import tpu as pltpu
from jax.sharding import Mesh
from jax.sharding import PartitionSpec as P

HD = 128
R = 16
ALPHA = 32
FACTOR = ALPHA / R
EPSILON = 1e-05
ROPE_BASE = 10000.0
BF16 = jnp.bfloat16
F32 = jnp.float32
NEG = -1e30
AXES = ("x", "c", "zh", "zl", "y")
VM = pl.BlockSpec(memory_space=pltpu.VMEM)
SM = pl.BlockSpec(memory_space=pltpu.SMEM)


def mm(left, right, lc=1, rc=0, precision=None):
    return lax.dot_general(
        left,
        right,
        (((lc,), (rc,)), ((), ())),
        preferred_element_type=F32,
        precision=precision,
    )


def params(mib=58):
    return pltpu.CompilerParams(vmem_limit_bytes=mib * 1024 * 1024)


def cost(flops, nbytes, trans=0):
    return pl.CostEstimate(
        flops=int(flops), bytes_accessed=int(nbytes), transcendentals=int(trans)
    )


def pack_kernel(a_w, f_w, a1, b1, mq, mo, a2, b2, mm_, a3, b3, md, out):
    out[...] = jnp.zeros(out.shape, out.dtype)

    def turned(block):
        width = block.shape[0]
        eye = (
            lax.broadcasted_iota(jnp.int32, (width, width), 0)
            == lax.broadcasted_iota(jnp.int32, (width, width), 1)
        ).astype(BF16)
        return mm(block.astype(BF16), eye, 0, 0).astype(BF16)

    for p in range(4):
        out[0, :R, p * a_w : (p + 1) * a_w] = turned(a1[p])
    for p in range(2):
        out[0, :R, (4 + p) * a_w : (5 + p) * a_w] = turned(a2[p])
    at = 6 * a_w
    out[0, :R, at : at + f_w] = turned(a3[...])
    at += f_w
    for p in range(4):
        out[0, :R, at : at + a_w] = b1[p].astype(BF16)
        at += a_w
    for p in range(2):
        out[0, :R, at : at + f_w] = b2[p].astype(BF16)
        at += f_w
    out[0, :R, at : at + a_w] = b3[...].astype(BF16)
    at = 0
    for p in range(3):
        out[0, R : R + 1, at : at + a_w] = mq[p : p + 1, :].astype(BF16)
        at += a_w
    out[0, R : R + 1, at : at + a_w] = mo[...].astype(BF16)
    at += a_w
    for p in range(2):
        out[0, R : R + 1, at : at + f_w] = mm_[p : p + 1, :].astype(BF16)
        at += f_w
    out[0, R : R + 1, at : at + a_w] = md[...].astype(BF16)


def unpack_kernel(
    a_w, f_w, dp, order, where_, g, at_qkv, at_gu, at_o, at_d, at_o0, at_d0,
    b_qkv, b_gu, b_o, b_d, m_qkv, m_o, m_gu, m_d,
):
    n = g.shape[0]
    b_at = 6 * a_w + f_w
    for d in range(n):
        s = order[d]
        lo, hi = d * a_w, (d + 1) * a_w
        for p in range(3):
            at_qkv[p * R : (p + 1) * R, lo:hi] = g[s, :R, p * a_w : (p + 1) * a_w]
        for p in range(2):
            at_gu[p, :, lo:hi] = g[s, :R, (4 + p) * a_w : (5 + p) * a_w]
        b_o[:, lo:hi] = g[s, :R, b_at + 3 * a_w : b_at + 4 * a_w]
        end = b_at + 4 * a_w + 2 * f_w
        b_d[:, lo:hi] = g[s, :R, end : end + a_w]
        m_o[:, lo:hi] = g[s, R : R + 1, 3 * a_w : 4 * a_w].astype(F32)
        end = 4 * a_w + 2 * f_w
        m_d[:, lo:hi] = g[s, R : R + 1, end : end + a_w].astype(F32)
    for i in range(dp):
        s = order[where_[0] * dp + i]
        lo, hi = i * a_w, (i + 1) * a_w
        flo, fhi = i * f_w, (i + 1) * f_w
        at_o[:, lo:hi] = g[s, :R, 3 * a_w : 4 * a_w]
        at_d[:, flo:fhi] = g[s, :R, 6 * a_w : 6 * a_w + f_w]
        for p in range(3):
            b_qkv[p, :, lo:hi] = g[s, :R, b_at + p * a_w : b_at + (p + 1) * a_w]
            m_qkv[p, :, lo:hi] = g[s, R : R + 1, p * a_w : (p + 1) * a_w].astype(F32)
        for p in range(2):
            e = b_at + 4 * a_w + p * f_w
            b_gu[p, :, flo:fhi] = g[s, :R, e : e + f_w]
            e = 4 * a_w + p * f_w
            m_gu[p, :, flo:fhi] = g[s, R : R + 1, e : e + f_w].astype(F32)
        s = order[where_[1] * dp + i]
        at_o0[:, lo:hi] = g[s, :R, 3 * a_w : 4 * a_w]
        at_d0[:, flo:fhi] = g[s, :R, 6 * a_w : 6 * a_w + f_w]


def pack_grads_kernel(
    a_w, f_w, dp, order, where_, ga_full, gb_full, m_full, ga_attn, ga_d, gb_qkv, gb_gu,
    m_qkv, m_gu, out
):
    n = out.shape[0]
    out[...] = jnp.zeros(out.shape, out.dtype)
    b_at = 6 * a_w + f_w
    dt = out.dtype
    for d in range(n):
        s = order[d]
        lo, hi = d * a_w, (d + 1) * a_w
        for i, p in enumerate((0, 1, 2, 4, 5)):
            out[s, :R, p * a_w : (p + 1) * a_w] = ga_full[i * R : (i + 1) * R, lo:hi].astype(dt)
        out[s, :R, b_at + 3 * a_w : b_at + 4 * a_w] = gb_full[:R, lo:hi].astype(dt)
        end = b_at + 4 * a_w + 2 * f_w
        out[s, :R, end : end + a_w] = gb_full[R:, lo:hi].astype(dt)
        out[s, R : R + 1, 3 * a_w : 4 * a_w] = m_full[0:1, lo:hi].astype(dt)
        end = 4 * a_w + 2 * f_w
        out[s, R : R + 1, end : end + a_w] = m_full[1:2, lo:hi].astype(dt)
    for i in range(dp):
        s = order[where_[0] * dp + i]
        lo, hi = i * a_w, (i + 1) * a_w
        flo, fhi = i * f_w, (i + 1) * f_w
        out[s, :R, 3 * a_w : 4 * a_w] = ga_attn[:, lo:hi].astype(dt)
        out[s, :R, 6 * a_w : 6 * a_w + f_w] = ga_d[:, flo:fhi].astype(dt)
        for p in range(3):
            out[s, :R, b_at + p * a_w : b_at + (p + 1) * a_w] = gb_qkv[p, :, lo:hi].astype(dt)
            out[s, R : R + 1, p * a_w : (p + 1) * a_w] = m_qkv[p, :, lo:hi].astype(dt)
        for p in range(2):
            e = b_at + 4 * a_w + p * f_w
            out[s, :R, e : e + f_w] = gb_gu[p, :, flo:fhi].astype(dt)
            e = 4 * a_w + p * f_w
            out[s, R : R + 1, e : e + f_w] = m_gu[p, :, flo:fhi].astype(dt)


def merge_cols_kernel(x_parts, flags, own, *refs):
    parts = refs[:x_parts]
    at, b, vb, ssq = refs[x_parts:]
    h = pl.program_id(2)
    k = lax.rem(h - flags[1] + x_parts, x_parts)
    w = parts[0][0]
    for i in range(1, x_parts):
        w = jnp.where(k == i, parts[i][0], w)
    w = jnp.where(flags[0] == 1, own[0], w)
    v = w.astype(F32) + FACTOR * mm(at[...], b[0], 0, 0)
    vb[...] = v.astype(BF16)

    @pl.when(h == 0)
    def _():
        ssq[...] = jnp.zeros_like(ssq)

    ssq[...] += jnp.sum(v * v, axis=0, keepdims=True)


def merge_qkv(flags, own, parts, at_qkv, b_qkv):
    members, rows, width = own.shape
    heads = width // HD
    xs = len(parts)
    part_rows = rows // xs
    spec = pl.BlockSpec((1, part_rows, HD), lambda p, h, t, f: (p, 0, h))
    return pl.pallas_call(
        functools.partial(merge_cols_kernel, xs),
        grid_spec=pltpu.PrefetchScalarGridSpec(
            num_scalar_prefetch=1,
            grid=(members, heads, xs),
            in_specs=[pl.BlockSpec((1, part_rows, HD), lambda p, h, t, f: (p, t, h))]
            + [spec] * xs
            + [
                pl.BlockSpec((R, part_rows), lambda p, h, t, f: (p, t)),
                pl.BlockSpec((1, R, HD), lambda p, h, t, f: (p, 0, h)),
            ],
            out_specs=[
                pl.BlockSpec((part_rows, HD), lambda p, h, t, f: (t, h * members + p)),
                pl.BlockSpec((1, HD), lambda p, h, t, f: (0, h * members + p)),
            ],
        ),
        out_shape=[
            jax.ShapeDtypeStruct((rows, members * width), BF16),
            jax.ShapeDtypeStruct((1, members * width), F32),
        ],
        compiler_params=params(),
        cost_estimate=cost(2 * rows * width * members * 256, 4 * members * rows * width * 2),
    )(flags, own, *parts, at_qkv, b_qkv)


def merge_gu_kernel(x_parts, flags, own, *refs):
    parts = refs[:x_parts]
    at, b, vb, ssq = refs[x_parts:]
    h = pl.program_id(1)
    k = lax.rem(h - flags[1] + x_parts, x_parts)
    w = parts[0][0]
    for i in range(1, x_parts):
        w = jnp.where(k == i, parts[i][0], w)
    w = jnp.where(flags[0] == 1, own[0], w)
    v = w.astype(F32) + FACTOR * mm(at[0], b[0], 0, 0)
    vb[0] = v.astype(BF16)

    @pl.when(h == 0)
    def _():
        ssq[...] = jnp.zeros_like(ssq)

    ssq[0] += jnp.sum(v * v, axis=0, keepdims=True)


def merge_gu(flags, own, parts, at_gu, b_gu):
    members, rows, width = own.shape
    xs = len(parts)
    part_rows = rows // xs
    return pl.pallas_call(
        functools.partial(merge_gu_kernel, xs),
        grid_spec=pltpu.PrefetchScalarGridSpec(
            num_scalar_prefetch=1,
            grid=(members, xs),
            in_specs=[pl.BlockSpec((1, part_rows, width), lambda p, t, f: (p, t, 0))]
            + [pl.BlockSpec((1, part_rows, width), lambda p, t, f: (p, 0, 0))] * xs
            + [
                pl.BlockSpec((1, R, part_rows), lambda p, t, f: (p, 0, t)),
                pl.BlockSpec((1, R, width), lambda p, t, f: (p, 0, 0)),
            ],
            out_specs=[
                pl.BlockSpec((1, part_rows, width), lambda p, t, f: (p, t, 0)),
                pl.BlockSpec((1, 1, width), lambda p, t, f: (p, 0, 0)),
            ],
        ),
        out_shape=[
            jax.ShapeDtypeStruct((members, rows, width), BF16),
            jax.ShapeDtypeStruct((members, 1, width), F32),
        ],
        compiler_params=params(),
        cost_estimate=cost(2 * rows * width * members * 256, 4 * members * rows * width * 2),
    )(flags, own, *parts, at_gu, b_gu)


def merge_rows_kernel(x_parts, flags, own, *refs):
    parts = refs[:x_parts]
    at, b, vb = refs[x_parts:]
    k = lax.rem(pl.program_id(0) - flags[1] + x_parts, x_parts)
    w = parts[0][...]
    for i in range(1, x_parts):
        w = jnp.where(k == i, parts[i][...], w)
    w = jnp.where(flags[0] == 1, own[...], w)
    v = w.astype(F32) + FACTOR * mm(at[...], b[...], 0, 0)
    vb[...] = v.astype(BF16)


def merge_rows(flags, own, parts, at, b):
    rows, width = own.shape
    xs = len(parts)
    part = width // xs
    return pl.pallas_call(
        functools.partial(merge_rows_kernel, xs),
        grid_spec=pltpu.PrefetchScalarGridSpec(
            num_scalar_prefetch=1,
            grid=(xs,),
            in_specs=[pl.BlockSpec((rows, part), lambda t, f: (0, t))]
            + [pl.BlockSpec((rows, part), lambda t, f: (0, 0))] * xs
            + [
                pl.BlockSpec((R, rows), lambda t, f: (0, 0)),
                pl.BlockSpec((R, part), lambda t, f: (0, t)),
            ],
            out_specs=pl.BlockSpec((rows, part), lambda t, f: (0, t)),
        ),
        out_shape=jax.ShapeDtypeStruct((rows, width), BF16),
        compiler_params=params(),
        cost_estimate=cost(2 * rows * width * 256, 4 * rows * width * 2),
    )(flags, own, *parts, at, b)


def qkv_kernel(rows, blk, *refs):
    count = len(rows)
    xs = refs[:count]
    w, scale, cos0, cos1, sin0, sin1, out = refs[count:]
    cos = jnp.concatenate([cos0[...], cos1[...]], axis=0)
    sin = jnp.concatenate([sin0[...], sin1[...]], axis=0)
    at = 0
    for x, r in zip(xs, rows):
        z = mm(x[...], w[...]) * scale[...]
        co, si = cos[at : at + r], sin[at : at + r]
        q = z[:, :HD]
        k = z[:, HD : 2 * HD]
        q = (q * co + pltpu.roll(q, HD // 2, 1) * si) * HD ** (-0.5)
        k = k * co + pltpu.roll(k, HD // 2, 1) * si
        out[at : at + r, :HD] = q.astype(BF16)
        out[at : at + r, HD : 2 * HD] = k.astype(BF16)
        out[at : at + r, 2 * HD :] = z[:, 2 * HD :].astype(BF16)
        at += r


def qkv_chunk(blk, chunk, pieces, w, scale, cos, sin):
    rows = [p.shape[0] for p in pieces]
    total = sum(rows)
    tokens = total // 2
    depth, width = w.shape
    heads = width // (3 * HD)

    def table(k):
        return pl.BlockSpec((tokens, HD), lambda h, b: (b[2 * chunk + k], 0))

    return pl.pallas_call(
        functools.partial(qkv_kernel, rows),
        grid_spec=pltpu.PrefetchScalarGridSpec(
            num_scalar_prefetch=1,
            grid=(heads,),
            in_specs=[pl.BlockSpec((r, depth), lambda h, b: (0, 0)) for r in rows]
            + [
                pl.BlockSpec((depth, 3 * HD), lambda h, b: (0, h)),
                pl.BlockSpec((1, 3 * HD), lambda h, b: (0, h)),
                table(0),
                table(1),
                table(0),
                table(1),
            ],
            out_specs=pl.BlockSpec((total, 3 * HD), lambda h, b: (0, h)),
        ),
        out_shape=jax.ShapeDtypeStruct((total, width), BF16),
        compiler_params=params(),
        cost_estimate=cost(2 * total * depth * width, 2 * (depth * width + total * depth)),
    )(blk, *pieces, w, scale, cos, cos, sin, sin)


def masked(scores, low, first_key, first_query, valid_count):
    keys = first_key + lax.broadcasted_iota(jnp.int32, scores.shape, 0)
    queries = first_query + lax.broadcasted_iota(jnp.int32, (1, scores.shape[1]), 1)
    high = jnp.minimum(queries, valid_count - 1)
    allowed = ((keys >= low) & (keys <= high)) | (keys == queries)
    return jnp.where(allowed, scores, NEG)


def attn_fwd_kernel(n_chunks, tokens, bq, info, *refs):
    chunks = refs[:n_chunks]
    low, qkv_abs, att_abs, att_slot, lse, m_sc, l_sc, acc = refs[n_chunks:]
    i = pl.program_id(1)
    last = pl.num_programs(1) - 1
    slots = 2 * n_chunks
    valid_count = info[slots]

    @pl.when(i == 0)
    def _():
        for s in range(slots):
            start = pl.multiple_of(info[s] * tokens, tokens)
            qkv_abs[pl.ds(start, tokens), :] = chunks[s // 2][
                (s % 2) * tokens : (s % 2 + 1) * tokens, :
            ]

    q0 = pl.multiple_of(i * bq, bq)
    q = qkv_abs[pl.ds(q0, bq), :HD]
    lo = low[:, pl.ds(q0, bq)]
    m_sc[...] = jnp.full(m_sc.shape, NEG, F32)
    l_sc[...] = jnp.zeros_like(l_sc)
    acc[...] = jnp.zeros_like(acc)

    def step(j, carry):
        k0 = pl.multiple_of(j * bq, bq)
        k = qkv_abs[pl.ds(k0, bq), HD : 2 * HD]
        v = qkv_abs[pl.ds(k0, bq), 2 * HD :]
        s = masked(mm(k, q, 1, 1), lo, k0, q0, valid_count)
        m_old = m_sc[...]
        m_new = jnp.maximum(m_old, jnp.max(s, axis=0, keepdims=True))
        p = jnp.exp(s - m_new)
        alpha = jnp.exp(m_old - m_new)
        m_sc[...] = m_new
        l_sc[...] = l_sc[...] * alpha + jnp.sum(p, axis=0, keepdims=True)
        acc[...] = acc[...] * alpha + mm(v, p.astype(BF16), 0, 0)
        return carry

    lax.fori_loop(info[slots + 1 + i], i + 1, step, 0)
    total = l_sc[...]
    lse[0, :, pl.ds(q0, bq)] = m_sc[...] + jnp.log(total)
    att_abs[pl.ds(q0, bq), :] = (acc[...] / total).T.astype(BF16)

    @pl.when(i == last)
    def _():
        for s in range(slots):
            start = pl.multiple_of(info[s] * tokens, tokens)
            att_slot[s * tokens : (s + 1) * tokens, :] = att_abs[pl.ds(start, tokens), :]


def attn_fwd(info, chunks, low, tokens, bq):
    rows, width = chunks[0].shape
    heads = width // (3 * HD)
    seq = rows * len(chunks)
    n_blocks = seq // bq
    whole = pl.BlockSpec((seq, HD), lambda h, i, f: (0, h))
    return pl.pallas_call(
        functools.partial(attn_fwd_kernel, len(chunks), tokens, bq),
        grid_spec=pltpu.PrefetchScalarGridSpec(
            num_scalar_prefetch=1,
            grid=(heads, n_blocks),
            in_specs=[pl.BlockSpec((rows, 3 * HD), lambda h, i, f: (0, h))] * len(chunks)
            + [pl.BlockSpec((1, seq), lambda h, i, f: (0, 0))],
            out_specs=[
                pl.BlockSpec((seq, 3 * HD), lambda h, i, f: (0, h)),
                whole,
                whole,
                pl.BlockSpec((1, 1, seq), lambda h, i, f: (h, 0, 0)),
            ],
            scratch_shapes=[
                pltpu.VMEM((1, bq), F32),
                pltpu.VMEM((1, bq), F32),
                pltpu.VMEM((HD, bq), F32),
            ],
        ),
        out_shape=[
            jax.ShapeDtypeStruct((seq, width), BF16),
            jax.ShapeDtypeStruct((seq, heads * HD), BF16),
            jax.ShapeDtypeStruct((seq, heads * HD), BF16),
            jax.ShapeDtypeStruct((heads, 1, seq), F32),
        ],
        compiler_params=params(),
        cost_estimate=cost(
            4 * heads * seq * seq * HD, 2 * seq * width * 3, heads * seq * seq // 2
        ),
    )(info, *chunks, low)


def attn_bwd_kernel(
    n_chunks, tokens, bq, info, qkv, *refs
):
    dos = refs[:n_chunks]
    att, lse, low, cos, sin, scale, dz, dc, do_abs, delta, dq, dk, dv = refs[n_chunks:]
    slots = 2 * n_chunks
    valid_count = info[slots]
    seq = qkv.shape[0]
    n_blocks = seq // bq
    for s in range(slots):
        start = pl.multiple_of(info[s] * tokens, tokens)
        do_abs[pl.ds(start, tokens), :] = dos[s // 2][(s % 2) * tokens : (s % 2 + 1) * tokens, :]
    ones = jnp.ones((8, HD), F32)
    for i in range(n_blocks):
        r = slice(i * bq, (i + 1) * bq)
        prod = do_abs[r, :].astype(F32) * att[r, :].astype(F32)
        delta[:, r] = mm(ones, prod, 1, 1, lax.Precision.HIGHEST)[:1]
    dq[...] = jnp.zeros_like(dq)

    def outer(j, carry):
        k0 = pl.multiple_of(j * bq, bq)
        k = qkv[pl.ds(k0, bq), HD : 2 * HD]
        v = qkv[pl.ds(k0, bq), 2 * HD :]
        krow = pl.ds(k0, bq)
        dk[krow, :] = jnp.zeros((bq, HD), F32)
        dv[krow, :] = jnp.zeros((bq, HD), F32)

        def inner(i, c):
            @pl.when(info[slots + 1 + i] <= j)
            def _():
                q0 = pl.multiple_of(i * bq, bq)
                qrow = pl.ds(q0, bq)
                q = qkv[qrow, :HD]
                do = do_abs[qrow, :]
                s = masked(mm(k, q, 1, 1), low[:, qrow], k0, q0, valid_count)
                p = jnp.exp(s - lse[0, :, qrow])
                dp = mm(v, do, 1, 1)
                ds = (p * (dp - delta[:, qrow])).astype(BF16)
                dv[krow, :] += mm(p.astype(BF16), do)
                dk[krow, :] += mm(ds, q)
                dq[qrow, :] += mm(ds, k, 0, 0)

            return c

        return lax.fori_loop(j, n_blocks, inner, carry)

    lax.fori_loop(0, n_blocks, outer, 0)
    dcq = jnp.zeros((1, HD), F32)
    dck = jnp.zeros((1, HD), F32)
    dcv = jnp.zeros((1, HD), F32)
    half = HD // 2
    for s in range(slots):
        rows = pl.ds(pl.multiple_of(info[s] * tokens, tokens), tokens)
        co, si = cos[rows, :], sin[rows, :]
        out = slice(s * tokens, (s + 1) * tokens)

        def back(u):
            return u * co - pltpu.roll(u, half, 1) * si

        gq = back(dq[rows, :]) * HD ** (-0.5)
        gk = back(dk[rows, :])
        gv = dv[rows, :]
        q = back(qkv[rows, :HD].astype(F32)) * HD**0.5
        k = back(qkv[rows, HD : 2 * HD].astype(F32))
        v = qkv[rows, 2 * HD :].astype(F32)
        dcq += jnp.sum(gq * q, axis=0, keepdims=True)
        dck += jnp.sum(gk * k, axis=0, keepdims=True)
        dcv += jnp.sum(gv * v, axis=0, keepdims=True)
        dz[out, :HD] = (gq * scale[:, :HD]).astype(BF16)
        dz[out, HD : 2 * HD] = (gk * scale[:, HD : 2 * HD]).astype(BF16)
        dz[out, 2 * HD :] = (gv * scale[:, 2 * HD :]).astype(BF16)
    dc[:, :HD] = dcq / scale[:, :HD]
    dc[:, HD : 2 * HD] = dck / scale[:, HD : 2 * HD]
    dc[:, 2 * HD :] = dcv / scale[:, 2 * HD :]


def attn_bwd(info, qkv_abs, do_chunks, att_abs, lse, low, cos, sin, scale, tokens, bq):
    seq, width = qkv_abs.shape
    heads = width // (3 * HD)
    rows = do_chunks[0].shape[0]
    once = lambda h, f: (0, 0)
    head = lambda h, f: (0, h)
    return pl.pallas_call(
        functools.partial(attn_bwd_kernel, len(do_chunks), tokens, bq),
        grid_spec=pltpu.PrefetchScalarGridSpec(
            num_scalar_prefetch=1,
            grid=(heads,),
            in_specs=[pl.BlockSpec((seq, 3 * HD), head)]
            + [pl.BlockSpec((rows, HD), head)] * len(do_chunks)
            + [
                pl.BlockSpec((seq, HD), head),
                pl.BlockSpec((1, 1, seq), lambda h, f: (h, 0, 0)),
                pl.BlockSpec((1, seq), once),
                pl.BlockSpec((seq, HD), once),
                pl.BlockSpec((seq, HD), once),
                pl.BlockSpec((1, 3 * HD), head),
            ],
            out_specs=[
                pl.BlockSpec((seq, 3 * HD), head),
                pl.BlockSpec((1, 3 * HD), head),
            ],
            scratch_shapes=[
                pltpu.VMEM((seq, HD), BF16),
                pltpu.VMEM((1, seq), F32),
                pltpu.VMEM((seq, HD), F32),
                pltpu.VMEM((seq, HD), F32),
                pltpu.VMEM((seq, HD), F32),
            ],
        ),
        out_shape=[
            jax.ShapeDtypeStruct((seq, width), BF16),
            jax.ShapeDtypeStruct((1, width), F32),
        ],
        compiler_params=params(),
        cost_estimate=cost(
            10 * heads * seq * seq * HD, 2 * seq * width * 4, heads * seq * seq // 2
        ),
    )(info, qkv_abs, *do_chunks, att_abs, lse, low, cos, sin, scale)


def mlp_kernel(rows, *refs):
    count = len(rows)
    xs = refs[:count]
    dhid, w, scale, hid, dz, dx_own, dx_mate, dc = refs[count:]
    tokens = dx_own.shape[0]
    sum_gate = jnp.zeros(scale.shape[1:], F32)
    sum_up = jnp.zeros(scale.shape[1:], F32)
    at = 0
    for x, r in zip(xs, rows):
        part = slice(at, at + r)
        xv = x[...]
        zg = mm(xv, w[0])
        zu = mm(xv, w[1])
        gate = zg * scale[0]
        up = zu * scale[1]
        s = 1.0 / (1.0 + jnp.exp(-gate))
        act = gate * s
        hid[part, :] = (act * up).astype(BF16)
        d = dhid[part, :].astype(F32)
        dgate = d * up * s * (1.0 + gate * (1.0 - s))
        dup = d * act
        sum_gate += jnp.sum(dgate * zg, axis=0, keepdims=True)
        sum_up += jnp.sum(dup * zu, axis=0, keepdims=True)
        dzg = (dgate * scale[0]).astype(BF16)
        dzu = (dup * scale[1]).astype(BF16)
        dz[0, part, :] = dzg
        dz[1, part, :] = dzu
        dx = (mm(dzg, w[0], 1, 1) + mm(dzu, w[1], 1, 1)).astype(BF16)
        if at < tokens:
            dx_own[part, :] = dx
        else:
            dx_mate[at - tokens : at - tokens + r, :] = dx
        at += r
    dc[0] = sum_gate
    dc[1] = sum_up


def mlp_chunk(pieces, dhid, w, scale):
    rows = [p.shape[0] for p in pieces]
    total = sum(rows)
    _, depth, width = w.shape
    half = jax.ShapeDtypeStruct((total // 2, depth), BF16)
    return pl.pallas_call(
        functools.partial(mlp_kernel, rows),
        in_specs=[VM] * (len(pieces) + 3),
        out_specs=[VM] * 5,
        out_shape=[
            jax.ShapeDtypeStruct((total, width), BF16),
            jax.ShapeDtypeStruct((2, total, width), BF16),
            half,
            half,
            jax.ShapeDtypeStruct((2, 1, width), F32),
        ],
        compiler_params=params(),
        cost_estimate=cost(
            8 * total * depth * width, 4 * depth * width + 4 * total * depth, total * width
        ),
    )(*pieces, dhid, w, scale)


def rank_kernel(nx, nd, spans, *refs):
    xs = refs[:nx]
    ds = refs[nx : nx + nd]
    at, b, v, s, ga, gb = refs[nx + nd :]
    ga_sum = None
    gb_sum = None
    for xi, xa, di, da, r in spans:
        x = xs[xi][xa : xa + r, :]
        d = ds[di][da : da + r, :]
        u = mm(d, b[...], 1, 1).astype(BF16)
        t = mm(x, at[...], 1, 1).astype(BF16)
        a_part = mm(u, x, 0, 0)
        b_part = mm(t, d, 0, 0)
        ga_sum = a_part if ga_sum is None else ga_sum + a_part
        gb_sum = b_part if gb_sum is None else gb_sum + b_part
    sv = s[...]
    sb = (b[...].astype(F32) * sv).astype(BF16)
    ga[...] = FACTOR * (ga_sum - mm(sb, v[...], 1, 1))
    gb[...] = FACTOR * (gb_sum - mm(at[...], v[...]) * sv)


def rank_grads(xs, ds, at, b, v, s):
    spans = []
    xi = xa = di = da = 0
    while xi < len(xs):
        r = min(xs[xi].shape[0] - xa, ds[di].shape[0] - da)
        spans.append((xi, xa, di, da, r))
        xa += r
        da += r
        if xa == xs[xi].shape[0]:
            xi, xa = xi + 1, 0
        if da == ds[di].shape[0]:
            di, da = di + 1, 0
    total = sum(x.shape[0] for x in xs)
    rank, n_in = at.shape
    n_out = b.shape[1]
    return pl.pallas_call(
        functools.partial(rank_kernel, len(xs), len(ds), tuple(spans)),
        in_specs=[VM] * (len(xs) + len(ds) + 4),
        out_specs=[VM] * 2,
        out_shape=[
            jax.ShapeDtypeStruct((rank, n_in), F32),
            jax.ShapeDtypeStruct((rank, n_out), F32),
        ],
        compiler_params=params(),
        cost_estimate=cost(
            4 * total * (n_in + n_out) * 256, 2 * (total * (n_in + n_out) + n_in * n_out)
        ),
    )(*xs, *ds, at, b, v, s)


def norm_forward(values):
    inverse = lax.rsqrt(jnp.mean(values * values, axis=-1, keepdims=True) + EPSILON)
    return values * inverse, inverse


def norm_backward(grad_normed, unit_vals, inverse, gain):
    scaled = grad_normed * gain
    return inverse * (scaled - unit_vals * jnp.mean(scaled * unit_vals, axis=-1, keepdims=True))


def after(value, *others):
    return lax.optimization_barrier((value,) + others)[0]


def on_device(
    sizes,
    layer_input,
    cotangent,
    segment_ids,
    token_valid,
    norm_attn,
    norm_mlp,
    base_qkv,
    base_attn_out,
    base_gate_up,
    base_down,
    rank_in_attn,
    rank_out_attn,
    magnitude_qkv,
    magnitude_out,
    rank_in_mlp,
    rank_out_mlp,
    magnitude_mlp,
    rank_in_down,
    rank_out_down,
    magnitude_down,
):
    X, C, ZH, ZL, Y = (sizes[a] for a in AXES)
    ix, ic, izh, izl, iy = (lax.axis_index(a) for a in AXES)
    dp, mp = X * C, ZH * ZL * Y
    n_dev = dp * mp
    tokens, model = layer_input.shape
    seq = segment_ids.shape[0]
    width = base_qkv.shape[2]
    hidden = base_gate_up.shape[2]
    heads = width // HD
    a_w = rank_in_attn.shape[1]
    f_w = rank_in_down.shape[0]
    used = 11 * a_w + 3 * f_w
    packed_w = -(-used // 128) * 128
    bq = min(512, seq)
    stay = ic == izh

    def from_offset(a, axis, k):
        n = sizes[axis]
        return lax.ppermute(a, axis, [(s, (s - k) % n) for s in range(n)])

    def to_offset(a, axis, k):
        n = sizes[axis]
        return lax.ppermute(a, axis, [(s, (s + k) % n) for s in range(n)])

    def mate(a):
        return from_offset(a, "c", 1)

    offsets = [(dz, dy) for dz in range(ZL) for dy in range(Y)]

    def chips(a, off, sign):
        dz, dy = off
        perm = []
        for z in range(ZL):
            for y in range(Y):
                perm.append((z * Y + y, (z + sign * dz) % ZL * Y + (y + sign * dy) % Y))
        return lax.ppermute(a, ("zl", "y"), perm)

    def swap_rows(a):
        return lax.ppermute(a, ("c", "zh"), [(1, 2), (2, 1)])

    def gather_square(a):
        if ZL == 2 and Y == 2:
            half = a.shape[0] // 2
            py, pz = chips(a, (0, 1), -1), chips(a, (1, 0), -1)
            d0 = chips(pz[:half], (0, 1), -1)
            d1 = chips(py[half:], (1, 0), -1)
            lists = [[a], [py], [pz], [d0, d1]]
        else:
            lists = [[a]] + [[chips(a, o, -1)] for o in offsets[1:]]
        return [pieces + [mate(p) for p in pieces] for pieces in lists]

    def scatter_square(parts):
        total = None
        for o in list(range(len(offsets)))[::-1]:
            own, other = parts[o]
            got = mate(other)
            block = own.astype(F32) + got.astype(F32)
            if o:
                block = chips(block.astype(BF16), offsets[o], 1).astype(F32)
            total = block if total is None else total + block
        return total

    def square_sum(a):
        total = a
        for axis in ("c", "zl", "y"):
            total = sum((from_offset(total, axis, k) for k in range(1, sizes[axis])), total)
        return total

    d = np.arange(n_dev)
    d_dp, d_mp = d // mp, d % mp

    def digit(values, own, n):
        return (jnp.asarray(values, jnp.int32) - own + n) % n

    order = digit(d_dp % 2, ic, C)
    order = order * X + digit(d_dp // 2, ix, X)
    order = order * Y + digit(d_mp % Y, iy, Y)
    order = order * ZL + digit(d_mp // Y % ZL, izl, ZL)
    order = order * ZH + digit(d_mp // (Y * ZL), izh, ZH)
    shard = (ic * ZL + izl) * Y + iy
    shard_here = (izh * ZL + izl) * Y + iy
    where_ = jnp.stack([shard, shard_here]).astype(jnp.int32)
    flags = jnp.stack([stay.astype(jnp.int32), ix]).astype(jnp.int32)
    slots = []
    for dz, dy in offsets:
        for k in range(2):
            slots.append(((ic + k) % 2 * ZL + (izl + dz) % ZL) * Y + (iy + dy) % Y)
    blk = jnp.stack(slots).astype(jnp.int32)

    packed = pl.pallas_call(
        functools.partial(pack_kernel, a_w, f_w),
        in_specs=[VM] * 10,
        out_specs=VM,
        out_shape=jax.ShapeDtypeStruct((1, R + 1, packed_w), BF16),
    )(
        rank_in_attn,
        rank_out_attn,
        magnitude_qkv,
        magnitude_out[None],
        rank_in_mlp,
        rank_out_mlp,
        magnitude_mlp,
        rank_in_down,
        rank_out_down,
        magnitude_down[None],
    )

    moved_input = swap_rows(layer_input)
    gathered = packed
    for axis in ("zh", "zl", "y", "x", "c"):
        gathered = jnp.concatenate(
            [gathered] + [from_offset(gathered, axis, k) for k in range(1, sizes[axis])], axis=0
        )

    def sds(shape, dtype=BF16):
        return jax.ShapeDtypeStruct(shape, dtype)

    (
        at_qkv, at_gu, at_o, at_d, at_o0, at_d0, b_qkv, b_gu, b_o, b_d, m_qkv, m_o, m_gu, m_d,
    ) = pl.pallas_call(
        functools.partial(unpack_kernel, a_w, f_w, dp),
        in_specs=[SM, SM, VM],
        out_specs=[VM] * 14,
        out_shape=[
            sds((3 * R, model)),
            sds((2, R, model)),
            sds((R, width)),
            sds((R, hidden)),
            sds((R, width)),
            sds((R, hidden)),
            sds((3, R, width)),
            sds((2, R, hidden)),
            sds((R, model)),
            sds((R, model)),
            sds((3, 1, width), F32),
            sds((1, model), F32),
            sds((2, 1, hidden), F32),
            sds((1, model), F32),
        ],
    )(order, where_, gathered)

    def fetch(w, axis):
        part = w.shape[axis] // X
        mine = lax.dynamic_slice_in_dim(w, ix * part, part, axis)
        mine = lax.ppermute(mine, ("c", "zh"), [(0, 1), (3, 2)])
        parts = [mine]
        for k in range(1, X):
            perm = []
            for x in range(X):
                for cz in (1, 2):
                    perm.append((x * 4 + cz, (x - k) % X * 4 + cz))
            parts.append(lax.ppermute(mine, ("x", "c", "zh"), perm))
        return parts

    parts_qkv = fetch(base_qkv, 1)
    local_input = jnp.where(stay, layer_input, moved_input)
    parts_o = fetch(after(base_attn_out, local_input), 1)
    moved_cot = swap_rows(after(cotangent, local_input))
    parts_gu = fetch(after(base_gate_up, parts_qkv[-1]), 1)
    parts_d = fetch(after(base_down, parts_qkv[-1]), 1)
    local_cot = jnp.where(stay, cotangent, moved_cot)

    gain_one = norm_attn.astype(F32)
    gain_two = norm_mlp.astype(F32)
    input_full = local_input.astype(F32)
    unit_one, inverse_one = norm_forward(input_full)
    normed_one = (unit_one * gain_one).astype(BF16)
    one = gather_square(normed_one)

    seg_mate = mate(segment_ids)
    valid_mate = mate(token_valid)
    segments = jnp.where(stay, segment_ids, seg_mate)
    valid = jnp.where(stay, token_valid, valid_mate)
    steps = jnp.arange(seq, dtype=jnp.int32)
    earlier = jnp.concatenate([segments[:1] - 1, segments[:-1]])
    first = lax.cummax(jnp.where(segments != earlier, steps, 0), axis=0)
    low = first[None]
    positions = steps - first
    frequency = ROPE_BASE ** (-(2.0 * jnp.arange(HD // 2, dtype=F32)) / HD)
    angle = positions.astype(F32)[:, None] * frequency[None, :]
    cos_half, sin_half = jnp.cos(angle), jnp.sin(angle)
    cos = jnp.concatenate([cos_half, cos_half], axis=1)
    sin = jnp.concatenate([-sin_half, sin_half], axis=1)
    info = jnp.concatenate([blk, jnp.sum(valid)[None].astype(jnp.int32), first[::bq] // bq])

    v_qkv, square_qkv = merge_qkv(flags, base_qkv, parts_qkv, at_qkv, b_qkv)
    norms_qkv = jnp.sqrt(square_qkv)

    def head_major(a):
        k = a.shape[1]
        return a.reshape(3, k, heads, HD).transpose(1, 2, 0, 3).reshape(k, 3 * width)

    mags_qkv = head_major(m_qkv)
    scale_qkv = mags_qkv / norms_qkv

    def rows_square(base, at0, b):
        v = base.astype(F32) + FACTOR * mm(at0, b, 0, 0)
        return jnp.sum(v * v, axis=0)

    squares = jnp.stack(
        [rows_square(base_attn_out, at_o0, b_o), rows_square(base_down, at_d0, b_d)]
    )
    for axis in ("zh", "zl", "y"):
        squares = sum((from_offset(squares, axis, k) for k in range(1, sizes[axis])), squares)
    norms_rows = jnp.sqrt(squares)
    norms_o, norms_d = norms_rows[0:1], norms_rows[1:2]
    scale_o = m_o / norms_o
    scale_d = m_d / norms_d

    qkv = [
        qkv_chunk(blk, o, one[o], v_qkv, scale_qkv, cos, sin) for o in range(len(offsets))
    ]
    qkv_abs, att_abs, att_slot, lse = attn_fwd(info, qkv, low, tokens, bq)
    v_o = merge_rows(flags, base_attn_out, parts_o, at_o, b_o)

    def slot(a, o, k):
        at = (2 * o + k) * tokens
        return lax.slice_in_dim(a, at, at + tokens, axis=0)

    parts = [
        tuple(mm(slot(att_slot, o, k), v_o).astype(BF16) for k in range(2))
        for o in range(len(offsets))
    ]
    summed_out = scatter_square(parts)
    residual = input_full + summed_out * scale_o
    unit_two, inverse_two = norm_forward(residual)
    normed_two = (unit_two * gain_two).astype(BF16)
    two = gather_square(normed_two)

    v_gu, square_gu = merge_gu(flags, base_gate_up, parts_gu, at_gu, b_gu)
    norms_gu = jnp.sqrt(square_gu)
    scale_gu = m_gu / norms_gu
    v_d = merge_rows(flags, base_down, parts_d, at_d, b_d)
    grad_output = local_cot.astype(F32)
    low_down = (grad_output * scale_d).astype(BF16)
    down = gather_square(after(low_down, qkv[-1]))
    hid, dz_gu, parts, dc_gu = [], [], [], 0.0
    for o in range(len(offsets)):
        dhid = jnp.concatenate([mm(p, v_d, 1, 1) for p in down[o]], axis=0)
        h, dz, own, other, dc = mlp_chunk(two[o], dhid, v_gu, scale_gu)
        hid.append(h)
        dz_gu.append(dz)
        parts.append((own, other))
        dc_gu = dc_gu + dc
    grad_normed_two = scatter_square(parts)
    grad_residual = grad_output + norm_backward(grad_normed_two, unit_two, inverse_two, gain_two)
    low_out = (grad_residual * scale_o).astype(BF16)
    out = gather_square(low_out)

    do_chunks = [
        jnp.concatenate([mm(p, v_o, 1, 1).astype(BF16) for p in out[o]], axis=0)
        for o in range(len(offsets))
    ]
    dz_qkv, dc_qkv = attn_bwd(
        info, qkv_abs, do_chunks, att_abs, lse, low, cos, sin, scale_qkv, tokens, bq
    )

    parts = [
        tuple(
            mm(lax.slice_in_dim(h, k * tokens, (k + 1) * tokens, axis=0), v_d).astype(BF16)
            for k in range(2)
        )
        for h in [after(h, low_out) for h in hid]
    ]
    summed_down = scatter_square(parts)
    output_here = (residual + summed_down * scale_d).astype(BF16)
    layer_output = jnp.where(stay, output_here, swap_rows(output_here))

    col_own = jnp.stack(
        [
            jnp.sum(grad_residual * summed_out, axis=0),
            jnp.sum(grad_output * summed_down, axis=0),
        ]
    )
    col_row = square_sum(col_own)

    parts = [
        tuple(mm(slot(dz_qkv, o, k), v_qkv, 1, 1).astype(BF16) for k in range(2))
        for o in range(len(offsets))
    ]
    grad_normed_one = scatter_square(parts)
    grad_here = grad_residual + norm_backward(grad_normed_one, unit_one, inverse_one, gain_one)
    input_grad = jnp.where(stay, grad_here, swap_rows(grad_here.astype(BF16)).astype(F32))

    def flat(lists):
        return [p for pieces in lists for p in pieces]

    def shrink(col, mags, norms):
        return col * mags / (norms * norms * norms)

    ga_gu, gb_gu = [], []
    s_gu = shrink(dc_gu, m_gu, norms_gu)
    for p in range(2):
        ga, gb = rank_grads(
            flat(two), [dz[p] for dz in dz_gu], at_gu[p], b_gu[p], v_gu[p], s_gu[p]
        )
        ga_gu.append(ga)
        gb_gu.append(gb)
    ga_o, gb_o = rank_grads(
        [att_slot], flat(out), at_o, b_o, v_o, shrink(col_row[0:1], m_o, norms_o)
    )
    ga_d, gb_d = rank_grads(
        hid, flat(down), at_d, b_d, v_d, shrink(col_row[1:2], m_d, norms_d)
    )
    b_blocks = jnp.concatenate(
        [
            head_major(jnp.stack([b_qkv[q] if q == p else jnp.zeros_like(b_qkv[q]) for q in range(3)]))
            for p in range(3)
        ],
        axis=0,
    )
    ga_qkv, gb_all = rank_grads(
        flat(one), [dz_qkv], at_qkv, b_blocks, v_qkv, shrink(dc_qkv, mags_qkv, norms_qkv)
    )
    gb_qkv = jnp.stack(
        [
            gb_all[p * R : (p + 1) * R].reshape(R, heads, 3, HD)[:, :, p].reshape(R, width)
            for p in range(3)
        ]
    )
    mag_qkv = (dc_qkv / norms_qkv).reshape(heads, 3, HD).transpose(1, 0, 2).reshape(3, 1, width)
    mag_full = jnp.concatenate([col_own[0:1] / norms_o, col_own[1:2] / norms_d], axis=0)

    grads = pl.pallas_call(
        functools.partial(pack_grads_kernel, a_w, f_w, dp),
        in_specs=[SM, SM] + [VM] * 9,
        out_specs=VM,
        out_shape=jax.ShapeDtypeStruct((n_dev, R + 1, packed_w), F32),
    )(
        order,
        where_,
        jnp.concatenate([ga_qkv] + ga_gu, axis=0),
        jnp.concatenate([gb_o, gb_d], axis=0),
        mag_full,
        ga_o,
        ga_d,
        gb_qkv,
        jnp.stack(gb_gu),
        mag_qkv,
        dc_gu / norms_gu,
    )
    for axis in ("c", "x", "y", "zl", "zh"):
        m = grads.shape[0] // sizes[axis]
        grads = sum(
            (to_offset(grads[k * m : (k + 1) * m], axis, k) for k in range(1, sizes[axis])),
            grads[:m],
        )
    g = grads[0]
    gm = g[R]
    g = g[:R]

    def cols(start, count, w):
        return g[:, start : start + count * w].reshape(R, count, w)

    grad_in_attn = cols(0, 4, a_w).transpose(1, 2, 0)
    grad_in_mlp = cols(4 * a_w, 2, a_w).transpose(1, 2, 0)
    grad_in_down = g[:, 6 * a_w : 6 * a_w + f_w].T
    b_at = 6 * a_w + f_w
    grad_out_attn = cols(b_at, 4, a_w).transpose(1, 0, 2)
    grad_out_mlp = cols(b_at + 4 * a_w, 2, f_w).transpose(1, 0, 2)
    grad_out_down = g[:, b_at + 4 * a_w + 2 * f_w : used]
    grad_mag_qkv = gm[: 3 * a_w].reshape(3, a_w)
    grad_mag_out = gm[3 * a_w : 4 * a_w]
    grad_mag_mlp = gm[4 * a_w : 4 * a_w + 2 * f_w].reshape(2, f_w)
    grad_mag_down = gm[4 * a_w + 2 * f_w : 5 * a_w + 2 * f_w]
    return (
        layer_output,
        input_grad,
        grad_in_attn,
        grad_out_attn,
        grad_mag_qkv,
        grad_mag_out,
        grad_in_mlp,
        grad_out_mlp,
        grad_mag_mlp,
        grad_in_down,
        grad_out_down,
        grad_mag_down,
    )


def solution(mesh):
    dp, mp = mesh.shape["dp"], mesh.shape["mp"]
    shape = (dp // 2, 2, 2, 2, mp // 4)
    fine = Mesh(mesh.devices.reshape(shape), AXES)
    rows, cols = ("x", "c"), ("zh", "zl", "y")
    both = rows + cols
    return jax.shard_map(
        functools.partial(on_device, dict(zip(AXES, shape))),
        mesh=fine,
        in_specs=(
            P(both, None),
            P(both, None),
            P(rows),
            P(rows),
            P(),
            P(),
            P(None, None, cols),
            P(cols, None),
            P(None, None, cols),
            P(cols, None),
            P(None, both, None),
            P(None, None, both),
            P(None, both),
            P(both),
            P(None, both, None),
            P(None, None, both),
            P(None, both),
            P(both, None),
            P(None, both),
            P(both),
        ),
        out_specs=(
            P(both, None),
            P(both, None),
            P(None, both, None),
            P(None, None, both),
            P(None, both),
            P(both),
            P(None, both, None),
            P(None, None, both),
            P(None, both),
            P(both, None),
            P(None, both),
            P(both),
        ),
        check_vma=False,
    )
```

time: 2660 us -> 850 us (0.32)
  the two profiles are of different devices: /device:TPU:0 before, /device:TPU:3 now
where the time goes in v1:
time: 850 us; the launch traced here: 839 us
  Pallas kernels  240 us (28%)
  waiting for transfers between devices  230 us (27%)
  starting transfers between devices  154 us (18%)
  local copies, waits for them, and re-layouts  80.1 us (9%)
  matrix products  73.6 us (9%)
  other arithmetic  57.1 us (7%)
    ppermute x28, waiting for transfers between devices, chips(): return lax.ppermute(a, ('zl', 'y'), perm)  155 us
    ppermute x49, starting transfers between devices, from_offset(): return lax.ppermute(a, axis, [(s, (s - k) % n) for s in range(n)])  85 us
    dot_general x46, matrix products, mm(): lax.dot_general(left, right, (((lc,), (rc,)), ((), ())), preferred_elemen...  73.6 us
    pallas_call x5, Pallas kernels, rank_grads(): pl.pallas_call(functools.partial(rank_kernel, len(xs), len(ds), tuple(spa...  64.8 us
    pallas_call x4, Pallas kernels, mlp_chunk(): pl.pallas_call(functools.partial(mlp_kernel, rows), in_specs=[VM] * (len(...  53.7 us
    pallas_call x1, Pallas kernels, attn_bwd(): pl.pallas_call(functools.partial(attn_bwd_kernel, len(do_chunks), tokens,...  32.1 us
    pallas_call x4, Pallas kernels, qkv_chunk(): pl.pallas_call(functools.partial(qkv_kernel, rows), grid_spec=pltpu.Prefe...  25.1 us
    pallas_call x1, Pallas kernels, attn_fwd(): pl.pallas_call(functools.partial(attn_fwd_kernel, len(chunks), tokens, bq...  24.9 us
  transfers between devices with their start and end apart: 94, of which 24 were waited for; matrix products, arithmetic and copies ran while one was open for 22% of the time, Pallas kernels for 28%

profile of v1, /device:TPU:3, one launch (start us, length us, event | category | flops | bytes accessed | tf_op | source)
XLA Modules:
  0.0 839.1 jit_solution(3053685737096473981)
XLA Ops:
  19.2 8.5 %copy.98.own = bf16[2,2048,704]{2,1,0:T(8,128)(2,1)} copy(bf16[2,2048,704]{1,2,0:T(8,128)(2,1)} %param.33) | data formatting | bytes 11534336 | tf_op args[8]
  55.7 6.8 collective-permute-start.10
  76.0 29.6 %collective-permute-start.28 = (f32[2,2048]{1,0:T(2,128)S(1)}, f32[2,2048]{1,0:T(2,128)S(1)}, u32[]{:S(2)}, u32[]{:S(2)}) collective-permute-start(f32[2,2048]{1,0:T(2,128)S(1)} %pad_maximum_fusion.19), channel_id=1, source_target_pairs={{0,4},{4,0},{1,5},{5,1},{2,6},{6,2},{3,7},{7,3},{8,12},{12,8},{9,1... | collective-permute-start | bytes 49160 | tf_op jit(solution)/shard_map/ppermute | solution.py:722
  107.0 15.1 %collective-permute-start.29 = (f32[2,2048]{1,0:T(2,128)S(1)}, f32[2,2048]{1,0:T(2,128)S(1)}, u32[]{:S(2)}, u32[]{:S(2)}) collective-permute-start(f32[2,2048]{1,0:T(2,128)S(1)} %fusion.91), channel_id=1, source_target_pairs={{0,2},{2,0},{1,3},{3,1},{4,6},{6,4},{5,7},{7,5},{8,10},{10,8},{9,1... | collective-permute-start | bytes 49160 | tf_op jit(solution)/shard_map/ppermute | solution.py:722
  137.8 11.6 %collective-permute-done.20.refs_1_ = bf16[256,1024]{1,0:T(8,128)(2,1)} collective-permute-done((bf16[256,1024]{1,0:T(8,128)(2,1)S(1)}, bf16[256,1024]{1,0:T(8,128)(2,1)}, u32[]{:S(2)}, u32[]{:S(2)}) %collective-permute-start.20) | collective-permute-done | bytes 524320 | tf_op jit(solution)/shard_map/ppermute | solution.py:855
  155.0 11.3 %shard_map.330 = (bf16[2048,768]{1,0:T(8,128)(2,1)}, f32[1,768]{1,0:T(1,128)}) custom-call(s32[2]{0:T(128)} %pad_add_fusion.flags, bf16[3,2048,256]{2,1,0:T(8,128)(2,1)} %own.4, bf16[3,1024,256]{2,1,0:T(8,128)(2,1)} %collective-permute-done.4.refs_0_, bf16[3,1024,256]{2,1,0:T(8,128)(2,1)} %copy-done.29, bf16[48,2048]{1,0:T(8,128)(2,1)} %get-tuple-element.75.refs_2_.refs_11_, ...), custom_call_target="tpu_custom_call" | custom-call | flops 805306368 | bytes 12582912 | tf_op jit(solution)/shard_map/pallas_call | solution.py:181
  184.6 6.3 shard_map.333.refs_2_
  190.9 6.3 shard_map.334.refs_3_
  197.3 24.9 %shard_map.335 = (bf16[2048,768]{1,0:T(8,128)(2,1)}, bf16[2048,256]{1,0:T(8,128)(2,1)}, bf16[2048,256]{1,0:T(8,128)(2,1)}, f32[2,1,2048]{2,1,0:T(1,128)}) custom-call(s32[13]{0:T(128)} %concatenate.69.info, bf16[512,768]{1,0:T(8,128)(2,1)} %shard_map.331.refs_0_, bf16[512,768]{1,0:T(8,128)(2,1)} %shard_map.332.refs_1_, bf16[512,768]{1,0:T(8,128)(2,1)} %shard_map.333.refs_2_, ...), custom_call_target="tpu_custom_call" | custom-call | flops 4294967296 | bytes 9437184 | tf_op jit(solution)/shard_map/pallas_call | solution.py:404
  232.3 12.0 %collective-permute-start.40 = (bf16[704,1024]{1,0:T(8,128)(2,1)S(1)}, bf16[704,1024]{1,0:T(8,128)(2,1)}, u32[]{:S(2)}, u32[]{:S(2)}) collective-permute-start(bf16[704,1024]{1,0:T(8,128)(2,1)S(1)} %constant_dynamic-slice_fusion.1), channel_id=1, source_target_pairs={{0,4},{12,8},{1,5},{13,9},{2,6},{14,10},{3,7},{15,11},{16,20},{28,... | collective-permute-start | bytes 4325384 | tf_op jit(solution)/shard_map/ppermute | solution.py:848
  257.4 13.2 %collective-permute-done.38.refs_8_ = bf16[256,2048]{1,0:T(8,128)(2,1)} collective-permute-done((bf16[256,2048]{1,0:T(8,128)(2,1)}, bf16[256,2048]{1,0:T(8,128)(2,1)}, u32[]{:S(2)}, u32[]{:S(2)}) %collective-permute-start.38) | collective-permute-done | bytes 1048608 | tf_op jit(solution)/shard_map/ppermute | solution.py:739
  290.7 33.3 %collective-permute-done.24 = bf16[256,2048]{1,0:T(8,128)(2,1)} collective-permute-done((bf16[256,2048]{1,0:T(8,128)(2,1)}, bf16[256,2048]{1,0:T(8,128)(2,1)}, u32[]{:S(2)}, u32[]{:S(2)}) %collective-permute-start.24) | collective-permute-done | bytes 1048608 | tf_op jit(solution)/shard_map/ppermute | solution.py:739
  324.0 22.4 %collective-permute-done.22 = bf16[256,2048]{1,0:T(8,128)(2,1)} collective-permute-done((bf16[256,2048]{1,0:T(8,128)(2,1)}, bf16[256,2048]{1,0:T(8,128)(2,1)}, u32[]{:S(2)}, u32[]{:S(2)}) %collective-permute-start.22) | collective-permute-done | bytes 1048608 | tf_op jit(solution)/shard_map/ppermute | solution.py:739
  390.6 16.4 %collective-permute-done.31.refs_0_.refs_4_ = bf16[256,2048]{1,0:T(8,128)(2,1)} collective-permute-done((bf16[256,2048]{1,0:T(8,128)(2,1)}, bf16[256,2048]{1,0:T(8,128)(2,1)}, u32[]{:S(2)}, u32[]{:S(2)}) %collective-permute-start.31) | collective-permute-done | bytes 1048608 | tf_op jit(solution)/shard_map/ppermute | solution.py:739
  431.8 10.5 %shard_map.338 = (bf16[2,2048,704]{2,1,0:T(8,128)(2,1)}, f32[2,1,704]{2,1,0:T(1,128)}) custom-call(s32[2]{0:T(128)} %pad_add_fusion.flags, bf16[2,2048,704]{2,1,0:T(8,128)(2,1)} %copy.98.own, bf16[2,1024,704]{2,1,0:T(8,128)(2,1)} %copy.99.refs_0_, bf16[2,1024,704]{2,1,0:T(8,128)(2,1)} %copy.100.refs_1_, bf16[2,16,2048]{2,1,0:T(8,128)(2,1)} %get-tuple-element.94.refs_2_, ...), custom_call_target="tpu_custom_call" | custom-call | flops 1476395008 | bytes 23068672 | tf_op jit(solution)/shard_map/pallas_call | solution.py:229
  443.6 12.1 %shard_map.342 = (bf16[512,704]{1,0:T(8,128)(2,1)}, bf16[2,512,704]{2,1,0:T(8,128)(2,1)}, bf16[256,2048]{1,0:T(8,128)(2,1)}, bf16[256,2048]{1,0:T(8,128)(2,1)}, f32[2,1,704]{2,1,0:T(1,128)}) custom-call(bf16[256,2048]{1,0:T(8,128)(2,1)} %multiply_convert_fusion.1.refs_0_, bf16[256,2048]{1,0:T(8,128)(2,1)} %collective-permute-done.58.refs_1_, ...), custom_call_target="tpu_custom_call" | custom-call | flops 5905580032 | bytes 9961472 | tf_op jit(solution)/shard_map/pallas_call | solution.py:598
  456.2 12.1 %shard_map.341 = (bf16[512,704]{1,0:T(8,128)(2,1)}, bf16[2,512,704]{2,1,0:T(8,128)(2,1)}, bf16[256,2048]{1,0:T(8,128)(2,1)}, bf16[256,2048]{1,0:T(8,128)(2,1)}, f32[2,1,704]{2,1,0:T(1,128)}) custom-call(bf16[256,2048]{1,0:T(8,128)(2,1)} %collective-permute-done.33.refs_0_.refs_2_, bf16[256,2048]{1,0:T(8,128)(2,1)} %collective-permute-done.54.refs_1_.refs_3_, ...), custom_call_target="tpu_custom_call" | custom-call | flops 5905580032 | bytes 9961472 | tf_op jit(solution)/shard_map/pallas_call | solution.py:598
  468.3 12.3 %shard_map.340 = (bf16[512,704]{1,0:T(8,128)(2,1)}, bf16[2,512,704]{2,1,0:T(8,128)(2,1)}, bf16[256,2048]{1,0:T(8,128)(2,1)}, bf16[256,2048]{1,0:T(8,128)(2,1)}, f32[2,1,704]{2,1,0:T(1,128)}) custom-call(bf16[256,2048]{1,0:T(8,128)(2,1)} %collective-permute-done.31.refs_0_.refs_4_, bf16[256,2048]{1,0:T(8,128)(2,1)} %collective-permute-done.50.refs_1_.refs_5_, ...), custom_call_target="tpu_custom_call" | custom-call | flops 5905580032 | bytes 9961472 | tf_op jit(solution)/shard_map/pallas_call | solution.py:598
  481.1 17.2 %shard_map.339 = (bf16[512,704]{1,0:T(8,128)(2,1)}, bf16[2,512,704]{2,1,0:T(8,128)(2,1)}, bf16[256,2048]{1,0:T(8,128)(2,1)}, bf16[256,2048]{1,0:T(8,128)(2,1)}, f32[2,1,704]{2,1,0:T(1,128)}) custom-call(bf16[128,2048]{1,0:T(8,128)(2,1)} %collective-permute-done.32.refs_0_.refs_6_, bf16[128,2048]{1,0:T(8,128)(2,1)} %collective-permute-done.34.refs_1_.refs_7_, ...), custom_call_target="tpu_custom_call" | custom-call | flops 5905580032 | bytes 9961472 | tf_op jit(solution)/shard_map/pallas_call | solution.py:598
  521.0 13.3 %shard_map.346 = (f32[16,2048]{1,0:T(8,128)}, f32[16,704]{1,0:T(8,128)}) custom-call(bf16[256,2048]{1,0:T(8,128)(2,1)} %multiply_convert_fusion.1.refs_0_, bf16[256,2048]{1,0:T(8,128)(2,1)} %collective-permute-done.58.refs_1_, bf16[256,2048]{1,0:T(8,128)(2,1)} %collective-permute-done.33.refs_0_.refs_2_, ...), custom_call_target="tpu_custom_call" | custom-call | flops 5771362304 | bytes 14155776 | tf_op jit(solution)/shard_map/pallas_call | solution.py:652
  534.3 13.8 %shard_map.345 = (f32[16,2048]{1,0:T(8,128)}, f32[16,704]{1,0:T(8,128)}) custom-call(bf16[256,2048]{1,0:T(8,128)(2,1)} %multiply_convert_fusion.1.refs_0_, bf16[256,2048]{1,0:T(8,128)(2,1)} %collective-permute-done.58.refs_1_, bf16[256,2048]{1,0:T(8,128)(2,1)} %collective-permute-done.33.refs_0_.refs_2_, ...), custom_call_target="tpu_custom_call" | custom-call | flops 5771362304 | bytes 14155776 | tf_op jit(solution)/shard_map/pallas_call | solution.py:652
  549.5 15.4 %collective-permute-done.49 = bf16[256,2048]{1,0:T(8,128)(2,1)} collective-permute-done((bf16[256,2048]{1,0:T(8,128)(2,1)}, bf16[256,2048]{1,0:T(8,128)(2,1)}, u32[]{:S(2)}, u32[]{:S(2)}) %collective-permute-start.49) | collective-permute-done | bytes 1048608 | tf_op jit(solution)/shard_map/ppermute | solution.py:739
  582.0 16.3 %collective-permute-done.70.refs_3_ = bf16[256,2048]{1,0:T(8,128)(2,1)S(1)} collective-permute-done((bf16[256,2048]{1,0:T(8,128)(2,1)S(1)}, bf16[256,2048]{1,0:T(8,128)(2,1)S(1)}, u32[]{:S(2)}, u32[]{:S(2)}) %collective-permute-start.70) | collective-permute-done | bytes 1048608 | tf_op jit(solution)/shard_map/ppermute | solution.py:739
  623.6 32.1 %shard_map.343 = (bf16[2048,768]{1,0:T(8,128)(2,1)}, f32[1,768]{1,0:T(1,128)}) custom-call(s32[13]{0:T(128)} %concatenate.69.info, bf16[2048,768]{1,0:T(8,128)(2,1)} %get-tuple-element.115.qkv, bf16[512,256]{1,0:T(8,128)(2,1)} %pad_maximum_fusion.8.refs_0_, bf16[512,256]{1,0:T(8,128)(2,1)} %pad_maximum_fusion.9.refs_1_, ...), custom_call_target="tpu_custom_call" | custom-call | flops 10737418240 | bytes 12582912 | tf_op jit(solution)/shard_map/pallas_call | solution.py:518
  669.8 13.1 %shard_map.344 = (f32[48,2048]{1,0:T(8,128)}, f32[48,768]{1,0:T(8,128)}) custom-call(bf16[256,2048]{1,0:T(8,128)(2,1)} %fusion.40.refs_0_, bf16[256,2048]{1,0:T(8,128)(2,1)} %copy-done.34, bf16[256,2048]{1,0:T(8,128)(2,1)} %collective-permute-done.11.refs_0_.refs_2_, bf16[256,2048]{1,0:T(8,128)(2,1)} %copy-done.35, ...), custom_call_target="tpu_custom_call" | custom-call | flops 5905580032 | bytes 14680064 | tf_op jit(solution)/shard_map/pallas_call | solution.py:652
  686.5 8.0 collective-permute-done.87
  697.9 13.8 %shard_map.348 = (f32[16,704]{1,0:T(8,128)}, f32[16,2048]{1,0:T(8,128)}) custom-call(bf16[512,704]{1,0:T(8,128)(2,1)} %get-tuple-element.114.refs_0_, bf16[512,704]{1,0:T(8,128)(2,1)} %get-tuple-element.112.refs_1_, bf16[512,704]{1,0:T(8,128)(2,1)} %get-tuple-element.110.refs_2_, bf16[512,704]{1,0:T(8,128)(2,1)} %get-tuple-element.108.refs_3_, ...), custom_call_target="tpu_custom_call" | custom-call | flops 5771362304 | bytes 14155776 | tf_op jit(solution)/shard_map/pallas_call | solution.py:652
  711.7 10.9 %shard_map.347 = (f32[16,256]{1,0:T(8,128)}, f32[16,2048]{1,0:T(8,128)}) custom-call(bf16[2048,256]{1,0:T(8,128)(2,1)} %get-tuple-element.80.refs_0_, bf16[256,2048]{1,0:T(8,128)(2,1)} %copy-done.19, bf16[256,2048]{1,0:T(8,128)(2,1)} %copy-done.41, bf16[256,2048]{1,0:T(8,128)(2,1)} %copy-done.21, bf16[256,2048]{1,0:T(8,128)(2,1)} %copy-done.42, ...), custom_call_target="tpu_custom_call" | custom-call | flops 4831838208 | bytes 10485760 | tf_op jit(solution)/shard_map/pallas_call | solution.py:652
  747.7 11.8 %collective-permute-done.90 = f32[8,17,1280]{2,0,1:T(8,128)S(1)} collective-permute-done((f32[8,17,1280]{2,0,1:T(8,128)S(1)}, f32[8,17,1280]{2,0,1:T(8,128)S(1)}, u32[]{:S(2)}, u32[]{:S(2)}) %collective-permute-start.90) | collective-permute-done | bytes 696352 | tf_op jit(solution)/shard_map/ppermute | solution.py:726
  765.8 23.4 %collective-permute-done.79 = bf16[256,2048]{1,0:T(8,128)(2,1)S(1)} collective-permute-done((bf16[256,2048]{1,0:T(8,128)(2,1)S(1)}, bf16[256,2048]{1,0:T(8,128)(2,1)S(1)}, u32[]{:S(2)}, u32[]{:S(2)}) %collective-permute-start.79) | collective-permute-done | bytes 1048608 | tf_op jit(solution)/shard_map/ppermute | solution.py:739
  804.4 6.7 collective-permute-start.85
  817.3 17.5 %collective-permute-done.85 = bf16[256,2048]{1,0:T(8,128)(2,1)} collective-permute-done((bf16[256,2048]{1,0:T(8,128)(2,1)}, bf16[256,2048]{1,0:T(8,128)(2,1)}, u32[]{:S(2)}, u32[]{:S(2)}) %collective-permute-start.85) | collective-permute-done | bytes 1048608 | tf_op jit(solution)/shard_map/ppermute | solution.py:742
  (600 shorter events, 357.4 us)
Async XLA Ops:
  9.4 55.4 %collective-permute-start = (bf16[256,2048]{1,0:T(8,128)(2,1)}, bf16[256,2048]{1,0:T(8,128)(2,1)S(1)}, u32[]{:S(2)}, u32[]{:S(2)}) collective-permute-start(bf16[256,2048]{1,0:T(8,128)(2,1)} %param.25), channel_id=1, source_target_pairs={{4,8},{8,4},{5,9},{9,5},{6,10},{10,6},{7,11},{11,7},{20,24},{24,20... | collective-permute-start | bytes 3145736 | tf_op jit(solution)/shard_map/ppermute | solution.py:742
  15.4 106.7 %collective-permute-start.4 = (bf16[3,1024,256]{2,1,0:T(8,128)(2,1)}, bf16[3,1024,256]{2,1,0:T(8,128)(2,1)}, u32[]{:S(2)}, u32[]{:S(2)}) collective-permute-start(bf16[3,1024,256]{2,1,0:T(8,128)(2,1)} %constant_dynamic-slice_fusion.3), channel_id=1, source_target_pairs={{0,4},{12,8},{1,5},{13,9},{2,6},{14,10},{3,7},{15,11},{16,20},{28,... | collective-permute-start | bytes 4718600 | tf_op jit(solution)/shard_map/ppermute | solution.py:848
  67.5 65.0 %collective-permute-start.11 = (bf16[256,2048]{1,0:T(8,128)(2,1)}, bf16[256,2048]{1,0:T(8,128)(2,1)}, u32[]{:S(2)}, u32[]{:S(2)}) collective-permute-start(bf16[256,2048]{1,0:T(8,128)(2,1)} %fusion.40.refs_0_), channel_id=1, source_target_pairs={{0,1},{1,0},{2,3},{3,2},{4,5},{5,4},{6,7},{7,6},{8,9},{9,8},{10,11... | collective-permute-start | bytes 3145736 | tf_op jit(solution)/shard_map/ppermute | solution.py:739
  68.8 60.4 %collective-permute-start.13 = (bf16[256,2048]{1,0:T(8,128)(2,1)}, bf16[256,2048]{1,0:T(8,128)(2,1)}, u32[]{:S(2)}, u32[]{:S(2)}) collective-permute-start(bf16[256,2048]{1,0:T(8,128)(2,1)} %fusion.40.refs_0_), channel_id=1, source_target_pairs={{0,2},{1,3},{2,0},{3,1},{4,6},{5,7},{6,4},{7,5},{8,10},{9,11},{10,... | collective-permute-start | bytes 3145736 | tf_op jit(solution)/shard_map/ppermute | solution.py:739
  153.6 37.3 %collective-permute-start.17 = (bf16[128,2048]{1,0:T(8,128)(2,1)S(1)}, bf16[128,2048]{1,0:T(8,128)(2,1)}, u32[]{:S(2)}, u32[]{:S(2)}) collective-permute-start(bf16[128,2048]{1,0:T(8,128)(2,1)S(1)} %collective-permute-done.15.refs_0_.refs_6_), channel_id=1, source_target_pairs={{0,8},{8,0},{1,9},{9,1},{2,10},{10,2},{3,11},{11,3},{4,12},{12,4},... | collective-permute-start | bytes 1572872 | tf_op jit(solution)/shard_map/ppermute | solution.py:722
  153.8 37.2 %collective-permute-start.18 = (bf16[128,2048]{1,0:T(8,128)(2,1)S(1)}, bf16[128,2048]{1,0:T(8,128)(2,1)}, u32[]{:S(2)}, u32[]{:S(2)}) collective-permute-start(bf16[128,2048]{1,0:T(8,128)(2,1)S(1)} %collective-permute-done.16.refs_1_.refs_7_), channel_id=1, source_target_pairs={{0,8},{8,0},{1,9},{9,1},{2,10},{10,2},{3,11},{11,3},{4,12},{12,4},... | collective-permute-start | bytes 1572872 | tf_op jit(solution)/shard_map/ppermute | solution.py:722
  167.6 57.7 %collective-permute-start.37 = (bf16[256,2048]{1,0:T(8,128)(2,1)S(1)}, bf16[256,2048]{1,0:T(8,128)(2,1)}, u32[]{:S(2)}, u32[]{:S(2)}) collective-permute-start(bf16[256,2048]{1,0:T(8,128)(2,1)S(1)} %copy-done.33), channel_id=1, source_target_pairs={{4,8},{8,4},{5,9},{9,5},{6,10},{10,6},{7,11},{11,7},{20,24},{24,20... | collective-permute-start | bytes 3145736 | tf_op jit(solution)/shard_map/ppermute | solution.py:742
  230.8 39.8 %collective-permute-start.38 = (bf16[256,2048]{1,0:T(8,128)(2,1)}, bf16[256,2048]{1,0:T(8,128)(2,1)}, u32[]{:S(2)}, u32[]{:S(2)}) collective-permute-start(bf16[256,2048]{1,0:T(8,128)(2,1)} %get-tuple-element.90.refs_4_), channel_id=1, source_target_pairs={{0,2},{1,3},{2,0},{3,1},{4,6},{5,7},{6,4},{7,5},{8,10},{9,11},{10,... | collective-permute-start | bytes 3145736 | tf_op jit(solution)/shard_map/ppermute | solution.py:739
  232.3 45.8 %collective-permute-start.40 = (bf16[704,1024]{1,0:T(8,128)(2,1)S(1)}, bf16[704,1024]{1,0:T(8,128)(2,1)}, u32[]{:S(2)}, u32[]{:S(2)}) collective-permute-start(bf16[704,1024]{1,0:T(8,128)(2,1)S(1)} %constant_dynamic-slice_fusion.1), channel_id=1, source_target_pairs={{0,4},{12,8},{1,5},{13,9},{2,6},{14,10},{3,7},{15,11},{16,20},{28,... | collective-permute-start | bytes 4325384 | tf_op jit(solution)/shard_map/ppermute | solution.py:848
  245.9 39.1 %collective-permute-start.26 = (bf16[256,2048]{1,0:T(8,128)(2,1)}, bf16[256,2048]{1,0:T(8,128)(2,1)S(1)}, u32[]{:S(2)}, u32[]{:S(2)}) collective-permute-start(bf16[256,2048]{1,0:T(8,128)(2,1)} %fusion.25), channel_id=1, source_target_pairs={{0,1},{1,0},{2,3},{3,2},{4,5},{5,4},{6,7},{7,6},{8,9},{9,8},{10,11... | collective-permute-start | bytes 3145736 | tf_op jit(solution)/shard_map/ppermute | solution.py:739
  247.4 76.6 %collective-permute-start.24 = (bf16[256,2048]{1,0:T(8,128)(2,1)}, bf16[256,2048]{1,0:T(8,128)(2,1)}, u32[]{:S(2)}, u32[]{:S(2)}) collective-permute-start(bf16[256,2048]{1,0:T(8,128)(2,1)} %fusion.22), channel_id=1, source_target_pairs={{0,2},{1,3},{2,0},{3,1},{4,6},{5,7},{6,4},{7,5},{8,10},{9,11},{10,... | collective-permute-start | bytes 3145736 | tf_op jit(solution)/shard_map/ppermute | solution.py:739
  254.0 92.4 %collective-permute-start.22 = (bf16[256,2048]{1,0:T(8,128)(2,1)}, bf16[256,2048]{1,0:T(8,128)(2,1)}, u32[]{:S(2)}, u32[]{:S(2)}) collective-permute-start(bf16[256,2048]{1,0:T(8,128)(2,1)} %fusion.19), channel_id=1, source_target_pairs={{0,3},{1,2},{2,1},{3,0},{4,7},{5,6},{6,5},{7,4},{8,11},{9,10},{10,... | collective-permute-start | bytes 3145736 | tf_op jit(solution)/shard_map/ppermute | solution.py:739
  270.6 101.0 %collective-permute-start.46 = (bf16[2,1024,704]{1,2,0:T(8,128)(2,1)}, bf16[2,1024,704]{1,2,0:T(8,128)(2,1)}, u32[]{:S(2)}, u32[]{:S(2)}) collective-permute-start(bf16[2,1024,704]{1,2,0:T(8,128)(2,1)} %constant_dynamic-slice_fusion), channel_id=1, source_target_pairs={{0,4},{12,8},{1,5},{13,9},{2,6},{14,10},{3,7},{15,11},{16,20},{28,... | collective-permute-start | bytes 8650760 | tf_op jit(solution)/shard_map/ppermute | solution.py:848
  278.1 76.0 %collective-permute-start.41 = (bf16[704,1024]{1,0:T(8,128)(2,1)}, bf16[704,1024]{1,0:T(8,128)(2,1)S(1)}, u32[]{:S(2)}, u32[]{:S(2)}) collective-permute-start(bf16[704,1024]{1,0:T(8,128)(2,1)} %collective-permute-done.40.refs_0_), channel_id=1, source_target_pairs={{4,20},{8,24},{20,4},{24,8},{5,21},{9,25},{21,5},{25,9},{6,22},{10... | collective-permute-start | bytes 4325384 | tf_op jit(solution)/shard_map/ppermute | solution.py:855
  285.1 85.3 %collective-permute-start.59 = (bf16[256,2048]{1,0:T(8,128)(2,1)}, bf16[256,2048]{1,0:T(8,128)(2,1)}, u32[]{:S(2)}, u32[]{:S(2)}) collective-permute-start(bf16[256,2048]{1,0:T(8,128)(2,1)} %get-tuple-element.90.refs_4_), channel_id=1, source_target_pairs={{0,8},{8,0},{1,9},{9,1},{2,10},{10,2},{3,11},{11,3},{4,12},{12,4},... | collective-permute-start | bytes 3145736 | tf_op jit(solution)/shard_map/ppermute | solution.py:722
  324.0 47.6 %collective-permute-start.43 = (bf16[128,2048]{1,0:T(8,128)(2,1)S(1)}, bf16[128,2048]{1,0:T(8,128)(2,1)}, u32[]{:S(2)}, u32[]{:S(2)}) collective-permute-start(bf16[128,2048]{1,0:T(8,128)(2,1)S(1)} %slice.378), channel_id=1, source_target_pairs={{0,2},{1,3},{2,0},{3,1},{4,6},{5,7},{6,4},{7,5},{8,10},{9,11},{10,... | collective-permute-start | bytes 1572872 | tf_op jit(solution)/shard_map/ppermute | solution.py:739
  371.7 55.5 %collective-permute-start.47 = (bf16[2,1024,704]{1,2,0:T(8,128)(2,1)}, bf16[2,1024,704]{1,2,0:T(8,128)(2,1)}, u32[]{:S(2)}, u32[]{:S(2)}) collective-permute-start(bf16[2,1024,704]{1,2,0:T(8,128)(2,1)} %collective-permute-done.46), channel_id=1, source_target_pairs={{4,20},{8,24},{20,4},{24,8},{5,21},{9,25},{21,5},{25,9},{6,22},{10... | collective-permute-start | bytes 8650760 | tf_op jit(solution)/shard_map/ppermute | solution.py:855
  385.7 57.9 %collective-permute-start.58 = (bf16[256,2048]{1,0:T(8,128)(2,1)}, bf16[256,2048]{1,0:T(8,128)(2,1)}, u32[]{:S(2)}, u32[]{:S(2)}) collective-permute-start(bf16[256,2048]{1,0:T(8,128)(2,1)} %multiply_convert_fusion.1.refs_0_), channel_id=1, source_target_pairs={{0,8},{8,0},{1,9},{9,1},{2,10},{10,2},{3,11},{11,3},{4,12},{12,4},... | collective-permute-start | bytes 3145736 | tf_op jit(solution)/shard_map/ppermute | solution.py:722
  423.5 44.8 %collective-permute-start.50 = (bf16[256,2048]{1,0:T(8,128)(2,1)}, bf16[256,2048]{1,0:T(8,128)(2,1)}, u32[]{:S(2)}, u32[]{:S(2)}) collective-permute-start(bf16[256,2048]{1,0:T(8,128)(2,1)} %collective-permute-done.31.refs_0_.refs_4_), channel_id=1, source_target_pairs={{0,8},{8,0},{1,9},{9,1},{2,10},{10,2},{3,11},{11,3},{4,12},{12,4},... | collective-permute-start | bytes 3145736 | tf_op jit(solution)/shard_map/ppermute | solution.py:722
  425.6 55.6 %collective-permute-start.35 = (bf16[128,2048]{1,0:T(8,128)(2,1)}, bf16[128,2048]{1,0:T(8,128)(2,1)}, u32[]{:S(2)}, u32[]{:S(2)}) collective-permute-start(bf16[128,2048]{1,0:T(8,128)(2,1)} %collective-permute-done.32.refs_0_.refs_6_), channel_id=1, source_target_pairs={{0,8},{8,0},{1,9},{9,1},{2,10},{10,2},{3,11},{11,3},{4,12},{12,4},... | collective-permute-start | bytes 1572872 | tf_op jit(solution)/shard_map/ppermute | solution.py:722
  427.1 54.0 %collective-permute-start.36 = (bf16[128,2048]{1,0:T(8,128)(2,1)}, bf16[128,2048]{1,0:T(8,128)(2,1)}, u32[]{:S(2)}, u32[]{:S(2)}) collective-permute-start(bf16[128,2048]{1,0:T(8,128)(2,1)} %collective-permute-done.34.refs_1_.refs_7_), channel_id=1, source_target_pairs={{0,8},{8,0},{1,9},{9,1},{2,10},{10,2},{3,11},{11,3},{4,12},{12,4},... | collective-permute-start | bytes 1572872 | tf_op jit(solution)/shard_map/ppermute | solution.py:722
  455.7 93.8 %collective-permute-start.60 = (bf16[256,2048]{1,0:T(8,128)(2,1)}, bf16[256,2048]{1,0:T(8,128)(2,1)S(1)}, u32[]{:S(2)}, u32[]{:S(2)}) collective-permute-start(bf16[256,2048]{1,0:T(8,128)(2,1)} %get-tuple-element.107), channel_id=1, source_target_pairs={{0,8},{8,0},{1,9},{9,1},{2,10},{10,2},{3,11},{11,3},{4,12},{12,4},... | collective-permute-start | bytes 3145736 | tf_op jit(solution)/shard_map/ppermute | solution.py:722
  468.3 44.6 %collective-permute-start.56 = (bf16[256,2048]{1,0:T(8,128)(2,1)}, bf16[256,2048]{1,0:T(8,128)(2,1)S(1)}, u32[]{:S(2)}, u32[]{:S(2)}) collective-permute-start(bf16[256,2048]{1,0:T(8,128)(2,1)} %get-tuple-element.105), channel_id=1, source_target_pairs={{0,8},{8,0},{1,9},{9,1},{2,10},{10,2},{3,11},{11,3},{4,12},{12,4},... | collective-permute-start | bytes 3145736 | tf_op jit(solution)/shard_map/ppermute | solution.py:722
  518.5 46.5 %collective-permute-start.49 = (bf16[256,2048]{1,0:T(8,128)(2,1)}, bf16[256,2048]{1,0:T(8,128)(2,1)}, u32[]{:S(2)}, u32[]{:S(2)}) collective-permute-start(bf16[256,2048]{1,0:T(8,128)(2,1)} %add_convert_fusion.3), channel_id=1, source_target_pairs={{0,3},{1,2},{2,1},{3,0},{4,7},{5,6},{6,5},{7,4},{8,11},{9,10},{10,... | collective-permute-start | bytes 3145736 | tf_op jit(solution)/shard_map/ppermute | solution.py:739
  598.3 63.7 %collective-permute-start.67 = (bf16[256,2048]{1,0:T(8,128)(2,1)}, bf16[256,2048]{1,0:T(8,128)(2,1)}, u32[]{:S(2)}, u32[]{:S(2)}) collective-permute-start(bf16[256,2048]{1,0:T(8,128)(2,1)} %convolution_convert_fusion), channel_id=1, source_target_pairs={{0,8},{8,0},{1,9},{9,1},{2,10},{10,2},{3,11},{11,3},{4,12},{12,4},... | collective-permute-start | bytes 3145736 | tf_op jit(solution)/shard_map/ppermute | solution.py:722
  612.4 49.6 %collective-permute-start.66 = (bf16[256,2048]{1,0:T(8,128)(2,1)}, bf16[256,2048]{1,0:T(8,128)(2,1)S(1)}, u32[]{:S(2)}, u32[]{:S(2)}) collective-permute-start(bf16[256,2048]{1,0:T(8,128)(2,1)} %fusion.10), channel_id=1, source_target_pairs={{0,1},{1,0},{2,3},{3,2},{4,5},{5,4},{6,7},{7,6},{8,9},{9,8},{10,11... | collective-permute-start | bytes 3145736 | tf_op jit(solution)/shard_map/ppermute | solution.py:739
  614.8 47.2 %collective-permute-start.64 = (bf16[256,2048]{1,0:T(8,128)(2,1)}, bf16[256,2048]{1,0:T(8,128)(2,1)}, u32[]{:S(2)}, u32[]{:S(2)}) collective-permute-start(bf16[256,2048]{1,0:T(8,128)(2,1)} %fusion.13), channel_id=1, source_target_pairs={{0,2},{1,3},{2,0},{3,1},{4,6},{5,7},{6,4},{7,5},{8,10},{9,11},{10,... | collective-permute-start | bytes 3145736 | tf_op jit(solution)/shard_map/ppermute | solution.py:739
  620.1 42.5 %collective-permute-start.62 = (bf16[256,2048]{1,0:T(8,128)(2,1)}, bf16[256,2048]{1,0:T(8,128)(2,1)S(1)}, u32[]{:S(2)}, u32[]{:S(2)}) collective-permute-start(bf16[256,2048]{1,0:T(8,128)(2,1)} %fusion.16), channel_id=1, source_target_pairs={{0,3},{1,2},{2,1},{3,0},{4,7},{5,6},{6,5},{7,4},{8,11},{9,10},{10,... | collective-permute-start | bytes 3145736 | tf_op jit(solution)/shard_map/ppermute | solution.py:739
  665.8 78.2 %collective-permute-start.68 = (bf16[256,2048]{1,0:T(8,128)(2,1)S(1)}, bf16[256,2048]{1,0:T(8,128)(2,1)S(1)}, u32[]{:S(2)}, u32[]{:S(2)}) collective-permute-start(bf16[256,2048]{1,0:T(8,128)(2,1)S(1)} %get-tuple-element.153), channel_id=1, source_target_pairs={{4,8},{8,4},{5,9},{9,5},{6,10},{10,6},{7,11},{11,7},{20,24},{24,20... | collective-permute-start | bytes 3145736 | tf_op jit(solution)/shard_map/ppermute | solution.py:742
  668.0 68.8 %collective-permute-start.82 = (bf16[256,2048]{1,0:T(8,128)(2,1)}, bf16[256,2048]{1,0:T(8,128)(2,1)}, u32[]{:S(2)}, u32[]{:S(2)}) collective-permute-start(bf16[256,2048]{1,0:T(8,128)(2,1)} %convolution_convert_fusion.18), channel_id=1, source_target_pairs={{0,8},{8,0},{1,9},{9,1},{2,10},{10,2},{3,11},{11,3},{4,12},{12,4},... | collective-permute-start | bytes 3145736 | tf_op jit(solution)/shard_map/ppermute | solution.py:722
  668.6 70.6 %collective-permute-start.80 = (bf16[256,2048]{1,0:T(8,128)(2,1)}, bf16[256,2048]{1,0:T(8,128)(2,1)}, u32[]{:S(2)}, u32[]{:S(2)}) collective-permute-start(bf16[256,2048]{1,0:T(8,128)(2,1)} %convolution_convert_fusion.20), channel_id=1, source_target_pairs={{0,8},{8,0},{1,9},{9,1},{2,10},{10,2},{3,11},{11,3},{4,12},{12,4},... | collective-permute-start | bytes 3145736 | tf_op jit(solution)/shard_map/ppermute | solution.py:722
  744.1 45.1 %collective-permute-start.79 = (bf16[256,2048]{1,0:T(8,128)(2,1)S(1)}, bf16[256,2048]{1,0:T(8,128)(2,1)S(1)}, u32[]{:S(2)}, u32[]{:S(2)}) collective-permute-start(bf16[256,2048]{1,0:T(8,128)(2,1)S(1)} %fusion.39), channel_id=1, source_target_pairs={{0,3},{1,2},{2,1},{3,0},{4,7},{5,6},{6,5},{7,4},{8,11},{9,10},{10,... | collective-permute-start | bytes 3145736 | tf_op jit(solution)/shard_map/ppermute | solution.py:739
  (169 other events, 2870.3 us)

commit v2 on v1

v2 whole, which is shorter than its diff:
```python
import functools

import jax
import jax.numpy as jnp
import numpy as np
from jax import lax
from jax.experimental import pallas as pl
from jax.experimental.pallas import tpu as pltpu
from jax.sharding import Mesh
from jax.sharding import PartitionSpec as P

HD = 128
R = 16
ALPHA = 32
FACTOR = ALPHA / R
EPSILON = 1e-05
ROPE_BASE = 10000.0
BF16 = jnp.bfloat16
F32 = jnp.float32
NEG = -1e30
AXES = ("x", "c", "zh", "zl", "y")
VM = pl.BlockSpec(memory_space=pltpu.VMEM)
SM = pl.BlockSpec(memory_space=pltpu.SMEM)


def mm(left, right, lc=1, rc=0, precision=None):
    return lax.dot_general(
        left,
        right,
        (((lc,), (rc,)), ((), ())),
        preferred_element_type=F32,
        precision=precision,
    )


def params(mib=58):
    return pltpu.CompilerParams(vmem_limit_bytes=mib * 1024 * 1024)


def cost(flops, nbytes, trans=0):
    scale = 1000
    return pl.CostEstimate(
        flops=int(flops) // scale,
        bytes_accessed=int(nbytes) // scale,
        transcendentals=int(trans) // scale,
    )


class Shift:
    def __init__(self, ref, at):
        self.ref, self.at = ref, at

    def __getitem__(self, i):
        return self.ref[self.at + i]


def pack_kernel(a_w, f_w, a1, b1, mq, mo, a2, b2, mm_, a3, b3, md, out):
    out[...] = jnp.zeros(out.shape, out.dtype)
    at = 0
    for ref, count, w in ((a1, 4, a_w), (a2, 2, a_w), (a3, 1, f_w), (b1, 4, a_w), (b2, 2, f_w), (b3, 1, a_w)):
        for p in range(count):
            out[0, :R, at : at + w] = ref[p].astype(BF16)
            at += w
    at = 0
    for ref, count, w in ((mq, 3, a_w), (mo, 1, a_w), (mm_, 2, f_w), (md, 1, a_w)):
        for p in range(count):
            out[0, R : R + 1, at : at + w] = ref[p : p + 1, :].astype(BF16)
            at += w


def unpack_grads_kernel(a_w, f_w, g, a1, b1, mq, mo, a2, b2, mm_, a3, b3, md):
    at = 0
    for ref, count, w in ((a1, 4, a_w), (a2, 2, a_w), (a3, 1, f_w), (b1, 4, a_w), (b2, 2, f_w), (b3, 1, a_w)):
        for p in range(count):
            ref[p] = g[0, :R, at : at + w]
            at += w
    at = 0
    for ref, count, w in ((mq, 3, a_w), (mo, 1, a_w), (mm_, 2, f_w), (md, 1, a_w)):
        for p in range(count):
            ref[p : p + 1, :] = g[0, R : R + 1, at : at + w]
            at += w


def unpack_kernel(
    a_w, f_w, dp, table, g, at_qkv, at_gu, at_o, at_d, at_o0, at_d0,
    b_qkv, b_blocks, b_gu, b_o, b_d, m_qkv, m_o, m_gu, m_d,
):
    b_blocks[...] = jnp.zeros(b_blocks.shape, b_blocks.dtype)
    n = g.shape[0]
    order, where_ = Shift(table, 0), Shift(table, n)
    b_at = 6 * a_w + f_w
    for d in range(n):
        s = order[d]
        lo, hi = d * a_w, (d + 1) * a_w
        for p in range(3):
            at_qkv[p * R : (p + 1) * R, lo:hi] = g[s, :R, p * a_w : (p + 1) * a_w]
        for p in range(2):
            at_gu[p, :, lo:hi] = g[s, :R, (4 + p) * a_w : (5 + p) * a_w]
        b_o[:, lo:hi] = g[s, :R, b_at + 3 * a_w : b_at + 4 * a_w]
        end = b_at + 4 * a_w + 2 * f_w
        b_d[:, lo:hi] = g[s, :R, end : end + a_w]
        m_o[:, lo:hi] = g[s, R : R + 1, 3 * a_w : 4 * a_w].astype(F32)
        end = 4 * a_w + 2 * f_w
        m_d[:, lo:hi] = g[s, R : R + 1, end : end + a_w].astype(F32)
    for i in range(dp):
        s = order[where_[0] * dp + i]
        lo, hi = i * a_w, (i + 1) * a_w
        flo, fhi = i * f_w, (i + 1) * f_w
        at_o[:, lo:hi] = g[s, :R, 3 * a_w : 4 * a_w]
        at_d[:, flo:fhi] = g[s, :R, 6 * a_w : 6 * a_w + f_w]
        for p in range(3):
            b_qkv[p, :, lo:hi] = g[s, :R, b_at + p * a_w : b_at + (p + 1) * a_w]
            for h, at in pieces_of(lo, hi):
                head, inner = divmod(h, HD)
                to = (head * 3 + p) * HD + inner
                w = at[1] - at[0]
                src = p * a_w + at[0]
                b_blocks[p * R : (p + 1) * R, to : to + w] = g[s, :R, b_at + src : b_at + src + w]
                m_qkv[:, to : to + w] = g[s, R : R + 1, src : src + w].astype(F32)
        for p in range(2):
            e = b_at + 4 * a_w + p * f_w
            b_gu[p, :, flo:fhi] = g[s, :R, e : e + f_w]
            e = 4 * a_w + p * f_w
            m_gu[p, :, flo:fhi] = g[s, R : R + 1, e : e + f_w].astype(F32)
        s = order[where_[1] * dp + i]
        at_o0[:, lo:hi] = g[s, :R, 3 * a_w : 4 * a_w]
        at_d0[:, flo:fhi] = g[s, :R, 6 * a_w : 6 * a_w + f_w]


def pieces_of(lo, hi):
    found = []
    at = lo
    while at < hi:
        end = min(hi, (at // HD + 1) * HD)
        found.append((at, (at - lo, end - lo)))
        at = end
    return found


def pack_grads_kernel(
    a_w, f_w, dp, table, ga_qkv, ga_gu, gb_o, gb_d, m_full, ga_attn, ga_d, gb_all, gb_gu,
    m_qkv, m_gu, out
):
    n = out.shape[0]
    order, where_ = Shift(table, 0), Shift(table, n)
    heads = m_qkv.shape[1] // (3 * HD)
    out[...] = jnp.zeros(out.shape, out.dtype)
    b_at = 6 * a_w + f_w
    dt = out.dtype
    for d in range(n):
        s = order[d]
        lo, hi = d * a_w, (d + 1) * a_w
        for p in range(3):
            out[s, :R, p * a_w : (p + 1) * a_w] = ga_qkv[p * R : (p + 1) * R, lo:hi].astype(dt)
        for p in range(2):
            e = (4 + p) * a_w
            out[s, :R, e : e + a_w] = ga_gu[p * R : (p + 1) * R, lo:hi].astype(dt)
        out[s, :R, b_at + 3 * a_w : b_at + 4 * a_w] = gb_o[:, lo:hi].astype(dt)
        end = b_at + 4 * a_w + 2 * f_w
        out[s, :R, end : end + a_w] = gb_d[:, lo:hi].astype(dt)
        out[s, R : R + 1, 3 * a_w : 4 * a_w] = m_full[0:1, lo:hi].astype(dt)
        end = 4 * a_w + 2 * f_w
        out[s, R : R + 1, end : end + a_w] = m_full[1:2, lo:hi].astype(dt)
    for i in range(dp):
        s = order[where_[0] * dp + i]
        lo, hi = i * a_w, (i + 1) * a_w
        flo, fhi = i * f_w, (i + 1) * f_w
        out[s, :R, 3 * a_w : 4 * a_w] = ga_attn[:, lo:hi].astype(dt)
        out[s, :R, 6 * a_w : 6 * a_w + f_w] = ga_d[:, flo:fhi].astype(dt)
        for p in range(3):
            for h, at in pieces_of(lo, hi):
                head, inner = divmod(h, HD)
                src = (head * 3 + p) * HD + inner
                w = at[1] - at[0]
                to = p * a_w + at[0]
                out[s, :R, b_at + to : b_at + to + w] = gb_all[p * R : (p + 1) * R, src : src + w].astype(dt)
                out[s, R : R + 1, to : to + w] = m_qkv[:, src : src + w].astype(dt)
        for p in range(2):
            e = b_at + 4 * a_w + p * f_w
            out[s, :R, e : e + f_w] = gb_gu[p * R : (p + 1) * R, flo:fhi].astype(dt)
            e = 4 * a_w + p * f_w
            out[s, R : R + 1, e : e + f_w] = m_gu[p, :, flo:fhi].astype(dt)


def pick(flags, t, own, parts):
    n = len(parts)
    k = lax.rem(t - flags[1] + n, n)
    w = parts[0]
    for i in range(1, n):
        w = jnp.where(k == i, parts[i], w)
    return jnp.where(flags[0] == 1, own, w)


def own_block(t, f):
    return t * f[0]


def merge_qkv_kernel(n, flags, own, *refs):
    parts = refs[:n]
    at, b, vb, ssq = refs[n:]
    t = pl.program_id(0)

    @pl.when(t == 0)
    def _():
        ssq[...] = jnp.zeros_like(ssq)

    members, _, width = own.shape
    for p in range(members):
        w = pick(flags, t, own[p], [r[p] for r in parts])
        v = w.astype(F32) + FACTOR * mm(at[p * R : (p + 1) * R, :], b[p], 0, 0)
        total = jnp.sum(v * v, axis=0, keepdims=True)
        vb16 = v.astype(BF16)
        for h in range(width // HD):
            to = slice((h * members + p) * HD, (h * members + p + 1) * HD)
            vb[:, to] = vb16[:, h * HD : (h + 1) * HD]
            ssq[:, to] += total[:, h * HD : (h + 1) * HD]


def merge_qkv(flags, own, parts, at_qkv, b_qkv):
    members, rows, width = own.shape
    n = len(parts)
    part_rows = rows // n
    block = (members, part_rows, width)
    return pl.pallas_call(
        functools.partial(merge_qkv_kernel, n),
        grid_spec=pltpu.PrefetchScalarGridSpec(
            num_scalar_prefetch=1,
            grid=(n,),
            in_specs=[pl.BlockSpec(block, lambda t, f: (0, own_block(t, f), 0))]
            + [pl.BlockSpec(block, lambda t, f: (0, 0, 0))] * n
            + [
                pl.BlockSpec((members * R, part_rows), lambda t, f: (0, t)),
                pl.BlockSpec((members, R, width), lambda t, f: (0, 0, 0)),
            ],
            out_specs=[
                pl.BlockSpec((part_rows, members * width), lambda t, f: (t, 0)),
                pl.BlockSpec((1, members * width), lambda t, f: (0, 0)),
            ],
        ),
        out_shape=[
            jax.ShapeDtypeStruct((rows, members * width), BF16),
            jax.ShapeDtypeStruct((1, members * width), F32),
        ],
        compiler_params=params(),
        cost_estimate=cost(2 * rows * width * members * 256, 4 * members * rows * width * 2),
    )(flags, own, *parts, at_qkv, b_qkv)


def merge_gu_kernel(n, flags, own, *refs):
    gates, ups = refs[:n], refs[n : 2 * n]
    at, b, vb, ssq, acc = refs[2 * n :]
    t = pl.program_id(1)
    first = pl.program_id(0) == 0
    w = pick(flags, t, own[0], [jnp.where(first, g[0], u[0]) for g, u in zip(gates, ups)])
    v = w.astype(F32) + FACTOR * mm(b[0], at[0], 0, 0)
    vb[0] = v.astype(BF16)
    sq = v * v
    lanes = sq[:, :HD]
    for i in range(1, sq.shape[1] // HD):
        lanes = lanes + sq[:, i * HD : (i + 1) * HD]

    @pl.when(t == 0)
    def _():
        acc[...] = lanes

    @pl.when(t > 0)
    def _():
        acc[...] += lanes

    @pl.when(t == pl.num_programs(1) - 1)
    def _():
        ssq[0] = mm(jnp.ones((8, HD), F32), acc[...], 1, 1, lax.Precision.HIGHEST)[:1]


def merge_gu(flags, own, gates, ups, at_gu, b_gu):
    members, width, rows = own.shape
    n = len(gates)
    part_rows = rows // n
    block = (1, width, part_rows)
    return pl.pallas_call(
        functools.partial(merge_gu_kernel, n),
        grid_spec=pltpu.PrefetchScalarGridSpec(
            num_scalar_prefetch=1,
            grid=(members, n),
            in_specs=[pl.BlockSpec(block, lambda p, t, f: (p * f[0], 0, own_block(t, f)))]
            + [pl.BlockSpec(block, lambda p, t, f: (0, 0, 0))] * (2 * n)
            + [
                pl.BlockSpec((1, R, part_rows), lambda p, t, f: (p, 0, t)),
                pl.BlockSpec((1, R, width), lambda p, t, f: (p, 0, 0)),
            ],
            out_specs=[
                pl.BlockSpec(block, lambda p, t, f: (p, 0, t)),
                pl.BlockSpec((1, 1, width), lambda p, t, f: (p, 0, 0)),
            ],
            scratch_shapes=[pltpu.VMEM((width, HD), F32)],
        ),
        out_shape=[
            jax.ShapeDtypeStruct((members, width, rows), BF16),
            jax.ShapeDtypeStruct((members, 1, width), F32),
        ],
        compiler_params=params(),
        cost_estimate=cost(2 * rows * width * members * 256, 4 * members * rows * width * 2),
    )(flags, own, *gates, *ups, at_gu, b_gu)


def merge_rows_kernel(n, flags, own, *refs):
    parts = refs[:n]
    at, b, vb = refs[n:]
    w = pick(flags, pl.program_id(0), own[...], [r[...] for r in parts])
    v = w.astype(F32) + FACTOR * mm(at[...], b[...], 0, 0)
    vb[...] = v.astype(BF16)


def merge_rows(flags, own, parts, at, b):
    rows, width = own.shape
    xs = len(parts)
    part = width // xs
    return pl.pallas_call(
        functools.partial(merge_rows_kernel, xs),
        grid_spec=pltpu.PrefetchScalarGridSpec(
            num_scalar_prefetch=1,
            grid=(xs,),
            in_specs=[pl.BlockSpec((rows, part), lambda t, f: (0, own_block(t, f)))]
            + [pl.BlockSpec((rows, part), lambda t, f: (0, 0))] * xs
            + [
                pl.BlockSpec((R, rows), lambda t, f: (0, 0)),
                pl.BlockSpec((R, part), lambda t, f: (0, t)),
            ],
            out_specs=pl.BlockSpec((rows, part), lambda t, f: (0, t)),
        ),
        out_shape=jax.ShapeDtypeStruct((rows, width), BF16),
        compiler_params=params(),
        cost_estimate=cost(2 * rows * width * 256, 4 * rows * width * 2),
    )(flags, own, *parts, at, b)


def merge_down_kernel(n, flags, own, *refs):
    parts = refs[:n]
    at, b, scale, vb, vs = refs[n:]
    w = pick(flags, pl.program_id(0), own[...], [r[...] for r in parts])
    v = (w.astype(F32) + FACTOR * mm(at[...], b[...], 0, 0)).astype(BF16)
    vb[...] = v
    vs[...] = (v.astype(F32) * scale[...]).astype(BF16)


def merge_down(flags, own, parts, at, b, scale):
    rows, width = own.shape
    n = len(parts)
    part = width // n
    return pl.pallas_call(
        functools.partial(merge_down_kernel, n),
        grid_spec=pltpu.PrefetchScalarGridSpec(
            num_scalar_prefetch=1,
            grid=(n,),
            in_specs=[pl.BlockSpec((rows, part), lambda t, f: (0, own_block(t, f)))]
            + [pl.BlockSpec((rows, part), lambda t, f: (0, 0))] * n
            + [
                pl.BlockSpec((R, rows), lambda t, f: (0, 0)),
                pl.BlockSpec((R, part), lambda t, f: (0, t)),
                pl.BlockSpec((1, part), lambda t, f: (0, t)),
            ],
            out_specs=[pl.BlockSpec((rows, part), lambda t, f: (0, t))] * 2,
        ),
        out_shape=[jax.ShapeDtypeStruct((rows, width), BF16)] * 2,
        compiler_params=params(),
        cost_estimate=cost(2 * rows * width * 256, 5 * rows * width * 2),
    )(flags, own, *parts, at, b, scale)


def qkv_kernel(rows, blk, *refs):
    count = len(rows)
    xs = refs[:count]
    w, scale, cos0, cos1, sin0, sin1, out = refs[count:]
    cos = jnp.concatenate([cos0[...], cos1[...]], axis=0)
    sin = jnp.concatenate([sin0[...], sin1[...]], axis=0)
    at = 0
    for x, r in zip(xs, rows):
        z = mm(x[...], w[...]) * scale[...]
        co, si = cos[at : at + r], sin[at : at + r]
        q = z[:, :HD]
        k = z[:, HD : 2 * HD]
        q = (q * co + pltpu.roll(q, HD // 2, 1) * si) * HD ** (-0.5)
        k = k * co + pltpu.roll(k, HD // 2, 1) * si
        out[at : at + r, :HD] = q.astype(BF16)
        out[at : at + r, HD : 2 * HD] = k.astype(BF16)
        out[at : at + r, 2 * HD :] = z[:, 2 * HD :].astype(BF16)
        at += r


def qkv_chunk(blk, chunk, pieces, w, scale, cos, sin):
    rows = [p.shape[0] for p in pieces]
    total = sum(rows)
    tokens = total // 2
    depth, width = w.shape
    heads = width // (3 * HD)

    def table(k):
        return pl.BlockSpec((tokens, HD), lambda h, b: (b[2 * chunk + k], 0))

    return pl.pallas_call(
        functools.partial(qkv_kernel, rows),
        grid_spec=pltpu.PrefetchScalarGridSpec(
            num_scalar_prefetch=1,
            grid=(heads,),
            in_specs=[pl.BlockSpec((r, depth), lambda h, b: (0, 0)) for r in rows]
            + [
                pl.BlockSpec((depth, 3 * HD), lambda h, b: (0, h)),
                pl.BlockSpec((1, 3 * HD), lambda h, b: (0, h)),
                table(0),
                table(1),
                table(0),
                table(1),
            ],
            out_specs=pl.BlockSpec((total, 3 * HD), lambda h, b: (0, h)),
        ),
        out_shape=jax.ShapeDtypeStruct((total, width), BF16),
        compiler_params=params(),
        cost_estimate=cost(2 * total * depth * width, 2 * (depth * width + total * depth)),
    )(blk, *pieces, w, scale, cos, cos, sin, sin)


def masked(scores, low, first_key, first_query, valid_count):
    keys = first_key + lax.broadcasted_iota(jnp.int32, scores.shape, 0)
    queries = first_query + lax.broadcasted_iota(jnp.int32, (1, scores.shape[1]), 1)
    high = jnp.minimum(queries, valid_count - 1)
    allowed = ((keys >= low) & (keys <= high)) | (keys == queries)
    return jnp.where(allowed, scores, NEG)


def attn_fwd_kernel(n_chunks, tokens, bq, info, *refs):
    chunks = refs[:n_chunks]
    low, qkv_abs, att_abs, att_slot, lse, m_sc, l_sc, acc = refs[n_chunks:]
    i = pl.program_id(1)
    last = pl.num_programs(1) - 1
    slots = 2 * n_chunks
    valid_count = info[slots]

    @pl.when(i == 0)
    def _():
        for s in range(slots):
            start = pl.multiple_of(info[s] * tokens, tokens)
            qkv_abs[pl.ds(start, tokens), :] = chunks[s // 2][
                (s % 2) * tokens : (s % 2 + 1) * tokens, :
            ]

    q0 = pl.multiple_of(i * bq, bq)
    q = qkv_abs[pl.ds(q0, bq), :HD]
    lo = low[:, pl.ds(q0, bq)]
    m_sc[...] = jnp.full(m_sc.shape, NEG, F32)
    l_sc[...] = jnp.zeros_like(l_sc)
    acc[...] = jnp.zeros_like(acc)

    def step(j, carry):
        k0 = pl.multiple_of(j * bq, bq)
        k = qkv_abs[pl.ds(k0, bq), HD : 2 * HD]
        v = qkv_abs[pl.ds(k0, bq), 2 * HD :]
        s = masked(mm(k, q, 1, 1), lo, k0, q0, valid_count)
        m_old = m_sc[...]
        m_new = jnp.maximum(m_old, jnp.max(s, axis=0, keepdims=True))
        p = jnp.exp(s - m_new)
        alpha = jnp.exp(m_old - m_new)
        m_sc[...] = m_new
        l_sc[...] = l_sc[...] * alpha + jnp.sum(p, axis=0, keepdims=True)
        acc[...] = acc[...] * alpha + mm(v, p.astype(BF16), 0, 0)
        return carry

    lax.fori_loop(info[slots + 1 + i], i + 1, step, 0)
    total = l_sc[...]
    lse[0, :, pl.ds(q0, bq)] = m_sc[...] + jnp.log(total)
    att_abs[pl.ds(q0, bq), :] = (acc[...] / total).T.astype(BF16)

    @pl.when(i == last)
    def _():
        for s in range(slots):
            start = pl.multiple_of(info[s] * tokens, tokens)
            att_slot[s * tokens : (s + 1) * tokens, :] = att_abs[pl.ds(start, tokens), :]


def attn_fwd(info, chunks, low, tokens, bq):
    rows, width = chunks[0].shape
    heads = width // (3 * HD)
    seq = rows * len(chunks)
    n_blocks = seq // bq
    whole = pl.BlockSpec((seq, HD), lambda h, i, f: (0, h))
    return pl.pallas_call(
        functools.partial(attn_fwd_kernel, len(chunks), tokens, bq),
        grid_spec=pltpu.PrefetchScalarGridSpec(
            num_scalar_prefetch=1,
            grid=(heads, n_blocks),
            in_specs=[pl.BlockSpec((rows, 3 * HD), lambda h, i, f: (0, h))] * len(chunks)
            + [pl.BlockSpec((1, seq), lambda h, i, f: (0, 0))],
            out_specs=[
                pl.BlockSpec((seq, 3 * HD), lambda h, i, f: (0, h)),
                whole,
                whole,
                pl.BlockSpec((1, 1, seq), lambda h, i, f: (h, 0, 0)),
            ],
            scratch_shapes=[
                pltpu.VMEM((1, bq), F32),
                pltpu.VMEM((1, bq), F32),
                pltpu.VMEM((HD, bq), F32),
            ],
        ),
        out_shape=[
            jax.ShapeDtypeStruct((seq, width), BF16),
            jax.ShapeDtypeStruct((seq, heads * HD), BF16),
            jax.ShapeDtypeStruct((seq, heads * HD), BF16),
            jax.ShapeDtypeStruct((heads, 1, seq), F32),
        ],
        compiler_params=params(),
        cost_estimate=cost(
            4 * heads * seq * seq * HD, 2 * seq * width * 3, heads * seq * seq // 2
        ),
    )(info, *chunks, low)


def attn_bwd_kernel(
    n_chunks, tokens, bq, info, qkv, *refs
):
    dos = refs[:n_chunks]
    att, lse, low, cos, sin, scale, dz, dc, do_abs, delta, dq, dk, dv = refs[n_chunks:]
    slots = 2 * n_chunks
    valid_count = info[slots]
    seq = qkv.shape[0]
    n_blocks = seq // bq
    for s in range(slots):
        start = pl.multiple_of(info[s] * tokens, tokens)
        do_abs[pl.ds(start, tokens), :] = dos[s // 2][(s % 2) * tokens : (s % 2 + 1) * tokens, :]
    ones = jnp.ones((8, HD), F32)
    for i in range(n_blocks):
        r = slice(i * bq, (i + 1) * bq)
        prod = do_abs[r, :].astype(F32) * att[r, :].astype(F32)
        delta[:, r] = mm(ones, prod, 1, 1, lax.Precision.HIGHEST)[:1]
    dq[...] = jnp.zeros_like(dq)

    def outer(j, carry):
        k0 = pl.multiple_of(j * bq, bq)
        k = qkv[pl.ds(k0, bq), HD : 2 * HD]
        v = qkv[pl.ds(k0, bq), 2 * HD :]
        krow = pl.ds(k0, bq)
        dk[krow, :] = jnp.zeros((bq, HD), F32)
        dv[krow, :] = jnp.zeros((bq, HD), F32)

        def inner(i, c):
            @pl.when(info[slots + 1 + i] <= j)
            def _():
                q0 = pl.multiple_of(i * bq, bq)
                qrow = pl.ds(q0, bq)
                q = qkv[qrow, :HD]
                do = do_abs[qrow, :]
                s = masked(mm(k, q, 1, 1), low[:, qrow], k0, q0, valid_count)
                p = jnp.exp(s - lse[0, :, qrow])
                dp = mm(v, do, 1, 1)
                ds = (p * (dp - delta[:, qrow])).astype(BF16)
                dv[krow, :] += mm(p.astype(BF16), do)
                dk[krow, :] += mm(ds, q)
                dq[qrow, :] += mm(ds, k, 0, 0)

            return c

        return lax.fori_loop(j, n_blocks, inner, carry)

    lax.fori_loop(0, n_blocks, outer, 0)
    dcq = jnp.zeros((1, HD), F32)
    dck = jnp.zeros((1, HD), F32)
    dcv = jnp.zeros((1, HD), F32)
    half = HD // 2
    for s in range(slots):
        rows = pl.ds(pl.multiple_of(info[s] * tokens, tokens), tokens)
        co, si = cos[rows, :], sin[rows, :]
        out = slice(s * tokens, (s + 1) * tokens)

        def back(u):
            return u * co - pltpu.roll(u, half, 1) * si

        gq = back(dq[rows, :]) * HD ** (-0.5)
        gk = back(dk[rows, :])
        gv = dv[rows, :]
        q = back(qkv[rows, :HD].astype(F32)) * HD**0.5
        k = back(qkv[rows, HD : 2 * HD].astype(F32))
        v = qkv[rows, 2 * HD :].astype(F32)
        dcq += jnp.sum(gq * q, axis=0, keepdims=True)
        dck += jnp.sum(gk * k, axis=0, keepdims=True)
        dcv += jnp.sum(gv * v, axis=0, keepdims=True)
        dz[out, :HD] = (gq * scale[:, :HD]).astype(BF16)
        dz[out, HD : 2 * HD] = (gk * scale[:, HD : 2 * HD]).astype(BF16)
        dz[out, 2 * HD :] = (gv * scale[:, 2 * HD :]).astype(BF16)
    dc[:, :HD] = dcq / scale[:, :HD]
    dc[:, HD : 2 * HD] = dck / scale[:, HD : 2 * HD]
    dc[:, 2 * HD :] = dcv / scale[:, 2 * HD :]


def attn_bwd(info, qkv_abs, do_chunks, att_abs, lse, low, cos, sin, scale, tokens, bq):
    seq, width = qkv_abs.shape
    heads = width // (3 * HD)
    rows = do_chunks[0].shape[0]
    once = lambda h, f: (0, 0)
    head = lambda h, f: (0, h)
    return pl.pallas_call(
        functools.partial(attn_bwd_kernel, len(do_chunks), tokens, bq),
        grid_spec=pltpu.PrefetchScalarGridSpec(
            num_scalar_prefetch=1,
            grid=(heads,),
            in_specs=[pl.BlockSpec((seq, 3 * HD), head)]
            + [pl.BlockSpec((rows, HD), head)] * len(do_chunks)
            + [
                pl.BlockSpec((seq, HD), head),
                pl.BlockSpec((1, 1, seq), lambda h, f: (h, 0, 0)),
                pl.BlockSpec((1, seq), once),
                pl.BlockSpec((seq, HD), once),
                pl.BlockSpec((seq, HD), once),
                pl.BlockSpec((1, 3 * HD), head),
            ],
            out_specs=[
                pl.BlockSpec((seq, 3 * HD), head),
                pl.BlockSpec((1, 3 * HD), head),
            ],
            scratch_shapes=[
                pltpu.VMEM((seq, HD), BF16),
                pltpu.VMEM((1, seq), F32),
                pltpu.VMEM((seq, HD), F32),
                pltpu.VMEM((seq, HD), F32),
                pltpu.VMEM((seq, HD), F32),
            ],
        ),
        out_shape=[
            jax.ShapeDtypeStruct((seq, width), BF16),
            jax.ShapeDtypeStruct((1, width), F32),
        ],
        compiler_params=params(),
        cost_estimate=cost(
            10 * heads * seq * seq * HD, 2 * seq * width * 4, heads * seq * seq // 2
        ),
    )(info, qkv_abs, *do_chunks, att_abs, lse, low, cos, sin, scale)


def mlp_kernel(rows, *refs):
    count = len(rows)
    xs = refs[:count]
    dhid, w, scale, hid, dz, dx_own, dx_mate, dc = refs[count:]
    tokens = dx_own.shape[0]
    sum_gate = jnp.zeros(scale.shape[1:], F32)
    sum_up = jnp.zeros(scale.shape[1:], F32)
    at = 0
    for x, r in zip(xs, rows):
        part = slice(at, at + r)
        xv = x[...]
        zg = mm(xv, w[0], 1, 1)
        zu = mm(xv, w[1], 1, 1)
        gate = zg * scale[0]
        up = zu * scale[1]
        s = 1.0 / (1.0 + jnp.exp(-gate))
        act = gate * s
        hid[part, :] = (act * up).astype(BF16)
        d = dhid[part, :].astype(F32)
        dgate = d * up * s * (1.0 + gate * (1.0 - s))
        dup = d * act
        sum_gate += jnp.sum(dgate * zg, axis=0, keepdims=True)
        sum_up += jnp.sum(dup * zu, axis=0, keepdims=True)
        dzg = (dgate * scale[0]).astype(BF16)
        dzu = (dup * scale[1]).astype(BF16)
        dz[0, part, :] = dzg
        dz[1, part, :] = dzu
        dx = (mm(dzg, w[0]) + mm(dzu, w[1])).astype(BF16)
        if at < tokens:
            dx_own[part, :] = dx
        else:
            dx_mate[at - tokens : at - tokens + r, :] = dx
        at += r
    dc[0] = sum_gate
    dc[1] = sum_up


def mlp_chunk(pieces, dhid, w, scale):
    rows = [p.shape[0] for p in pieces]
    total = sum(rows)
    _, width, depth = w.shape
    half = jax.ShapeDtypeStruct((total // 2, depth), BF16)
    return pl.pallas_call(
        functools.partial(mlp_kernel, rows),
        in_specs=[VM] * (len(pieces) + 3),
        out_specs=[VM] * 5,
        out_shape=[
            jax.ShapeDtypeStruct((total, width), BF16),
            jax.ShapeDtypeStruct((2, total, width), BF16),
            half,
            half,
            jax.ShapeDtypeStruct((2, 1, width), F32),
        ],
        compiler_params=params(),
        cost_estimate=cost(
            8 * total * depth * width, 4 * depth * width + 4 * total * depth, total * width
        ),
    )(*pieces, dhid, w, scale)


def rank_kernel(nx, nd, groups, turned, spans, *refs):
    xs = refs[:nx]
    ds = refs[nx : nx + nd]
    at, b, v, s, c, ga, gb = refs[nx + nd :]
    rank = at.shape[0]
    bs = [(b[g].astype(F32) * c[...]).astype(BF16) for g in range(groups)]
    share = rank // groups
    n_out = b.shape[2]
    ga_sum = None
    gb_sum = [None] * groups
    for xi, xa, di, da, r in spans:
        x = xs[xi][xa : xa + r, :]
        d = [ds[di][g, da : da + r, :] if groups > 1 else ds[di][da : da + r, :] for g in range(groups)]
        u = jnp.concatenate([mm(d[g], bs[g], 1, 1) for g in range(groups)], axis=1).astype(BF16)
        t = mm(x, at[...], 1, 1).astype(BF16)
        a_part = mm(u, x, 0, 0)
        ga_sum = a_part if ga_sum is None else ga_sum + a_part
        for g in range(groups):
            b_part = mm(t, d[g], 0, 0)
            gb_sum[g] = b_part if gb_sum[g] is None else gb_sum[g] + b_part
    for g in range(groups):
        rows = slice(g * share, (g + 1) * share)
        sv = s[g]
        sb = (b[g].astype(F32) * sv).astype(BF16)
        vg = v[g] if groups > 1 else v[...]
        back = mm(sb, vg, 1, 0 if turned else 1)
        ahead = mm(at[rows, :], vg, 1, 1 if turned else 0)
        ga[rows, :] = FACTOR * (ga_sum[rows, :] - back)
        gb[rows, :] = FACTOR * (gb_sum[g][rows, :] * c[...] - ahead * sv)


def rank_grads(xs, ds, at, b, v, s, turned=False, rows=None, scale=None):
    groups = b.shape[0]
    axis = 1 if groups > 1 else 0
    spans = []
    d_rows = used_rows(ds, rows) if rows else [d.shape[axis] for d in ds]
    xi = xa = di = da = 0
    while xi < len(xs):
        r = min(xs[xi].shape[0] - xa, d_rows[di] - da)
        spans.append((xi, xa, di, da, r))
        xa += r
        da += r
        if xa == xs[xi].shape[0]:
            xi, xa = xi + 1, 0
        if da == d_rows[di]:
            di, da = di + 1, 0
    total = sum(x.shape[0] for x in xs)
    rank, n_in = at.shape
    n_out = b.shape[2]
    return pl.pallas_call(
        functools.partial(rank_kernel, len(xs), len(ds), groups, turned, tuple(spans)),
        in_specs=[VM] * (len(xs) + len(ds) + 5),
        out_specs=[VM] * 2,
        out_shape=[
            jax.ShapeDtypeStruct((rank, n_in), F32),
            jax.ShapeDtypeStruct((rank, n_out), F32),
        ],
        compiler_params=params(),
        cost_estimate=cost(
            4 * total * (n_in + n_out * groups) * 256,
            2 * (total * (n_in + n_out * groups) + n_in * n_out * groups),
        ),
    )(*xs, *ds, at, b, v, s, jnp.ones((1, n_out), F32) if scale is None else scale)


def product_kernel(count, turned, spans, *refs):
    xs = refs[:count]
    w = refs[count]
    outs = refs[count + 1 :]
    for xi, oi, at, r in spans:
        outs[oi][at : at + r, :] = mm(xs[xi][...], w[...], 1, 1 if turned else 0).astype(BF16)


def used_rows(xs, tokens):
    rows = []
    left = tokens
    for x in xs:
        r = min(left, x.shape[0])
        rows.append(r)
        left -= r
        if left == 0:
            left = tokens
    return rows


def product(xs, w, turned, n_outs, steps, block=None, tokens=None):
    n = w.shape[0] if turned else w.shape[1]
    depth = w.shape[1] if turned else w.shape[0]
    tn = n // steps
    if block is not None:
        start, rows_in = block
        rows = [rows_in // n_outs] * n_outs
        x_specs = [
            pl.BlockSpec((r, depth), functools.partial(lambda k, i: (k, 0), start * n_outs + j))
            for j, r in enumerate(rows)
        ]
        xs = [xs] * n_outs
    else:
        rows = used_rows(xs, tokens) if tokens else [x.shape[0] for x in xs]
        x_specs = [pl.BlockSpec((r, depth), lambda i: (0, 0)) for r in rows]
    total = sum(rows)
    share = total // n_outs
    spans = []
    at = 0
    for xi, r in enumerate(rows):
        spans.append((xi, at // share, at % share, r))
        at += r
    w_spec = (
        pl.BlockSpec((tn, depth), lambda i: (i, 0))
        if turned
        else pl.BlockSpec((depth, tn), lambda i: (0, i))
    )
    return pl.pallas_call(
        functools.partial(product_kernel, len(xs), turned, tuple(spans)),
        grid=(steps,),
        in_specs=x_specs + [w_spec],
        out_specs=[pl.BlockSpec((share, tn), lambda i: (0, i))] * n_outs,
        out_shape=[jax.ShapeDtypeStruct((share, n), BF16)] * n_outs,
        compiler_params=params(),
        cost_estimate=cost(2 * total * n * depth, 2 * (n * depth + total * (n + depth))),
    )(*xs, w)


def down_kernel(rows, h, w, *refs):
    ds = refs[: len(rows)]
    own, other, dc = refs[len(rows) :]
    tokens = own.shape[0]
    total = jnp.zeros(dc.shape, F32)
    at = 0
    for d, r in zip(ds, rows):
        z = mm(h[at : at + r, :], w[...])
        total += jnp.sum(z * d[...].astype(F32), axis=0, keepdims=True)
        if at < tokens:
            own[at : at + r, :] = z.astype(BF16)
        else:
            other[at - tokens : at - tokens + r, :] = z.astype(BF16)
        at += r
    dc[...] = total


def down_product(h, w, ds):
    rows = [d.shape[0] for d in ds]
    total, depth = h.shape
    n = w.shape[1]
    tn = n // 2
    half = jax.ShapeDtypeStruct((total // 2, n), BF16)
    return pl.pallas_call(
        functools.partial(down_kernel, rows),
        grid=(2,),
        in_specs=[
            pl.BlockSpec((total, depth), lambda i: (0, 0)),
            pl.BlockSpec((depth, tn), lambda i: (0, i)),
        ]
        + [pl.BlockSpec((r, tn), lambda i: (0, i)) for r in rows],
        out_specs=[pl.BlockSpec((total // 2, tn), lambda i: (0, i))] * 2
        + [pl.BlockSpec((1, tn), lambda i: (0, i))],
        out_shape=[half, half, jax.ShapeDtypeStruct((1, n), F32)],
        compiler_params=params(),
        cost_estimate=cost(2 * total * n * depth, 2 * (n * depth + total * (2 * n + depth))),
    )(h, w, *ds)


def norm_forward(values):
    inverse = lax.rsqrt(jnp.mean(values * values, axis=-1, keepdims=True) + EPSILON)
    return values * inverse, inverse


def norm_backward(grad_normed, unit_vals, inverse, gain):
    scaled = grad_normed * gain
    return inverse * (scaled - unit_vals * jnp.mean(scaled * unit_vals, axis=-1, keepdims=True))


def after(value, *others):
    return lax.optimization_barrier((value,) + others)[0]


def on_device(
    sizes,
    layer_input,
    cotangent,
    segment_ids,
    token_valid,
    norm_attn,
    norm_mlp,
    base_qkv,
    base_attn_out,
    base_gate_up,
    base_down,
    rank_in_attn,
    rank_out_attn,
    magnitude_qkv,
    magnitude_out,
    rank_in_mlp,
    rank_out_mlp,
    magnitude_mlp,
    rank_in_down,
    rank_out_down,
    magnitude_down,
):
    X, C, ZH, ZL, Y = (sizes[a] for a in AXES)
    ix, ic, izh, izl, iy = (lax.axis_index(a) for a in AXES)
    dp, mp = X * C, ZH * ZL * Y
    n_dev = dp * mp
    tokens, model = layer_input.shape
    seq_len = segment_ids.shape[0]
    width = base_qkv.shape[2]
    hidden = base_gate_up.shape[2]
    heads = width // HD
    a_w = rank_in_attn.shape[1]
    f_w = rank_in_down.shape[0]
    used = 11 * a_w + 3 * f_w
    packed_w = -(-used // 128) * 128
    bq = min(512, seq_len)
    stay = ic == izh

    def from_offset(a, axis, k):
        n = sizes[axis]
        return lax.ppermute(a, axis, [(s, (s - k) % n) for s in range(n)])

    def to_offset(a, axis, k):
        n = sizes[axis]
        return lax.ppermute(a, axis, [(s, (s + k) % n) for s in range(n)])

    def mate(a):
        return from_offset(a, "c", 1)

    offsets = [(dz, dy) for dz in range(ZL) for dy in range(Y)]
    n_chips = len(offsets)

    def chips(a, off, sign):
        dz, dy = off
        perm = []
        for z in range(ZL):
            for y in range(Y):
                perm.append((z * Y + y, (z + sign * dz) % ZL * Y + (y + sign * dy) % Y))
        return lax.ppermute(a, ("zl", "y"), perm)

    def swap_rows(a):
        return lax.ppermute(a, ("c", "zh"), [(1, 2), (2, 1)])

    last = [None]

    def seq(x):
        return x if last[0] is None else after(x, last[0])

    def mark(x):
        last[0] = x
        return x

    relayed = ZL == 2 and Y == 2

    def gather_start(a):
        if relayed:
            return [[a, mate(a)], [chips(a, (0, 1), -1)], [chips(a, (1, 0), -1)]]
        return [[a, mate(a)]] + [[chips(a, o, -1)] for o in offsets[1:]]

    def gather_next(got):
        py, pz = seq(got[1][0]), seq(got[-1][0])
        if relayed:
            half = tokens // 2
            d0 = chips(pz[:half], (0, 1), -1)
            d1 = chips(py[half:], (1, 0), -1)
            return [got[0], [py, mate(py)], [pz, mate(pz)], [d0, d1]]
        return [got[0]] + [[g[0], mate(seq(g[0]))] for g in got[1:]]

    def gather_last(got):
        if relayed:
            d0, d1 = seq(got[3][0]), seq(got[3][1])
            return got[:3] + [[d0, d1, mate(d0), mate(d1)]]
        return got

    def block_of(own, other, wide=False):
        block = own.astype(F32) + mate(other).astype(F32)
        return block if wide else block.astype(BF16)

    def scatter_end(own, arrived):
        for a in arrived:
            own = own + a.astype(F32)
        return own

    def product_blocks(make, between=None):
        parts = [None] * n_chips
        for o in range(n_chips)[::-1]:
            parts[o] = make(o)
            mark(parts[o][0])
        blocks = [None] * n_chips
        if between is not None:
            blocks.append(between())
        for o in range(n_chips)[::-1]:
            own, other = parts[o]
            blocks[o] = mark(block_of(seq(own), other, wide=o == 0))
        return blocks

    def send_blocks(blocks):
        return [chips(blocks[o], offsets[o], 1) for o in range(1, n_chips)[::-1]]

    def square_sum(a):
        total = a
        for axis in ("c", "zl", "y"):
            total = sum((from_offset(total, axis, k) for k in range(1, sizes[axis])), total)
        return total

    place = np.zeros((n_dev, 2 * n_dev + 4 + 2 * n_chips), np.int32)
    for own in range(n_dev):
        x, c, zh, zl, y = np.unravel_index(own, (X, C, ZH, ZL, Y))
        xs, cs, zhs, zls, ys = np.unravel_index(np.arange(n_dev), (X, C, ZH, ZL, Y))
        order = (cs - c) % C
        order = order * X + (xs - x) % X
        order = order * Y + (ys - y) % Y
        order = order * ZL + (zls - zl) % ZL
        order = order * ZH + (zhs - zh) % ZH
        send = ((((cs - c) % C * X + xs) * ZH + zhs) * ZL + zls) * Y + ys
        blocks = [
            ((c + k) % 2 * ZL + (zl + dz) % ZL) * Y + (y + dy) % Y
            for dz, dy in offsets
            for k in range(2)
        ]
        place[own, :n_dev] = order
        place[own, n_dev : n_dev + 2] = (c * ZL + zl) * Y + y, (zh * ZL + zl) * Y + y
        place[own, n_dev + 2 : n_dev + 4] = int(c == zh), x
        place[own, n_dev + 4 : n_dev + 4 + 2 * n_chips] = blocks
        place[own, n_dev + 4 + 2 * n_chips :] = send
    own_id = (((ix * C + ic) * ZH + izh) * ZL + izl) * Y + iy
    row = lax.dynamic_slice_in_dim(jnp.asarray(place), own_id, 1, 0)[0]
    table = row[: n_dev + 2]
    flags = row[n_dev + 2 : n_dev + 4]
    blk = row[n_dev + 4 : n_dev + 4 + 2 * n_chips]
    send_table = jnp.concatenate([row[n_dev + 4 + 2 * n_chips :], row[n_dev : n_dev + 2]])

    def sds(shape, dtype=BF16):
        return jax.ShapeDtypeStruct(shape, dtype)

    packed = pl.pallas_call(
        functools.partial(pack_kernel, a_w, f_w),
        in_specs=[VM] * 10,
        out_specs=VM,
        out_shape=sds((1, R + 1, packed_w)),
    )(
        jnp.swapaxes(rank_in_attn, 1, 2),
        rank_out_attn,
        magnitude_qkv,
        magnitude_out[None],
        jnp.swapaxes(rank_in_mlp, 1, 2),
        rank_out_mlp,
        magnitude_mlp,
        rank_in_down.T[None],
        rank_out_down[None],
        magnitude_down[None],
    )
    def over_z(a):
        found = []
        for k in range(1, ZL * ZH):
            dl, dh = divmod(k, ZH)
            perm = []
            for zh in range(ZH):
                for zl in range(ZL):
                    perm.append((zh * ZL + zl, (zh - dh) % ZH * ZL + (zl - dl) % ZL))
            found.append(lax.ppermute(a, ("zh", "zl"), perm))
        return found

    gathered = jnp.concatenate([packed] + over_z(packed), axis=0)
    moved_input = swap_rows(after(layer_input, packed))
    for axis in ("y", "x", "c"):
        gathered = jnp.concatenate(
            [gathered] + [from_offset(gathered, axis, k) for k in range(1, sizes[axis])], axis=0
        )
    mark(gathered)

    def fetch(w, axis, gate):
        part = w.shape[axis] // X
        at = after(ix, *gate) if gate else ix
        mine = lax.dynamic_slice_in_dim(w, at * part, part, axis)
        return lax.ppermute(mine, ("c", "zh"), [(0, 1), (3, 2)])

    def fetch_rest(mine):
        mine = seq(mine)
        parts = [mine]
        for k in range(1, X):
            perm = []
            for x in range(X):
                for cz in (1, 2):
                    perm.append((x * 4 + cz, (x - k) % X * 4 + cz))
            parts.append(lax.ppermute(mine, ("x", "c", "zh"), perm))
        return parts

    mine_qkv = fetch(base_qkv, 1, [])
    local_input = jnp.where(stay, layer_input, seq(moved_input))
    gain_one = norm_attn.astype(F32)
    gain_two = norm_mlp.astype(F32)
    input_full = local_input.astype(F32)
    unit_one, inverse_one = norm_forward(input_full)
    normed_one = mark((unit_one * gain_one).astype(BF16))
    one = gather_start(normed_one)

    turned_gu = jnp.swapaxes(base_gate_up, 1, 2)

    (
        at_qkv, at_gu, at_o, at_d, at_o0, at_d0, b_qkv, b_blocks, b_gu, b_o, b_d, mags_qkv, m_o, m_gu, m_d,
    ) = pl.pallas_call(
        functools.partial(unpack_kernel, a_w, f_w, dp),
        in_specs=[SM, VM],
        out_specs=[VM] * 15,
        out_shape=[
            sds((3 * R, model)),
            sds((2, R, model)),
            sds((R, width)),
            sds((R, hidden)),
            sds((R, width)),
            sds((R, hidden)),
            sds((3, R, width)),
            sds((3 * R, 3 * width)),
            sds((2, R, hidden)),
            sds((R, model)),
            sds((R, model)),
            sds((1, 3 * width), F32),
            sds((1, model), F32),
            sds((2, 1, hidden), F32),
            sds((1, model), F32),
        ],
    )(table, seq(gathered))
    mark(at_qkv)

    rows_here = jnp.stack([segment_ids, token_valid])
    rows_here = jnp.where(stay, rows_here, mate(rows_here))
    segments, valid = rows_here[0], rows_here[1]
    steps = jnp.arange(seq_len, dtype=jnp.int32)
    earlier = jnp.concatenate([segments[:1] - 1, segments[:-1]])
    first = lax.cummax(jnp.where(segments != earlier, steps, 0), axis=0)
    low = first[None]
    positions = seq(steps - first)
    frequency = ROPE_BASE ** (-(2.0 * jnp.arange(HD // 2, dtype=F32)) / HD)
    sign = jnp.concatenate([-jnp.ones(HD // 2, F32), jnp.ones(HD // 2, F32)])
    angle = positions.astype(F32)[:, None] * jnp.concatenate([frequency, frequency])[None, :]
    cos, sin = jnp.cos(angle), jnp.sin(angle) * sign[None, :]
    info = jnp.concatenate([blk, jnp.sum(valid)[None].astype(jnp.int32), first[::bq] // bq])
    mark(cos)

    def rows_square(base, at0, b):
        v = base.astype(F32) + FACTOR * mm(at0, b, 0, 0)
        return jnp.sum(v * v, axis=0)

    squares = jnp.stack(
        [rows_square(base_attn_out, seq(at_o0), b_o), rows_square(base_down, seq(at_d0), b_d)]
    )
    mark(squares)

    def add_over(a, axis):
        return sum((from_offset(a, axis, k) for k in range(1, sizes[axis])), a)

    one = gather_next(one)
    parts_qkv = fetch_rest(mine_qkv)
    mine_o = fetch(base_attn_out, 1, [parts_qkv[0]])
    moved_cot = swap_rows(after(cotangent, parts_qkv[0]))
    one = gather_last(one)
    mine_gate = fetch(turned_gu[:1], 2, [one[-1][0]])
    v_qkv, square_qkv = merge_qkv(flags, base_qkv, parts_qkv, seq(at_qkv), b_qkv)
    mark(square_qkv)
    norms_qkv = jnp.sqrt(square_qkv)
    scale_qkv = mark(mags_qkv / norms_qkv)

    qkv = []
    for o in range(n_chips):
        qkv.append(mark(qkv_chunk(blk, o, one[o], v_qkv, seq(scale_qkv), cos, sin)))
    local_cot = mark(jnp.where(stay, cotangent, seq(moved_cot)))
    grad_output = local_cot.astype(F32)
    parts_o = fetch_rest(mine_o)
    rest_gate = fetch_rest(mine_gate)
    down = [[local_cot, mate(local_cot)]] + [[chips(local_cot, o, -1)] for o in offsets[1 : Y + 1]]
    mine_up = fetch(turned_gu[1:], 2, [local_cot])
    column = over_z(squares)
    qkv_abs, att_abs, att_slot, lse = attn_fwd(info, qkv, seq(low), tokens, bq)
    mark(lse)
    for i in range(1, Y + 1):
        down[i] = [mark(seq(down[i][0]))]
    v_o = mark(merge_rows(flags, base_attn_out, parts_o, seq(at_o), b_o))
    rest_up = fetch_rest(mine_up)
    squares = add_over(sum(column, seq(squares)), "y")
    blocks = product_blocks(
        lambda o: product(att_slot, seq(v_o), False, 2, 2, block=(o, 2 * tokens))
    )
    arrived = send_blocks(blocks)
    down += [[chips(seq(down[Y][0]), o, -1)] for o in offsets[1:Y]]
    down[1:] = [[p[0], mate(seq(p[0]))] for p in down[1 : Y + 1]] + down[Y + 1 :]
    mine_d = fetch(base_down, 1, [blocks[1]])
    v_gu, square_gu = merge_gu(flags, turned_gu, rest_gate, rest_up, seq(at_gu), b_gu)
    norms_gu = jnp.sqrt(square_gu)
    scale_gu = mark(m_gu / norms_gu)
    norms_rows = jnp.sqrt(squares)
    norms_o, norms_d = norms_rows[0:1], norms_rows[1:2]
    scale_o = m_o / norms_o
    scale_d = m_d / norms_d
    summed_out = scatter_end(seq(blocks[0]), arrived)
    residual = input_full + summed_out * scale_o
    unit_two, inverse_two = norm_forward(residual)
    normed_two = mark((unit_two * gain_two).astype(BF16))
    two = gather_start(normed_two)

    parts_d = fetch_rest(mine_d)
    for i in range(Y + 1, n_chips):
        down[i].append(mate(seq(down[i][0])))
    v_d, v_ds = merge_down(flags, base_down, parts_d, seq(at_d), b_d, scale_d)
    mark(v_d)
    dhid = []
    for o in range(n_chips):
        dhid.append(mark(product(down[o], seq(v_ds), True, 1, 1)[0]))
    two = gather_next(two)

    hid, dz_gu, parts, dc_gu = [], [], [], 0.0
    blocks = [None] * n_chips
    for o in range(n_chips):
        if o == n_chips - 1:
            two = gather_last(two)
        h, dz, own, other, dc = mlp_chunk(two[o], dhid[o], v_gu, seq(scale_gu))
        mark(h)
        hid.append(h)
        dz_gu.append(dz)
        parts.append((own, other))
        dc_gu = dc_gu + dc
    blocks = [None] * n_chips
    for o in list(range(1, n_chips)) + [0]:
        blocks[o] = mark(block_of(seq(parts[o][0]), parts[o][1], wide=o == 0))
    arrived = send_blocks(blocks)
    down_parts = []
    dc_down = 0.0
    for o in range(n_chips):
        own, other, dc = down_product(hid[o], seq(v_d), down[o])
        mark(dc)
        dc_down = dc_down + dc
        down_parts.append((own, other))
    def shrink(col, mags, norms):
        return col * mags / (norms * norms * norms)

    def flat(lists):
        return [p for pieces in lists for p in pieces]

    ga_gu, gb_gu = rank_grads(
        flat(two),
        dz_gu,
        seq(at_gu).reshape(2 * R, model),
        b_gu,
        v_gu,
        shrink(dc_gu, m_gu, norms_gu),
        turned=True,
    )
    mark(ga_gu)
    grad_normed_two = scatter_end(seq(blocks[0]), arrived)
    grad_residual = grad_output + norm_backward(grad_normed_two, unit_two, inverse_two, gain_two)
    col_out = jnp.sum(grad_residual * summed_out, axis=0, keepdims=True)
    extra = jnp.concatenate([col_out, dc_down, jnp.zeros((14, model), F32)], axis=0)
    low_out = mark(
        jnp.concatenate([(grad_residual * scale_o).astype(BF16), extra.astype(BF16)], axis=0)
    )
    out = gather_start(low_out)

    down_blocks = [block_of(seq(p[0]), p[1], wide=o == 0) for o, p in enumerate(down_parts)]
    mark(down_blocks[-1])
    out = gather_next(out)

    def tails(lists):
        found = []
        for pieces in lists:
            n = len(pieces) // 2
            found += [pieces[n - 1][-16:], pieces[-1][-16:]]
        return found

    do_chunks = []
    for o in range(n_chips):
        if o == n_chips - 1:
            out = gather_last(out)
        do_chunks.append(mark(product(out[o], seq(v_o), True, 1, 1, tokens=tokens)[0]))
    cols = sum(p[:2].astype(F32) for p in tails(out))
    arrived_down = send_blocks([seq(b) for b in down_blocks])
    dz_qkv, dc_qkv = attn_bwd(
        info, qkv_abs, do_chunks, att_abs, lse, seq(low), cos, sin, scale_qkv, tokens, bq
    )
    mark(dc_qkv)
    summed_down = scatter_end(seq(down_blocks[0]), arrived_down)
    output_here = mark((residual + summed_down * scale_d).astype(BF16))
    moved_output = swap_rows(output_here)
    blocks = product_blocks(
        lambda o: product(dz_qkv, seq(v_qkv), True, 2, 2, block=(o, 2 * tokens)),
        lambda: mark(jnp.where(stay, output_here, seq(moved_output))),
    )
    layer_output = blocks.pop()
    arrived = send_blocks(blocks)

    ga_qkv, gb_all = rank_grads(
        flat(one),
        [dz_qkv],
        seq(at_qkv),
        b_blocks[None],
        v_qkv,
        shrink(dc_qkv, mags_qkv, norms_qkv)[None],
    )
    mark(ga_qkv)
    ga_o, gb_o = rank_grads(
        [att_slot],
        flat(out),
        seq(at_o),
        b_o[None],
        v_o,
        shrink(cols[0:1], m_o, norms_o)[None],
        rows=tokens,
    )
    mark(ga_o)
    ga_d, gb_d = rank_grads(
        hid,
        flat(down),
        seq(at_d),
        b_d[None],
        v_d,
        shrink(cols[1:2], m_d, norms_d)[None],
        scale=scale_d,
    )
    mark(ga_d)
    grad_normed_one = scatter_end(seq(blocks[0]), arrived)
    grad_here = grad_residual + norm_backward(grad_normed_one, unit_one, inverse_one, gain_one)
    low_here = mark(grad_here.astype(BF16))
    input_grad = jnp.where(stay, grad_here, swap_rows(low_here).astype(F32))
    mag_full = jnp.concatenate([col_out / norms_o, dc_down / norms_d], axis=0)
    grads = pl.pallas_call(
        functools.partial(pack_grads_kernel, a_w, f_w, dp),
        in_specs=[SM] + [VM] * 11,
        out_specs=VM,
        out_shape=sds((n_dev, R + 1, packed_w)),
    )(
        send_table,
        seq(ga_qkv),
        ga_gu,
        gb_o,
        gb_d,
        mag_full,
        ga_o,
        ga_d,
        gb_all,
        gb_gu,
        dc_qkv / norms_qkv,
        dc_gu / norms_gu,
    )
    half = n_dev // 2
    grads = grads[:half].astype(F32) + mate(grads[half:]).astype(F32)
    pieces = lax.all_to_all(
        grads.astype(BF16), ("x", "zh", "zl", "y"), split_axis=0, concat_axis=0, tiled=True
    )
    grads = jnp.sum(pieces.astype(F32), axis=0, keepdims=True)
    a1, b1, mq, mo, a2, b2, mm_, a3, b3, md = pl.pallas_call(
        functools.partial(unpack_grads_kernel, a_w, f_w),
        in_specs=[VM],
        out_specs=[VM] * 10,
        out_shape=[
            sds((4, R, a_w), F32),
            sds((4, R, a_w), F32),
            sds((3, a_w), F32),
            sds((1, a_w), F32),
            sds((2, R, a_w), F32),
            sds((2, R, f_w), F32),
            sds((2, f_w), F32),
            sds((1, R, f_w), F32),
            sds((1, R, a_w), F32),
            sds((1, a_w), F32),
        ],
    )(grads)
    return (
        layer_output,
        input_grad,
        jnp.swapaxes(a1, 1, 2),
        b1,
        mq,
        mo[0],
        jnp.swapaxes(a2, 1, 2),
        b2,
        mm_,
        a3[0].T,
        b3[0],
        md[0],
    )


def solution(mesh):
    dp, mp = mesh.shape["dp"], mesh.shape["mp"]
    shape = (dp // 2, 2, 2, 2, mp // 4)
    fine = Mesh(mesh.devices.reshape(shape), AXES)
    rows, cols = ("x", "c"), ("zh", "zl", "y")
    both = rows + cols
    return jax.shard_map(
        functools.partial(on_device, dict(zip(AXES, shape))),
        mesh=fine,
        in_specs=(
            P(both, None),
            P(both, None),
            P(rows),
            P(rows),
            P(),
            P(),
            P(None, None, cols),
            P(cols, None),
            P(None, None, cols),
            P(cols, None),
            P(None, both, None),
            P(None, None, both),
            P(None, both),
            P(both),
            P(None, both, None),
            P(None, None, both),
            P(None, both),
            P(both, None),
            P(None, both),
            P(both),
        ),
        out_specs=(
            P(both, None),
            P(both, None),
            P(None, both, None),
            P(None, None, both),
            P(None, both),
            P(both),
            P(None, both, None),
            P(None, None, both),
            P(None, both),
            P(both, None),
            P(None, both),
            P(both),
        ),
        check_vma=False,
    )
```

time: 850 us -> 768 us (0.904)
  the two profiles are of different devices: /device:TPU:3 before, /device:TPU:0 now
where the time goes in v2:
time: 768 us; the launch traced here: 760 us
  Pallas kernels  312 us (41%)
  waiting for transfers between devices  170 us (22%)
  starting transfers between devices  149 us (19%)
  other arithmetic  82.6 us (11%)
  local copies, waits for them, and re-layouts  40.5 us (5%)
    ppermute x27, waiting for transfers between devices, chips(): return lax.ppermute(a, ('zl', 'y'), perm)  112 us
    pallas_call x16, Pallas kernels, product(): pl.pallas_call(functools.partial(product_kernel, len(xs), turned, tuple(s...  64.7 us
    pallas_call x4, Pallas kernels, rank_grads(): pl.pallas_call(functools.partial(rank_kernel, len(xs), len(ds), groups, t...  56.5 us
    pallas_call x4, Pallas kernels, mlp_chunk(): pl.pallas_call(functools.partial(mlp_kernel, rows), in_specs=[VM] * (len(...  52.4 us
    ppermute x41, starting transfers between devices, from_offset(): return lax.ppermute(a, axis, [(s, (s - k) % n) for s in range(n)])  49.3 us
    all_to_all x1, waiting for transfers between devices, on_device(): lax.all_to_all(grads.astype(BF16), ('x', 'zh', 'zl', 'y'), split_axis=0,...  39 us
    pallas_call x1, Pallas kernels, attn_bwd(): pl.pallas_call(functools.partial(attn_bwd_kernel, len(do_chunks), tokens,...  31.9 us
    ppermute x6, starting transfers between devices, over_z(): found.append(lax.ppermute(a, ('zh', 'zl'), perm))  31 us
  transfers between devices with their start and end apart: 89, of which 22 were waited for; matrix products, arithmetic and copies ran while one was open for 14% of the time, Pallas kernels for 40%

profile of v2, /device:TPU:0, one launch (start us, length us, event | category | flops | bytes accessed | tf_op | source)
XLA Modules:
  0.0 759.6 jit_solution(11733900847725707484)
XLA Ops:
  30.8 7.8 %collective-permute-done.5 = bf16[8,17,1280]{2,1,0:T(8,128)(2,1)S(1)} collective-permute-done((bf16[8,17,1280]{2,1,0:T(8,128)(2,1)}, bf16[8,17,1280]{2,1,0:T(8,128)(2,1)S(1)}, u32[]{:S(2)}, u32[]{:S(2)}) %collective-permute-start.5) | collective-permute-done | bytes 348192 | tf_op jit(solution)/shard_map/ppermute | solution.py:914
  52.0 5.6 fusion.12
  63.7 19.8 %collective-permute-start.8 = (bf16[256,2048]{1,0:T(8,128)(2,1)S(1)}, bf16[256,2048]{1,0:T(8,128)(2,1)S(1)}, u32[]{:S(2)}, u32[]{:S(2)}) collective-permute-start(bf16[256,2048]{1,0:T(8,128)(2,1)S(1)} %fusion.5.refs_0_), channel_id=1, source_target_pairs={{0,8},{8,0},{1,9},{9,1},{2,10},{10,2},{3,11},{11,3},{4,12},{12,4},... | collective-permute-start | bytes 3145736 | tf_op jit(solution)/shard_map/ppermute | solution.py:914
  84.4 8.3 %collective-permute-done.13.refs_0_.refs_4_ = bf16[256,2048]{1,0:T(8,128)(2,1)} collective-permute-done((bf16[256,2048]{1,0:T(8,128)(2,1)S(1)}, bf16[256,2048]{1,0:T(8,128)(2,1)}, u32[]{:S(2)}, u32[]{:S(2)}) %collective-permute-start.13) | collective-permute-done | bytes 1048608 | tf_op jit(solution)/shard_map/ppermute | solution.py:932
  95.4 8.5 %collective-permute-done.16.refs_1_.refs_7_ = bf16[128,2048]{1,0:T(8,128)(2,1)} collective-permute-done((bf16[128,2048]{1,0:T(8,128)(2,1)S(1)}, bf16[128,2048]{1,0:T(8,128)(2,1)}, u32[]{:S(2)}, u32[]{:S(2)}) %collective-permute-start.16) | collective-permute-done | bytes 524320 | tf_op jit(solution)/shard_map/ppermute | solution.py:932
  114.3 6.2 shard_map.294
  121.8 6.3 shard_map.295.refs_0_
  133.2 6.3 shard_map.296.refs_1_
  139.5 6.4 shard_map.297.refs_2_
  147.4 6.3 shard_map.298.refs_3_
  156.9 6.2 fusion.23
  174.9 24.8 %shard_map.299 = (bf16[2048,768]{1,0:T(8,128)(2,1)}, bf16[2048,256]{1,0:T(8,128)(2,1)}, bf16[2048,256]{1,0:T(8,128)(2,1)}, f32[2,1,2048]{2,1,0:T(1,128)}) custom-call(s32[13]{0:T(128)} %pad_add_fusion.1.info, bf16[512,768]{1,0:T(8,128)(2,1)} %shard_map.295.refs_0_, bf16[512,768]{1,0:T(8,128)(2,1)} %shard_map.296.refs_1_, ...), custom_call_target="tpu_custom_call" | custom-call | flops 4294967 | bytes 9437 | tf_op jit(solution)/shard_map/pallas_call | solution.py:485
  212.5 23.0 %collective-permute-start.37 = (f32[2,2048]{1,0:T(2,128)S(1)}, f32[2,2048]{1,0:T(2,128)S(1)}, u32[]{:S(2)}, u32[]{:S(2)}) collective-permute-start(f32[2,2048]{1,0:T(2,128)S(1)} %copy-done.50), channel_id=1, source_target_pairs={{0,6},{2,4},{4,2},{6,0},{1,7},{3,5},{5,3},{7,1},{8,14},{10,12},{12... | collective-permute-start | bytes 49160 | tf_op jit(solution)/shard_map/ppermute | solution.py:1054
  275.7 10.9 %shard_map.305 = (bf16[2,704,2048]{2,1,0:T(8,128)(2,1)}, f32[2,1,704]{2,1,0:T(1,128)}) custom-call(s32[2]{0:T(128)} %get-tuple-element.439.flags, bf16[2,704,2048]{2,1,0:T(8,128)(2,1)} %bitcast.63, bf16[1,704,1024]{2,1,0:T(8,128)(2,1)} %collective-permute-done.28.refs_0_, bf16[1,704,1024]{2,1,0:T(8,128)(2,1)} %collective-permute-done.29.refs_1_, ...), custom_call_target="tpu_custom_call" | custom-call | flops 1476395 | bytes 23068 | tf_op jit(solution)/shard_map/pallas_call | solution.py:280
  289.4 7.1 collective-permute-done.33
  296.6 23.5 %collective-permute-done.32 = bf16[256,2048]{1,0:T(8,128)(2,1)} collective-permute-done((bf16[256,2048]{1,0:T(8,128)(2,1)}, bf16[256,2048]{1,0:T(8,128)(2,1)}, u32[]{:S(2)}, u32[]{:S(2)}) %collective-permute-start.32) | collective-permute-done | bytes 1048608 | tf_op jit(solution)/shard_map/ppermute | solution.py:932
  325.8 9.2 %collective-permute-done.43.refs_0_.refs_10_ = bf16[256,2048]{1,0:T(8,128)(2,1)} collective-permute-done((bf16[256,2048]{1,0:T(8,128)(2,1)}, bf16[256,2048]{1,0:T(8,128)(2,1)}, u32[]{:S(2)}, u32[]{:S(2)}) %collective-permute-start.43) | collective-permute-done | bytes 1048608 | tf_op jit(solution)/shard_map/ppermute | solution.py:932
  336.5 6.8 shard_map.306
  348.4 7.2 collective-permute-start.39
  376.7 12.2 %shard_map.311 = (bf16[512,704]{1,0:T(8,128)(2,1)}, bf16[2,512,704]{2,1,0:T(8,128)(2,1)}, bf16[256,2048]{1,0:T(8,128)(2,1)}, bf16[256,2048]{1,0:T(8,128)(2,1)}, f32[2,1,704]{2,1,0:T(1,128)}) custom-call(bf16[256,2048]{1,0:T(8,128)(2,1)} %copy-done.6, bf16[256,2048]{1,0:T(8,128)(2,1)} %collective-permute-done.39.refs_1_, ...), custom_call_target="tpu_custom_call" | custom-call | flops 5905580 | bytes 9961 | tf_op jit(solution)/shard_map/pallas_call | solution.py:679
  388.9 11.9 %shard_map.312 = (bf16[512,704]{1,0:T(8,128)(2,1)}, bf16[2,512,704]{2,1,0:T(8,128)(2,1)}, bf16[256,2048]{1,0:T(8,128)(2,1)}, bf16[256,2048]{1,0:T(8,128)(2,1)}, f32[2,1,704]{2,1,0:T(1,128)}) custom-call(bf16[256,2048]{1,0:T(8,128)(2,1)} %copy-done.11, bf16[256,2048]{1,0:T(8,128)(2,1)} %collective-permute-done.51.refs_1_.refs_3_, ...), custom_call_target="tpu_custom_call" | custom-call | flops 5905580 | bytes 9961 | tf_op jit(solution)/shard_map/pallas_call | solution.py:679
  400.8 12.4 %shard_map.313 = (bf16[512,704]{1,0:T(8,128)(2,1)}, bf16[2,512,704]{2,1,0:T(8,128)(2,1)}, bf16[256,2048]{1,0:T(8,128)(2,1)}, bf16[256,2048]{1,0:T(8,128)(2,1)}, f32[2,1,704]{2,1,0:T(1,128)}) custom-call(bf16[256,2048]{1,0:T(8,128)(2,1)} %collective-permute-done.47.refs_0_.refs_4_, bf16[256,2048]{1,0:T(8,128)(2,1)} %collective-permute-done.49.refs_1_.refs_5_, ...), custom_call_target="tpu_custom_call" | custom-call | flops 5905580 | bytes 9961 | tf_op jit(solution)/shard_map/pallas_call | solution.py:679
  417.9 15.9 %shard_map.314 = (bf16[512,704]{1,0:T(8,128)(2,1)}, bf16[2,512,704]{2,1,0:T(8,128)(2,1)}, bf16[256,2048]{1,0:T(8,128)(2,1)}, bf16[256,2048]{1,0:T(8,128)(2,1)}, f32[2,1,704]{2,1,0:T(1,128)}) custom-call(bf16[128,2048]{1,0:T(8,128)(2,1)} %collective-permute-done.48.refs_0_.refs_6_, bf16[128,2048]{1,0:T(8,128)(2,1)} %copy-done.24, ...), custom_call_target="tpu_custom_call" | custom-call | flops 5905580 | bytes 9961 | tf_op jit(solution)/shard_map/pallas_call | solution.py:679
  467.7 18.7 %shard_map.319 = (f32[32,2048]{1,0:T(8,128)}, f32[32,704]{1,0:T(8,128)}) custom-call(bf16[256,2048]{1,0:T(8,128)(2,1)} %copy-done.6, bf16[256,2048]{1,0:T(8,128)(2,1)} %collective-permute-done.39.refs_1_, bf16[256,2048]{1,0:T(8,128)(2,1)} %copy-done.11, bf16[256,2048]{1,0:T(8,128)(2,1)} %collective-permute-done.51.refs_1_.refs_3_, ...), custom_call_target="tpu_custom_call" | custom-call | flops 7247757 | bytes 19922 | tf_op jit(solution)/shard_map/pallas_call | solution.py:746
  501.5 22.4 %collective-permute-done.65.refs_0_.refs_3_ = bf16[272,2048]{1,0:T(8,128)(2,1)S(1)} collective-permute-done((bf16[272,2048]{1,0:T(8,128)(2,1)S(1)}, bf16[272,2048]{1,0:T(8,128)(2,1)S(1)}, u32[]{:S(2)}, u32[]{:S(2)}) %collective-permute-start.65) | collective-permute-done | bytes 1114144 | tf_op jit(solution)/shard_map/ppermute | solution.py:932
  563.5 31.9 %shard_map.324 = (bf16[2048,768]{1,0:T(8,128)(2,1)}, f32[1,768]{1,0:T(1,128)}) custom-call(s32[13]{0:T(128)} %pad_add_fusion.1.info, bf16[2048,768]{1,0:T(8,128)(2,1)} %get-tuple-element.328.qkv, bf16[512,256]{1,0:T(8,128)(2,1)} %shard_map.320.refs_0_, bf16[512,256]{1,0:T(8,128)(2,1)} %shard_map.321.refs_1_, bf16[512,256]{1,0:T(8,128)(2,1)} %shard_map.322.refs_2_, ...), custom_call_target="tpu_custom_call" | custom-call | flops 10737418 | bytes 12582 | tf_op jit(solution)/shard_map/pallas_call | solution.py:599
  595.3 11.0 %collective-permute-done.75 = bf16[256,2048]{1,0:T(8,128)(2,1)} collective-permute-done((bf16[256,2048]{1,0:T(8,128)(2,1)}, bf16[256,2048]{1,0:T(8,128)(2,1)}, u32[]{:S(2)}, u32[]{:S(2)}) %collective-permute-start.75) | collective-permute-done | bytes 1048608 | tf_op jit(solution)/shard_map/ppermute | solution.py:932
  649.9 13.7 %shard_map.329 = (f32[48,2048]{1,0:T(8,128)}, f32[48,768]{1,0:T(8,128)}) custom-call(bf16[256,2048]{1,0:T(8,128)(2,1)} %copy-done.7, bf16[256,2048]{1,0:T(8,128)(2,1)} %copy-done.13, bf16[256,2048]{1,0:T(8,128)(2,1)} %copy-done.10, bf16[256,2048]{1,0:T(8,128)(2,1)} %collective-permute-done.12.refs_1_.refs_3_, ...), custom_call_target="tpu_custom_call" | custom-call | flops 5905580 | bytes 14680 | tf_op jit(solution)/shard_map/pallas_call | solution.py:746
  664.2 10.4 %shard_map.330 = (f32[16,256]{1,0:T(8,128)}, f32[16,2048]{1,0:T(8,128)}) custom-call(bf16[2048,256]{1,0:T(8,128)(2,1)} %get-tuple-element.231.refs_0_.refs_1_, bf16[272,2048]{1,0:T(8,128)(2,1)} %copy-done.5, bf16[272,2048]{1,0:T(8,128)(2,1)} %copy-done.12, bf16[272,2048]{1,0:T(8,128)(2,1)} %copy-done.9, ...), custom_call_target="tpu_custom_call" | custom-call | flops 4831838 | bytes 10485 | tf_op jit(solution)/shard_map/pallas_call | solution.py:746
  674.6 13.8 %shard_map.331 = (f32[16,704]{1,0:T(8,128)}, f32[16,2048]{1,0:T(8,128)}) custom-call(bf16[512,704]{1,0:T(8,128)(2,1)} %get-tuple-element.283.h.refs_0_, bf16[512,704]{1,0:T(8,128)(2,1)} %get-tuple-element.288.h.refs_1_, bf16[512,704]{1,0:T(8,128)(2,1)} %get-tuple-element.290.h.refs_2_, bf16[512,704]{1,0:T(8,128)(2,1)} %get-tuple-element.297.h.refs_3_, ...), custom_call_target="tpu_custom_call" | custom-call | flops 5771362 | bytes 14155 | tf_op jit(solution)/shard_map/pallas_call | solution.py:746
  688.4 6.6 collective-permute-done.85
  718.0 39.0 %all-to-all-done = bf16[16,17,1280]{2,1,0:T(8,128)(2,1)S(1)} async-done(((bf16[16,17,1280]{2,1,0:T(8,128)(2,1)}), bf16[16,17,1280]{2,1,0:T(8,128)(2,1)S(1)}, u32[]{:S(2)}, u32[]{:S(2)}) %all-to-all-start) | async-done | bytes 696352 | tf_op jit(solution)/shard_map/all_to_all | solution.py:1338
  (455 shorter events, 336.9 us)
Async XLA Ops:
  18.1 43.8 %collective-permute-start.9 = (bf16[3,1024,256]{2,1,0:T(8,128)(2,1)}, bf16[3,1024,256]{2,1,0:T(8,128)(2,1)}, u32[]{:S(2)}, u32[]{:S(2)}) collective-permute-start(bf16[3,1024,256]{2,1,0:T(8,128)(2,1)} %constant_dynamic-slice_fusion.4), channel_id=1, source_target_pairs={{0,4},{12,8},{1,5},{13,9},{2,6},{14,10},{3,7},{15,11},{16,20},{28,... | collective-permute-start | bytes 4718600 | tf_op jit(solution)/shard_map/ppermute | solution.py:1069
  45.1 38.4 %collective-permute-start.11 = (bf16[256,2048]{1,0:T(8,128)(2,1)S(1)}, bf16[256,2048]{1,0:T(8,128)(2,1)S(1)}, u32[]{:S(2)}, u32[]{:S(2)}) collective-permute-start(bf16[256,2048]{1,0:T(8,128)(2,1)S(1)} %fusion.5.refs_0_), channel_id=1, source_target_pairs={{0,1},{1,0},{2,3},{3,2},{4,5},{5,4},{6,7},{7,6},{8,9},{9,8},{10,11... | collective-permute-start | bytes 3145736 | tf_op jit(solution)/shard_map/ppermute | solution.py:932
  46.7 46.0 %collective-permute-start.13 = (bf16[256,2048]{1,0:T(8,128)(2,1)S(1)}, bf16[256,2048]{1,0:T(8,128)(2,1)}, u32[]{:S(2)}, u32[]{:S(2)}) collective-permute-start(bf16[256,2048]{1,0:T(8,128)(2,1)S(1)} %fusion.5.refs_0_), channel_id=1, source_target_pairs={{0,2},{1,3},{2,0},{3,1},{4,6},{5,7},{6,4},{7,5},{8,10},{9,11},{10,... | collective-permute-start | bytes 3145736 | tf_op jit(solution)/shard_map/ppermute | solution.py:932
  61.9 49.4 %collective-permute-start.10 = (bf16[3,1024,256]{2,1,0:T(8,128)(2,1)}, bf16[3,1024,256]{2,1,0:T(8,128)(2,1)}, u32[]{:S(2)}, u32[]{:S(2)}) collective-permute-start(bf16[3,1024,256]{2,1,0:T(8,128)(2,1)} %collective-permute-done.9.refs_0_), channel_id=1, source_target_pairs={{4,20},{8,24},{20,4},{24,8},{5,21},{9,25},{21,5},{25,9},{6,22},{10... | collective-permute-start | bytes 4718600 | tf_op jit(solution)/shard_map/ppermute | solution.py:1079
  63.7 46.6 %collective-permute-start.8 = (bf16[256,2048]{1,0:T(8,128)(2,1)S(1)}, bf16[256,2048]{1,0:T(8,128)(2,1)S(1)}, u32[]{:S(2)}, u32[]{:S(2)}) collective-permute-start(bf16[256,2048]{1,0:T(8,128)(2,1)S(1)} %fusion.5.refs_0_), channel_id=1, source_target_pairs={{0,8},{8,0},{1,9},{9,1},{2,10},{10,2},{3,11},{11,3},{4,12},{12,4},... | collective-permute-start | bytes 3145736 | tf_op jit(solution)/shard_map/ppermute | solution.py:914
  103.9 35.6 %collective-permute-start.14 = (bf16[256,2048]{1,0:T(8,128)(2,1)}, bf16[256,2048]{1,0:T(8,128)(2,1)}, u32[]{:S(2)}, u32[]{:S(2)}) collective-permute-start(bf16[256,2048]{1,0:T(8,128)(2,1)} %collective-permute-done.13.refs_0_.refs_4_), channel_id=1, source_target_pairs={{0,8},{8,0},{1,9},{9,1},{2,10},{10,2},{3,11},{11,3},{4,12},{12,4},... | collective-permute-start | bytes 3145736 | tf_op jit(solution)/shard_map/ppermute | solution.py:914
  108.1 45.7 %collective-permute-start.19 = (bf16[256,2048]{1,0:T(8,128)(2,1)}, bf16[256,2048]{1,0:T(8,128)(2,1)}, u32[]{:S(2)}, u32[]{:S(2)}) collective-permute-start(bf16[256,2048]{1,0:T(8,128)(2,1)} %param.22), channel_id=1, source_target_pairs={{4,8},{8,4},{5,9},{9,5},{6,10},{10,6},{7,11},{11,7},{20,24},{24,20... | collective-permute-start | bytes 3145736 | tf_op jit(solution)/shard_map/ppermute | solution.py:935
  128.0 40.1 %collective-permute-start.20 = (bf16[256,1024]{1,0:T(8,128)(2,1)}, bf16[256,1024]{1,0:T(8,128)(2,1)}, u32[]{:S(2)}, u32[]{:S(2)}) collective-permute-start(bf16[256,1024]{1,0:T(8,128)(2,1)} %constant_dynamic-slice_fusion.3), channel_id=1, source_target_pairs={{0,4},{12,8},{1,5},{13,9},{2,6},{14,10},{3,7},{15,11},{16,20},{28,... | collective-permute-start | bytes 1572872 | tf_op jit(solution)/shard_map/ppermute | solution.py:1069
  155.1 44.6 %collective-permute-start.23 = (bf16[256,2048]{1,0:T(8,128)(2,1)S(1)}, bf16[256,2048]{1,0:T(8,128)(2,1)}, u32[]{:S(2)}, u32[]{:S(2)}) collective-permute-start(bf16[256,2048]{1,0:T(8,128)(2,1)S(1)} %broadcast_select_fusion.1.refs_0_.refs_4_), channel_id=1, source_target_pairs={{0,1},{1,0},{2,3},{3,2},{4,5},{5,4},{6,7},{7,6},{8,9},{9,8},{10,11... | collective-permute-start | bytes 3145736 | tf_op jit(solution)/shard_map/ppermute | solution.py:932
  156.6 43.1 %collective-permute-start.22 = (bf16[256,2048]{1,0:T(8,128)(2,1)S(1)}, bf16[256,2048]{1,0:T(8,128)(2,1)}, u32[]{:S(2)}, u32[]{:S(2)}) collective-permute-start(bf16[256,2048]{1,0:T(8,128)(2,1)S(1)} %broadcast_select_fusion.1.refs_0_.refs_4_), channel_id=1, source_target_pairs={{0,2},{1,3},{2,0},{3,1},{4,6},{5,7},{6,4},{7,5},{8,10},{9,11},{10,... | collective-permute-start | bytes 3145736 | tf_op jit(solution)/shard_map/ppermute | solution.py:932
  165.6 74.0 %collective-permute-start.28 = (bf16[1,704,1024]{2,1,0:T(8,128)(2,1)}, bf16[1,704,1024]{2,1,0:T(8,128)(2,1)}, u32[]{:S(2)}, u32[]{:S(2)}) collective-permute-start(bf16[1,704,1024]{2,1,0:T(8,128)(2,1)} %constant_dynamic-slice_fusion.2), channel_id=1, source_target_pairs={{0,4},{12,8},{1,5},{13,9},{2,6},{14,10},{3,7},{15,11},{16,20},{28,... | collective-permute-start | bytes 4325384 | tf_op jit(solution)/shard_map/ppermute | solution.py:1069
  171.1 77.9 %collective-permute-start.30 = (bf16[1,704,1024]{2,1,0:T(8,128)(2,1)S(1)}, bf16[1,704,1024]{2,1,0:T(8,128)(2,1)}, u32[]{:S(2)}, u32[]{:S(2)}) collective-permute-start(bf16[1,704,1024]{2,1,0:T(8,128)(2,1)S(1)} %constant_dynamic-slice_fusion.1), channel_id=1, source_target_pairs={{0,4},{12,8},{1,5},{13,9},{2,6},{14,10},{3,7},{15,11},{16,20},{28,... | collective-permute-start | bytes 4325384 | tf_op jit(solution)/shard_map/ppermute | solution.py:1069
  206.2 42.8 %collective-permute-start.24 = (bf16[256,2048]{1,0:T(8,128)(2,1)}, bf16[256,2048]{1,0:T(8,128)(2,1)S(1)}, u32[]{:S(2)}, u32[]{:S(2)}) collective-permute-start(bf16[256,2048]{1,0:T(8,128)(2,1)} %get-tuple-element.248), channel_id=1, source_target_pairs={{0,8},{8,0},{1,9},{9,1},{2,10},{10,2},{3,11},{11,3},{4,12},{12,4},... | collective-permute-start | bytes 3145736 | tf_op jit(solution)/shard_map/ppermute | solution.py:914
  254.9 41.7 %collective-permute-start.33 = (bf16[256,2048]{1,0:T(8,128)(2,1)}, bf16[256,2048]{1,0:T(8,128)(2,1)S(1)}, u32[]{:S(2)}, u32[]{:S(2)}) collective-permute-start(bf16[256,2048]{1,0:T(8,128)(2,1)} %add_convert_fusion.11), channel_id=1, source_target_pairs={{0,2},{1,3},{2,0},{3,1},{4,6},{5,7},{6,4},{7,5},{8,10},{9,11},{10,... | collective-permute-start | bytes 3145736 | tf_op jit(solution)/shard_map/ppermute | solution.py:932
  254.9 65.2 %collective-permute-start.32 = (bf16[256,2048]{1,0:T(8,128)(2,1)}, bf16[256,2048]{1,0:T(8,128)(2,1)}, u32[]{:S(2)}, u32[]{:S(2)}) collective-permute-start(bf16[256,2048]{1,0:T(8,128)(2,1)} %add_convert_fusion.12), channel_id=1, source_target_pairs={{0,3},{1,2},{2,1},{3,0},{4,7},{5,6},{6,5},{7,4},{8,11},{9,10},{10,... | collective-permute-start | bytes 3145736 | tf_op jit(solution)/shard_map/ppermute | solution.py:932
  263.1 60.3 %collective-permute-start.41 = (bf16[704,1024]{1,0:T(8,128)(2,1)}, bf16[704,1024]{1,0:T(8,128)(2,1)}, u32[]{:S(2)}, u32[]{:S(2)}) collective-permute-start(bf16[704,1024]{1,0:T(8,128)(2,1)} %constant_dynamic-slice_fusion), channel_id=1, source_target_pairs={{0,4},{12,8},{1,5},{13,9},{2,6},{14,10},{3,7},{15,11},{16,20},{28,... | collective-permute-start | bytes 4325384 | tf_op jit(solution)/shard_map/ppermute | solution.py:1069
  271.5 63.5 %collective-permute-start.40 = (bf16[256,2048]{1,0:T(8,128)(2,1)S(1)}, bf16[256,2048]{1,0:T(8,128)(2,1)}, u32[]{:S(2)}, u32[]{:S(2)}) collective-permute-start(bf16[256,2048]{1,0:T(8,128)(2,1)S(1)} %broadcast_select_fusion.1.refs_0_.refs_4_), channel_id=1, source_target_pairs={{0,8},{8,0},{1,9},{9,1},{2,10},{10,2},{3,11},{11,3},{4,12},{12,4},... | collective-permute-start | bytes 3145736 | tf_op jit(solution)/shard_map/ppermute | solution.py:914
  288.0 47.0 %collective-permute-start.43 = (bf16[256,2048]{1,0:T(8,128)(2,1)}, bf16[256,2048]{1,0:T(8,128)(2,1)}, u32[]{:S(2)}, u32[]{:S(2)}) collective-permute-start(bf16[256,2048]{1,0:T(8,128)(2,1)} %collective-permute-done.22.refs_0_.refs_8_), channel_id=1, source_target_pairs={{0,1},{1,0},{2,3},{3,2},{4,5},{5,4},{6,7},{7,6},{8,9},{9,8},{10,11... | collective-permute-start | bytes 3145736 | tf_op jit(solution)/shard_map/ppermute | solution.py:932
  325.6 35.3 %collective-permute-start.45 = (bf16[256,2048]{1,0:T(8,128)(2,1)}, bf16[256,2048]{1,0:T(8,128)(2,1)}, u32[]{:S(2)}, u32[]{:S(2)}) collective-permute-start(bf16[256,2048]{1,0:T(8,128)(2,1)} %collective-permute-done.22.refs_0_.refs_8_), channel_id=1, source_target_pairs={{0,8},{8,0},{1,9},{9,1},{2,10},{10,2},{3,11},{11,3},{4,12},{12,4},... | collective-permute-start | bytes 3145736 | tf_op jit(solution)/shard_map/ppermute | solution.py:914
  335.0 36.2 %collective-permute-start.50 = (bf16[256,2048]{1,0:T(8,128)(2,1)S(1)}, bf16[256,2048]{1,0:T(8,128)(2,1)S(1)}, u32[]{:S(2)}, u32[]{:S(2)}) collective-permute-start(bf16[256,2048]{1,0:T(8,128)(2,1)S(1)} %multiply_convert_fusion.1.refs_0_), channel_id=1, source_target_pairs={{0,1},{1,0},{2,3},{3,2},{4,5},{5,4},{6,7},{7,6},{8,9},{9,8},{10,11... | collective-permute-start | bytes 3145736 | tf_op jit(solution)/shard_map/ppermute | solution.py:932
  374.4 38.9 %collective-permute-start.52 = (bf16[128,2048]{1,0:T(8,128)(2,1)}, bf16[128,2048]{1,0:T(8,128)(2,1)S(1)}, u32[]{:S(2)}, u32[]{:S(2)}) collective-permute-start(bf16[128,2048]{1,0:T(8,128)(2,1)} %slice.158), channel_id=1, source_target_pairs={{0,2},{1,3},{2,0},{3,1},{4,6},{5,7},{6,4},{7,5},{8,10},{9,11},{10,... | collective-permute-start | bytes 1572872 | tf_op jit(solution)/shard_map/ppermute | solution.py:932
  376.1 37.7 %collective-permute-start.48 = (bf16[128,2048]{1,0:T(8,128)(2,1)}, bf16[128,2048]{1,0:T(8,128)(2,1)}, u32[]{:S(2)}, u32[]{:S(2)}) collective-permute-start(bf16[128,2048]{1,0:T(8,128)(2,1)} %slice.157), channel_id=1, source_target_pairs={{0,1},{1,0},{2,3},{3,2},{4,5},{5,4},{6,7},{7,6},{8,9},{9,8},{10,11... | collective-permute-start | bytes 1572872 | tf_op jit(solution)/shard_map/ppermute | solution.py:932
  436.8 49.8 %collective-permute-start.61 = (bf16[256,2048]{1,0:T(8,128)(2,1)}, bf16[256,2048]{1,0:T(8,128)(2,1)}, u32[]{:S(2)}, u32[]{:S(2)}) collective-permute-start(bf16[256,2048]{1,0:T(8,128)(2,1)} %add_convert_fusion.9), channel_id=1, source_target_pairs={{0,1},{1,0},{2,3},{3,2},{4,5},{5,4},{6,7},{7,6},{8,9},{9,8},{10,11... | collective-permute-start | bytes 3145736 | tf_op jit(solution)/shard_map/ppermute | solution.py:932
  440.8 45.7 %collective-permute-start.60 = (bf16[256,2048]{1,0:T(8,128)(2,1)}, bf16[256,2048]{1,0:T(8,128)(2,1)}, u32[]{:S(2)}, u32[]{:S(2)}) collective-permute-start(bf16[256,2048]{1,0:T(8,128)(2,1)} %add_convert_fusion.8), channel_id=1, source_target_pairs={{0,2},{1,3},{2,0},{3,1},{4,6},{5,7},{6,4},{7,5},{8,10},{9,11},{10,... | collective-permute-start | bytes 3145736 | tf_op jit(solution)/shard_map/ppermute | solution.py:932
  442.6 46.1 %collective-permute-start.59 = (bf16[256,2048]{1,0:T(8,128)(2,1)}, bf16[256,2048]{1,0:T(8,128)(2,1)}, u32[]{:S(2)}, u32[]{:S(2)}) collective-permute-start(bf16[256,2048]{1,0:T(8,128)(2,1)} %add_convert_fusion.7), channel_id=1, source_target_pairs={{0,3},{1,2},{2,1},{3,0},{4,7},{5,6},{6,5},{7,4},{8,11},{9,10},{10,... | collective-permute-start | bytes 3145736 | tf_op jit(solution)/shard_map/ppermute | solution.py:932
  558.0 37.3 %collective-permute-start.73 = (bf16[256,2048]{1,0:T(8,128)(2,1)}, bf16[256,2048]{1,0:T(8,128)(2,1)}, u32[]{:S(2)}, u32[]{:S(2)}) collective-permute-start(bf16[256,2048]{1,0:T(8,128)(2,1)} %add_convert_fusion.6), channel_id=1, source_target_pairs={{0,3},{1,2},{2,1},{3,0},{4,7},{5,6},{6,5},{7,4},{8,11},{9,10},{10,... | collective-permute-start | bytes 3145736 | tf_op jit(solution)/shard_map/ppermute | solution.py:932
  559.8 46.5 %collective-permute-start.75 = (bf16[256,2048]{1,0:T(8,128)(2,1)}, bf16[256,2048]{1,0:T(8,128)(2,1)}, u32[]{:S(2)}, u32[]{:S(2)}) collective-permute-start(bf16[256,2048]{1,0:T(8,128)(2,1)} %add_convert_fusion.5), channel_id=1, source_target_pairs={{0,2},{1,3},{2,0},{3,1},{4,6},{5,7},{6,4},{7,5},{8,10},{9,11},{10,... | collective-permute-start | bytes 3145736 | tf_op jit(solution)/shard_map/ppermute | solution.py:932
  560.1 47.0 %collective-permute-start.77 = (bf16[256,2048]{1,0:T(8,128)(2,1)}, bf16[256,2048]{1,0:T(8,128)(2,1)}, u32[]{:S(2)}, u32[]{:S(2)}) collective-permute-start(bf16[256,2048]{1,0:T(8,128)(2,1)} %add_convert_fusion.4), channel_id=1, source_target_pairs={{0,1},{1,0},{2,3},{3,2},{4,5},{5,4},{6,7},{7,6},{8,9},{9,8},{10,11... | collective-permute-start | bytes 3145736 | tf_op jit(solution)/shard_map/ppermute | solution.py:932
  642.8 52.2 %collective-permute-start.84 = (bf16[256,2048]{1,0:T(8,128)(2,1)}, bf16[256,2048]{1,0:T(8,128)(2,1)S(1)}, u32[]{:S(2)}, u32[]{:S(2)}) collective-permute-start(bf16[256,2048]{1,0:T(8,128)(2,1)} %add_convert_fusion.1), channel_id=1, source_target_pairs={{0,2},{1,3},{2,0},{3,1},{4,6},{5,7},{6,4},{7,5},{8,10},{9,11},{10,... | collective-permute-start | bytes 3145736 | tf_op jit(solution)/shard_map/ppermute | solution.py:932
  643.4 51.6 %collective-permute-start.83 = (bf16[256,2048]{1,0:T(8,128)(2,1)}, bf16[256,2048]{1,0:T(8,128)(2,1)S(1)}, u32[]{:S(2)}, u32[]{:S(2)}) collective-permute-start(bf16[256,2048]{1,0:T(8,128)(2,1)} %add_convert_fusion.2), channel_id=1, source_target_pairs={{0,3},{1,2},{2,1},{3,0},{4,7},{5,6},{6,5},{7,4},{8,11},{9,10},{10,... | collective-permute-start | bytes 3145736 | tf_op jit(solution)/shard_map/ppermute | solution.py:932
  646.4 48.6 %collective-permute-start.85 = (bf16[256,2048]{1,0:T(8,128)(2,1)}, bf16[256,2048]{1,0:T(8,128)(2,1)}, u32[]{:S(2)}, u32[]{:S(2)}) collective-permute-start(bf16[256,2048]{1,0:T(8,128)(2,1)} %add_convert_fusion), channel_id=1, source_target_pairs={{0,1},{1,0},{2,3},{3,2},{4,5},{5,4},{6,7},{7,6},{8,9},{9,8},{10,11... | collective-permute-start | bytes 3145736 | tf_op jit(solution)/shard_map/ppermute | solution.py:932
  710.0 46.9 %all-to-all-start = ((bf16[16,17,1280]{2,1,0:T(8,128)(2,1)}), bf16[16,17,1280]{2,1,0:T(8,128)(2,1)S(1)}, u32[]{:S(2)}, u32[]{:S(2)}) async-start(bf16[16,17,1280]{2,1,0:T(8,128)(2,1)} %add_convert_fusion.13), calls=%async_computation | async-start | bytes 1966080 | tf_op jit(solution)/shard_map/all_to_all | solution.py:1338
  (138 other events, 2044.3 us)

commit v3 on v2

--- a/solution.py
+++ b/solution.py
@@ -18,6 +18,7 @@
 BF16 = jnp.bfloat16
 F32 = jnp.float32
 NEG = -1e30
+LOG2E = 1.4426950408889634
 AXES = ("x", "c", "zh", "zl", "y")
 VM = pl.BlockSpec(memory_space=pltpu.VMEM)
 SM = pl.BlockSpec(memory_space=pltpu.SMEM)
@@ -33,12 +34,12 @@
     )
 
 
-def params(mib=58):
+def params(mib=18):
     return pltpu.CompilerParams(vmem_limit_bytes=mib * 1024 * 1024)
 
 
 def cost(flops, nbytes, trans=0):
-    scale = 1000
+    scale = 10**6
     return pl.CostEstimate(
         flops=int(flops) // scale,
         bytes_accessed=int(nbytes) // scale,
@@ -379,7 +380,7 @@
         co, si = cos[at : at + r], sin[at : at + r]
         q = z[:, :HD]
         k = z[:, HD : 2 * HD]
-        q = (q * co + pltpu.roll(q, HD // 2, 1) * si) * HD ** (-0.5)
+        q = (q * co + pltpu.roll(q, HD // 2, 1) * si) * (LOG2E * HD ** (-0.5))
         k = k * co + pltpu.roll(k, HD // 2, 1) * si
         out[at : at + r, :HD] = q.astype(BF16)
         out[at : at + r, HD : 2 * HD] = k.astype(BF16)
@@ -419,8 +420,11 @@
     )(blk, *pieces, w, scale, cos, cos, sin, sin)
 
 
-def masked(scores, low, first_key, first_query, valid_count):
-    keys = first_key + lax.broadcasted_iota(jnp.int32, scores.shape, 0)
+def masked(scores, low, first_key, first_query, valid_count, diagonal):
+    keys = first_key + lax.broadcasted_iota(jnp.int32, (scores.shape[0], 1), 0)
+    if not diagonal:
+        allowed = (keys >= low) & (keys < valid_count)
+        return jnp.where(allowed, scores, NEG)
     queries = first_query + lax.broadcasted_iota(jnp.int32, (1, scores.shape[1]), 1)
     high = jnp.minimum(queries, valid_count - 1)
     allowed = ((keys >= low) & (keys <= high)) | (keys == queries)
@@ -430,8 +434,9 @@
 def attn_fwd_kernel(n_chunks, tokens, bq, info, *refs):
     chunks = refs[:n_chunks]
     low, qkv_abs, att_abs, att_slot, lse, m_sc, l_sc, acc = refs[n_chunks:]
-    i = pl.program_id(1)
-    last = pl.num_programs(1) - 1
+    i = pl.program_id(0)
+    last = pl.num_programs(0) - 1
+    heads = m_sc.shape[0]
     slots = 2 * n_chunks
     valid_count = info[slots]
 
@@ -444,30 +449,39 @@
             ]
 
     q0 = pl.multiple_of(i * bq, bq)
-    q = qkv_abs[pl.ds(q0, bq), :HD]
-    lo = low[:, pl.ds(q0, bq)]
+    rows = pl.ds(q0, bq)
+    lo = low[:, rows]
     m_sc[...] = jnp.full(m_sc.shape, NEG, F32)
     l_sc[...] = jnp.zeros_like(l_sc)
     acc[...] = jnp.zeros_like(acc)
 
-    def step(j, carry):
+    def step(j, diagonal):
         k0 = pl.multiple_of(j * bq, bq)
-        k = qkv_abs[pl.ds(k0, bq), HD : 2 * HD]
-        v = qkv_abs[pl.ds(k0, bq), 2 * HD :]
-        s = masked(mm(k, q, 1, 1), lo, k0, q0, valid_count)
-        m_old = m_sc[...]
-        m_new = jnp.maximum(m_old, jnp.max(s, axis=0, keepdims=True))
-        p = jnp.exp(s - m_new)
-        alpha = jnp.exp(m_old - m_new)
-        m_sc[...] = m_new
-        l_sc[...] = l_sc[...] * alpha + jnp.sum(p, axis=0, keepdims=True)
-        acc[...] = acc[...] * alpha + mm(v, p.astype(BF16), 0, 0)
+        keys = pl.ds(k0, bq)
+        for h in range(heads):
+            at = 3 * HD * h
+            q = qkv_abs[rows, at : at + HD]
+            k = qkv_abs[keys, at + HD : at + 2 * HD]
+            v = qkv_abs[keys, at + 2 * HD : at + 3 * HD]
+            s = masked(mm(k, q, 1, 1), lo, k0, q0, valid_count, diagonal)
+            m_old = m_sc[h]
+            m_new = jnp.maximum(m_old, jnp.max(s, axis=0, keepdims=True))
+            p = jnp.exp2(s - m_new)
+            alpha = jnp.exp2(m_old - m_new)
+            m_sc[h] = m_new
+            l_sc[h] = l_sc[h] * alpha + jnp.sum(p, axis=0, keepdims=True)
+            acc[h] = acc[h] * alpha + mm(v, p.astype(BF16), 0, 0)
+
+    def full(j, carry):
+        step(j, False)
         return carry
 
-    lax.fori_loop(info[slots + 1 + i], i + 1, step, 0)
-    total = l_sc[...]
-    lse[0, :, pl.ds(q0, bq)] = m_sc[...] + jnp.log(total)
-    att_abs[pl.ds(q0, bq), :] = (acc[...] / total).T.astype(BF16)
+    lax.fori_loop(info[slots + 1 + i], i, full, 0)
+    step(i, True)
+    for h in range(heads):
+        total = l_sc[h]
+        lse[h, :, rows] = m_sc[h] + jnp.log2(total)
+        att_abs[rows, h * HD : (h + 1) * HD] = (acc[h] / total).T.astype(BF16)
 
     @pl.when(i == last)
     def _():
@@ -481,24 +495,24 @@
     heads = width // (3 * HD)
     seq = rows * len(chunks)
     n_blocks = seq // bq
-    whole = pl.BlockSpec((seq, HD), lambda h, i, f: (0, h))
+    whole = pl.BlockSpec((seq, heads * HD), lambda i, f: (0, 0))
     return pl.pallas_call(
         functools.partial(attn_fwd_kernel, len(chunks), tokens, bq),
         grid_spec=pltpu.PrefetchScalarGridSpec(
             num_scalar_prefetch=1,
-            grid=(heads, n_blocks),
-            in_specs=[pl.BlockSpec((rows, 3 * HD), lambda h, i, f: (0, h))] * len(chunks)
-            + [pl.BlockSpec((1, seq), lambda h, i, f: (0, 0))],
+            grid=(n_blocks,),
+            in_specs=[pl.BlockSpec((rows, width), lambda i, f: (0, 0))] * len(chunks)
+            + [pl.BlockSpec((1, seq), lambda i, f: (0, 0))],
             out_specs=[
-                pl.BlockSpec((seq, 3 * HD), lambda h, i, f: (0, h)),
+                pl.BlockSpec((seq, width), lambda i, f: (0, 0)),
                 whole,
                 whole,
-                pl.BlockSpec((1, 1, seq), lambda h, i, f: (h, 0, 0)),
+                pl.BlockSpec((heads, 1, seq), lambda i, f: (0, 0, 0)),
             ],
             scratch_shapes=[
-                pltpu.VMEM((1, bq), F32),
-                pltpu.VMEM((1, bq), F32),
-                pltpu.VMEM((HD, bq), F32),
+                pltpu.VMEM((heads, 1, bq), F32),
+                pltpu.VMEM((heads, 1, bq), F32),
+                pltpu.VMEM((heads, HD, bq), F32),
             ],
         ),
         out_shape=[
@@ -507,127 +521,133 @@
             jax.ShapeDtypeStruct((seq, heads * HD), BF16),
             jax.ShapeDtypeStruct((heads, 1, seq), F32),
         ],
-        compiler_params=params(),
+        compiler_params=params(40),
         cost_estimate=cost(
             4 * heads * seq * seq * HD, 2 * seq * width * 3, heads * seq * seq // 2
         ),
     )(info, *chunks, low)
 
 
-def attn_bwd_kernel(
-    n_chunks, tokens, bq, info, qkv, *refs
-):
+def attn_bwd_kernel(n_chunks, tokens, bq, info, qkv, *refs):
     dos = refs[:n_chunks]
     att, lse, low, cos, sin, scale, dz, dc, do_abs, delta, dq, dk, dv = refs[n_chunks:]
     slots = 2 * n_chunks
     valid_count = info[slots]
     seq = qkv.shape[0]
+    heads = dq.shape[0]
     n_blocks = seq // bq
     for s in range(slots):
         start = pl.multiple_of(info[s] * tokens, tokens)
         do_abs[pl.ds(start, tokens), :] = dos[s // 2][(s % 2) * tokens : (s % 2 + 1) * tokens, :]
     ones = jnp.ones((8, HD), F32)
-    for i in range(n_blocks):
-        r = slice(i * bq, (i + 1) * bq)
-        prod = do_abs[r, :].astype(F32) * att[r, :].astype(F32)
-        delta[:, r] = mm(ones, prod, 1, 1, lax.Precision.HIGHEST)[:1]
-    dq[...] = jnp.zeros_like(dq)
+
+    def sums(i, c):
+        r = pl.ds(pl.multiple_of(i * bq, bq), bq)
+        for h in range(heads):
+            cols = slice(h * HD, (h + 1) * HD)
+            prod = do_abs[r, cols].astype(F32) * att[r, cols].astype(F32)
+            delta[h, :, r] = mm(ones, prod, 1, 1, lax.Precision.HIGHEST)[:1]
+        return c
+
+    lax.fori_loop(0, n_blocks, sums, 0)
 
     def outer(j, carry):
         k0 = pl.multiple_of(j * bq, bq)
-        k = qkv[pl.ds(k0, bq), HD : 2 * HD]
-        v = qkv[pl.ds(k0, bq), 2 * HD :]
         krow = pl.ds(k0, bq)
-        dk[krow, :] = jnp.zeros((bq, HD), F32)
-        dv[krow, :] = jnp.zeros((bq, HD), F32)
+
+        def pair(i, diagonal):
+            q0 = pl.multiple_of(i * bq, bq)
+            qrow = pl.ds(q0, bq)
+            lo = low[:, qrow]
+            for h in range(heads):
+                at = 3 * HD * h
+                k = qkv[krow, at + HD : at + 2 * HD]
+                v = qkv[krow, at + 2 * HD : at + 3 * HD]
+                q = qkv[qrow, at : at + HD]
+                do = do_abs[qrow, h * HD : (h + 1) * HD]
+                s = masked(mm(k, q, 1, 1), lo, k0, q0, valid_count, diagonal)
+                p = jnp.exp2(s - lse[h, :, qrow])
+                dp = mm(v, do, 1, 1)
+                ds = (p * (dp - delta[h, :, qrow])).astype(BF16)
+                if diagonal:
+                    dv[h, krow, :] = mm(p.astype(BF16), do)
+                    dk[h, krow, :] = mm(ds, q)
+                else:
+                    dv[h, krow, :] += mm(p.astype(BF16), do)
+                    dk[h, krow, :] += mm(ds, q)
+                part = mm(ds, k, 0, 0)
+
+                @pl.when(j == info[slots + 1 + i])
+                def _():
+                    dq[h, qrow, :] = part
+
+                @pl.when(j > info[slots + 1 + i])
+                def _():
+                    dq[h, qrow, :] += part
+
+        pair(j, True)
 
         def inner(i, c):
             @pl.when(info[slots + 1 + i] <= j)
             def _():
-                q0 = pl.multiple_of(i * bq, bq)
-                qrow = pl.ds(q0, bq)
-                q = qkv[qrow, :HD]
-                do = do_abs[qrow, :]
-                s = masked(mm(k, q, 1, 1), low[:, qrow], k0, q0, valid_count)
-                p = jnp.exp(s - lse[0, :, qrow])
-                dp = mm(v, do, 1, 1)
-                ds = (p * (dp - delta[:, qrow])).astype(BF16)
-                dv[krow, :] += mm(p.astype(BF16), do)
-                dk[krow, :] += mm(ds, q)
-                dq[qrow, :] += mm(ds, k, 0, 0)
+                pair(i, False)
 
             return c
 
-        return lax.fori_loop(j, n_blocks, inner, carry)
+        return lax.fori_loop(j + 1, n_blocks, inner, carry)
 
     lax.fori_loop(0, n_blocks, outer, 0)
-    dcq = jnp.zeros((1, HD), F32)
-    dck = jnp.zeros((1, HD), F32)
-    dcv = jnp.zeros((1, HD), F32)
     half = HD // 2
-    for s in range(slots):
+    dc[...] = jnp.zeros_like(dc)
+
+    def finish(s, c):
         rows = pl.ds(pl.multiple_of(info[s] * tokens, tokens), tokens)
+        out = pl.ds(pl.multiple_of(s * tokens, tokens), tokens)
         co, si = cos[rows, :], sin[rows, :]
-        out = slice(s * tokens, (s + 1) * tokens)
 
         def back(u):
             return u * co - pltpu.roll(u, half, 1) * si
 
-        gq = back(dq[rows, :]) * HD ** (-0.5)
-        gk = back(dk[rows, :])
-        gv = dv[rows, :]
-        q = back(qkv[rows, :HD].astype(F32)) * HD**0.5
-        k = back(qkv[rows, HD : 2 * HD].astype(F32))
-        v = qkv[rows, 2 * HD :].astype(F32)
-        dcq += jnp.sum(gq * q, axis=0, keepdims=True)
-        dck += jnp.sum(gk * k, axis=0, keepdims=True)
-        dcv += jnp.sum(gv * v, axis=0, keepdims=True)
-        dz[out, :HD] = (gq * scale[:, :HD]).astype(BF16)
-        dz[out, HD : 2 * HD] = (gk * scale[:, HD : 2 * HD]).astype(BF16)
-        dz[out, 2 * HD :] = (gv * scale[:, 2 * HD :]).astype(BF16)
-    dc[:, :HD] = dcq / scale[:, :HD]
-    dc[:, HD : 2 * HD] = dck / scale[:, HD : 2 * HD]
-    dc[:, 2 * HD :] = dcv / scale[:, 2 * HD :]
+        for h in range(heads):
+            at = 3 * HD * h
+            qc, kc, vc = (slice(at + n * HD, at + (n + 1) * HD) for n in range(3))
+            gq = back(dq[h, rows, :]) * HD ** (-0.5)
+            gk = back(dk[h, rows, :]) * (1 / LOG2E)
+            gv = dv[h, rows, :]
+            q = back(qkv[rows, qc].astype(F32)) * (HD**0.5 / LOG2E)
+            k = back(qkv[rows, kc].astype(F32))
+            v = qkv[rows, vc].astype(F32)
+            dc[:, qc] += jnp.sum(gq * q, axis=0, keepdims=True)
+            dc[:, kc] += jnp.sum(gk * k, axis=0, keepdims=True)
+            dc[:, vc] += jnp.sum(gv * v, axis=0, keepdims=True)
+            dz[out, qc] = (gq * scale[:, qc]).astype(BF16)
+            dz[out, kc] = (gk * scale[:, kc]).astype(BF16)
+            dz[out, vc] = (gv * scale[:, vc]).astype(BF16)
+        return c
+
+    lax.fori_loop(0, slots, finish, 0)
+    dc[...] = dc[...] / scale[...]
 
 
 def attn_bwd(info, qkv_abs, do_chunks, att_abs, lse, low, cos, sin, scale, tokens, bq):
     seq, width = qkv_abs.shape
     heads = width // (3 * HD)
-    rows = do_chunks[0].shape[0]
-    once = lambda h, f: (0, 0)
-    head = lambda h, f: (0, h)
     return pl.pallas_call(
         functools.partial(attn_bwd_kernel, len(do_chunks), tokens, bq),
-        grid_spec=pltpu.PrefetchScalarGridSpec(
-            num_scalar_prefetch=1,
-            grid=(heads,),
-            in_specs=[pl.BlockSpec((seq, 3 * HD), head)]
-            + [pl.BlockSpec((rows, HD), head)] * len(do_chunks)
-            + [
-                pl.BlockSpec((seq, HD), head),
-                pl.BlockSpec((1, 1, seq), lambda h, f: (h, 0, 0)),
-                pl.BlockSpec((1, seq), once),
-                pl.BlockSpec((seq, HD), once),
-                pl.BlockSpec((seq, HD), once),
-                pl.BlockSpec((1, 3 * HD), head),
-            ],
-            out_specs=[
-                pl.BlockSpec((seq, 3 * HD), head),
-                pl.BlockSpec((1, 3 * HD), head),
-            ],
-            scratch_shapes=[
-                pltpu.VMEM((seq, HD), BF16),
-                pltpu.VMEM((1, seq), F32),
-                pltpu.VMEM((seq, HD), F32),
-                pltpu.VMEM((seq, HD), F32),
-                pltpu.VMEM((seq, HD), F32),
-            ],
-        ),
+        in_specs=[SM] + [VM] * (len(do_chunks) + 7),
+        out_specs=[VM] * 2,
+        scratch_shapes=[
+            pltpu.VMEM((seq, heads * HD), BF16),
+            pltpu.VMEM((heads, 1, seq), F32),
+            pltpu.VMEM((heads, seq, HD), F32),
+            pltpu.VMEM((heads, seq, HD), F32),
+            pltpu.VMEM((heads, seq, HD), F32),
+        ],
         out_shape=[
             jax.ShapeDtypeStruct((seq, width), BF16),
             jax.ShapeDtypeStruct((1, width), F32),
         ],
-        compiler_params=params(),
+        compiler_params=params(44),
         cost_estimate=cost(
             10 * heads * seq * seq * HD, 2 * seq * width * 4, heads * seq * seq // 2
         ),
@@ -982,9 +1002,14 @@
         blocks = [None] * n_chips
         if between is not None:
             blocks.append(between())
+        here = last[0]
+
+        def gated(x):
+            return x if between is None else after(x, here)
+
         for o in range(n_chips)[::-1]:
             own, other = parts[o]
-            blocks[o] = mark(block_of(seq(own), other, wide=o == 0))
+            blocks[o] = mark(block_of(seq(own), gated(other), wide=o == 0))
         return blocks
 
     def send_blocks(blocks):
@@ -1062,10 +1087,18 @@
         )
     mark(gathered)
 
-    def fetch(w, axis, gate):
+    def cut(w, axis, member=None):
         part = w.shape[axis] // X
-        at = after(ix, *gate) if gate else ix
-        mine = lax.dynamic_slice_in_dim(w, at * part, part, axis)
+        start = [0] * w.ndim
+        size = list(w.shape)
+        start[axis] = ix * part
+        size[axis] = part
+        if member is not None:
+            start[0], size[0] = member, 1
+        return lax.dynamic_slice(w, start, size)
+
+    def fetch(mine, *gate):
+        mine = after(mine, *gate) if gate else mine
         return lax.ppermute(mine, ("c", "zh"), [(0, 1), (3, 2)])
 
     def fetch_rest(mine):
@@ -1079,7 +1112,14 @@
             parts.append(lax.ppermute(mine, ("x", "c", "zh"), perm))
         return parts
 
-    mine_qkv = fetch(base_qkv, 1, [])
+    turned_gu = jnp.swapaxes(base_gate_up, 1, 2)
+    mine_qkv = fetch(cut(base_qkv, 1))
+    cuts = [
+        cut(base_attn_out, 1),
+        cut(turned_gu, 2, 0),
+        cut(turned_gu, 2, 1),
+        cut(base_down, 1),
+    ]
     local_input = jnp.where(stay, layer_input, seq(moved_input))
     gain_one = norm_attn.astype(F32)
     gain_two = norm_mlp.astype(F32)
@@ -1088,7 +1128,7 @@
     normed_one = mark((unit_one * gain_one).astype(BF16))
     one = gather_start(normed_one)
 
-    turned_gu = jnp.swapaxes(base_gate_up, 1, 2)
+    gathered = after(gathered, *cuts)
 
     (
         at_qkv, at_gu, at_o, at_d, at_o0, at_d0, b_qkv, b_blocks, b_gu, b_o, b_d, mags_qkv, m_o, m_gu, m_d,
@@ -1144,11 +1184,12 @@
         return sum((from_offset(a, axis, k) for k in range(1, sizes[axis])), a)
 
     one = gather_next(one)
+    column = over_z(squares)
     parts_qkv = fetch_rest(mine_qkv)
-    mine_o = fetch(base_attn_out, 1, [parts_qkv[0]])
+    mine_o = fetch(cuts[0], parts_qkv[0])
     moved_cot = swap_rows(after(cotangent, parts_qkv[0]))
     one = gather_last(one)
-    mine_gate = fetch(turned_gu[:1], 2, [one[-1][0]])
+    mine_gate = fetch(cuts[1], one[-1][0])
     v_qkv, square_qkv = merge_qkv(flags, base_qkv, parts_qkv, seq(at_qkv), b_qkv)
     mark(square_qkv)
     norms_qkv = jnp.sqrt(square_qkv)
@@ -1157,27 +1198,28 @@
     qkv = []
     for o in range(n_chips):
         qkv.append(mark(qkv_chunk(blk, o, one[o], v_qkv, seq(scale_qkv), cos, sin)))
+        if o == 0:
+            squares = add_over(sum(column, seq(squares)), "y")
+    mark(squares)
     local_cot = mark(jnp.where(stay, cotangent, seq(moved_cot)))
     grad_output = local_cot.astype(F32)
     parts_o = fetch_rest(mine_o)
     rest_gate = fetch_rest(mine_gate)
     down = [[local_cot, mate(local_cot)]] + [[chips(local_cot, o, -1)] for o in offsets[1 : Y + 1]]
-    mine_up = fetch(turned_gu[1:], 2, [local_cot])
-    column = over_z(squares)
+    mine_up = fetch(cuts[2], local_cot)
     qkv_abs, att_abs, att_slot, lse = attn_fwd(info, qkv, seq(low), tokens, bq)
     mark(lse)
     for i in range(1, Y + 1):
         down[i] = [mark(seq(down[i][0]))]
     v_o = mark(merge_rows(flags, base_attn_out, parts_o, seq(at_o), b_o))
     rest_up = fetch_rest(mine_up)
-    squares = add_over(sum(column, seq(squares)), "y")
     blocks = product_blocks(
         lambda o: product(att_slot, seq(v_o), False, 2, 2, block=(o, 2 * tokens))
     )
     arrived = send_blocks(blocks)
     down += [[chips(seq(down[Y][0]), o, -1)] for o in offsets[1:Y]]
     down[1:] = [[p[0], mate(seq(p[0]))] for p in down[1 : Y + 1]] + down[Y + 1 :]
-    mine_d = fetch(base_down, 1, [blocks[1]])
+    mine_d = fetch(cuts[3], blocks[1])
     v_gu, square_gu = merge_gu(flags, turned_gu, rest_gate, rest_up, seq(at_gu), b_gu)
     norms_gu = jnp.sqrt(square_gu)
     scale_gu = mark(m_gu / norms_gu)
@@ -1270,14 +1312,14 @@
         info, qkv_abs, do_chunks, att_abs, lse, seq(low), cos, sin, scale_qkv, tokens, bq
     )
     mark(dc_qkv)
-    summed_down = scatter_end(seq(down_blocks[0]), arrived_down)
-    output_here = mark((residual + summed_down * scale_d).astype(BF16))
-    moved_output = swap_rows(output_here)
     blocks = product_blocks(
         lambda o: product(dz_qkv, seq(v_qkv), True, 2, 2, block=(o, 2 * tokens)),
-        lambda: mark(jnp.where(stay, output_here, seq(moved_output))),
-    )
-    layer_output = blocks.pop()
+        lambda: mark(
+            (residual + scatter_end(seq(down_blocks[0]), arrived_down) * scale_d).astype(BF16)
+        ),
+    )
+    output_here = blocks.pop()
+    moved_output = swap_rows(output_here)
     arrived = send_blocks(blocks)
 
     ga_qkv, gb_all = rank_grads(
@@ -1309,10 +1351,6 @@
         scale=scale_d,
     )
     mark(ga_d)
-    grad_normed_one = scatter_end(seq(blocks[0]), arrived)
-    grad_here = grad_residual + norm_backward(grad_normed_one, unit_one, inverse_one, gain_one)
-    low_here = mark(grad_here.astype(BF16))
-    input_grad = jnp.where(stay, grad_here, swap_rows(low_here).astype(F32))
     mag_full = jnp.concatenate([col_out / norms_o, dc_down / norms_d], axis=0)
     grads = pl.pallas_call(
         functools.partial(pack_grads_kernel, a_w, f_w, dp),
@@ -1333,7 +1371,14 @@
         dc_qkv / norms_qkv,
         dc_gu / norms_gu,
     )
+    mark(grads)
+    layer_output = mark(jnp.where(stay, output_here, seq(moved_output)))
+    grad_normed_one = scatter_end(seq(blocks[0]), arrived)
+    grad_here = grad_residual + norm_backward(grad_normed_one, unit_one, inverse_one, gain_one)
+    low_here = mark(grad_here.astype(BF16))
+    input_grad = jnp.where(stay, grad_here, swap_rows(low_here).astype(F32))
     half = n_dev // 2
+    grads = seq(grads)
     grads = grads[:half].astype(F32) + mate(grads[half:]).astype(F32)
     pieces = lax.all_to_all(
         grads.astype(BF16), ("x", "zh", "zl", "y"), split_axis=0, concat_axis=0, tiled=True

time: 768 us -> 688 us (0.90)
  Pallas kernels: 312 us -> 195 us
  waiting for transfers between devices: 170 us -> 217 us
  other arithmetic: 82.6 us -> 63.3 us
    pallas_call x16, Pallas kernels: 64.7 us -> 28.4 us  [product(): pl.pallas_call(functools.partial(product_kernel, len(xs), turned, tuple(s...]
    ppermute x5, starting transfers between devices: 18.6 us -> 42.8 us  [fetch(): return lax.ppermute(mine, ('c', 'zh'), [(0, 1), (3, 2)])]
    ppermute x27, waiting for transfers between devices: 112 us -> 135 us  [chips(): return lax.ppermute(a, ('zl', 'y'), perm)]
    pallas_call x4, Pallas kernels: 56.5 us -> 35.5 us  [rank_grads(): pl.pallas_call(functools.partial(rank_kernel, len(xs), len(ds), groups, t...]
    ppermute x6, starting transfers between devices: 31 us -> 12.9 us  [over_z(): found.append(lax.ppermute(a, ('zh', 'zl'), perm))]
    pallas_call x4, Pallas kernels: 52.4 us -> 35.5 us  [mlp_chunk(): pl.pallas_call(functools.partial(mlp_kernel, rows), in_specs=[VM] * (len(...]
    unnamed x165 -> x327, local copies, waits for them, and re-layouts: 10.4 us -> 24.8 us
    ppermute x5, waiting for transfers between devices: 0.01 us -> 12.6 us  [fetch(): return lax.ppermute(mine, ('c', 'zh'), [(0, 1), (3, 2)])]
  transfers between devices with their start and end apart: 89 -> 89, of which waited for: 22 -> 25; matrix products, arithmetic and copies ran while one was open for 14% -> 11% of each run, Pallas kernels for 40% -> 28%
where the time goes in v3:
time: 688 us; the launch traced here: 678 us
  waiting for transfers between devices  217 us (32%)
  Pallas kernels  195 us (28%)
  starting transfers between devices  156 us (23%)
  other arithmetic  63.3 us (9%)
  local copies, waits for them, and re-layouts  40.9 us (6%)
    ppermute x27, waiting for transfers between devices, chips(): return lax.ppermute(a, ('zl', 'y'), perm)  135 us
    ppermute x41, starting transfers between devices, from_offset(): return lax.ppermute(a, axis, [(s, (s - k) % n) for s in range(n)])  45 us
    ppermute x5, starting transfers between devices, fetch(): return lax.ppermute(mine, ('c', 'zh'), [(0, 1), (3, 2)])  42.8 us
    ppermute x27, starting transfers between devices, chips(): return lax.ppermute(a, ('zl', 'y'), perm)  40.2 us
    all_to_all x1, waiting for transfers between devices, on_device(): lax.all_to_all(grads.astype(BF16), ('x', 'zh', 'zl', 'y'), split_axis=0,...  37.7 us
    pallas_call x4, Pallas kernels, mlp_chunk(): pl.pallas_call(functools.partial(mlp_kernel, rows), in_specs=[VM] * (len(...  35.5 us
    pallas_call x4, Pallas kernels, rank_grads(): pl.pallas_call(functools.partial(rank_kernel, len(xs), len(ds), groups, t...  35.5 us
    pallas_call x16, Pallas kernels, product(): pl.pallas_call(functools.partial(product_kernel, len(xs), turned, tuple(s...  28.4 us
  transfers between devices with their start and end apart: 89, of which 25 were waited for; matrix products, arithmetic and copies ran while one was open for 11% of the time, Pallas kernels for 28%

profile of v3, /device:TPU:0, one launch (start us, length us, event | category | flops | bytes accessed | tf_op | source)
XLA Modules:
  0.0 678.3 jit_solution(14368728114789999661)
XLA Ops:
  35.7 9.1 %collective-permute-done.5 = bf16[8,17,1280]{2,1,0:T(8,128)(2,1)S(1)} collective-permute-done((bf16[8,17,1280]{2,1,0:T(8,128)(2,1)}, bf16[8,17,1280]{2,1,0:T(8,128)(2,1)S(1)}, u32[]{:S(2)}, u32[]{:S(2)}) %collective-permute-start.5) | collective-permute-done | bytes 348192 | tf_op jit(solution)/shard_map/ppermute | solution.py:934
  64.8 13.4 %collective-permute-start.8 = (bf16[256,2048]{1,0:T(8,128)(2,1)}, bf16[256,2048]{1,0:T(8,128)(2,1)S(1)}, u32[]{:S(2)}, u32[]{:S(2)}) collective-permute-start(bf16[256,2048]{1,0:T(8,128)(2,1)} %fusion.5.refs_0_), channel_id=1, source_target_pairs={{0,8},{8,0},{1,9},{9,1},{2,10},{10,2},{3,11},{11,3},{4,12},{12,4},... | collective-permute-start | bytes 3145736 | tf_op jit(solution)/shard_map/ppermute | solution.py:934
  88.9 14.6 %collective-permute-done.20 = f32[2,2048]{1,0:T(2,128)S(1)} collective-permute-done((f32[2,2048]{1,0:T(2,128)S(1)}, f32[2,2048]{1,0:T(2,128)S(1)}, u32[]{:S(2)}, u32[]{:S(2)}) %collective-permute-start.20) | collective-permute-done | bytes 16416 | tf_op jit(solution)/shard_map/ppermute | solution.py:1079
  108.4 4.7 shard_map.295.refs_0_
  113.8 6.4 collective-permute-start.24
  124.0 7.7 %collective-permute-done.24.refs_0_ = bf16[256,1024]{1,0:T(8,128)(2,1)} collective-permute-done((bf16[256,1024]{1,0:T(8,128)(2,1)S(1)}, bf16[256,1024]{1,0:T(8,128)(2,1)}, u32[]{:S(2)}, u32[]{:S(2)}) %collective-permute-start.24) | collective-permute-done | bytes 524320 | tf_op jit(solution)/shard_map/ppermute | solution.py:1102
  133.2 18.3 %collective-permute-done.16.refs_1_.refs_7_ = bf16[128,2048]{1,0:T(8,128)(2,1)S(1)} collective-permute-done((bf16[128,2048]{1,0:T(8,128)(2,1)S(1)}, bf16[128,2048]{1,0:T(8,128)(2,1)S(1)}, u32[]{:S(2)}, u32[]{:S(2)}) %collective-permute-start.16) | collective-permute-done | bytes 524320 | tf_op jit(solution)/shard_map/ppermute | solution.py:952
  160.6 10.4 %collective-permute-start.32 = (bf16[1,704,1024]{2,1,0:T(8,128)(2,1)}, bf16[1,704,1024]{2,1,0:T(8,128)(2,1)}, u32[]{:S(2)}, u32[]{:S(2)}) collective-permute-start(bf16[1,704,1024]{2,1,0:T(8,128)(2,1)} %get-tuple-element.264), channel_id=1, source_target_pairs={{0,4},{12,8},{1,5},{13,9},{2,6},{14,10},{3,7},{15,11},{16,20},{28,... | collective-permute-start | bytes 4325384 | tf_op jit(solution)/shard_map/ppermute | solution.py:1102
  191.0 15.1 %shard_map.299 = (bf16[2048,768]{1,0:T(8,128)(2,1)S(1)}, bf16[2048,256]{1,0:T(8,128)(2,1)S(1)}, bf16[2048,256]{1,0:T(8,128)(2,1)S(1)}, f32[2,1,2048]{2,1,0:T(1,128)S(1)}) custom-call(s32[13]{0:T(128)S(1)} %pad_add_fusion.1.info, bf16[512,768]{1,0:T(8,128)(2,1)S(1)} %copy-done.48, bf16[512,768]{1,0:T(8,128)(2,1)S(1)} %shard_map.296.refs_1_, ...), custom_call_target="tpu_custom_call" | custom-call | flops 4294 | bytes 9 | tf_op jit(solution)/shard_map/pallas_call | solution.py:499
  218.3 13.4 %collective-permute-start.37 = (bf16[256,2048]{1,0:T(8,128)(2,1)S(1)}, bf16[256,2048]{1,0:T(8,128)(2,1)S(1)}, u32[]{:S(2)}, u32[]{:S(2)}) collective-permute-start(bf16[256,2048]{1,0:T(8,128)(2,1)S(1)} %add_convert_fusion.11), channel_id=1, source_target_pairs={{0,2},{1,3},{2,0},{3,1},{4,6},{5,7},{6,4},{7,5},{8,10},{9,11},{10,... | collective-permute-start | bytes 3145736 | tf_op jit(solution)/shard_map/ppermute | solution.py:952
  233.8 21.7 %collective-permute-start.41 = (bf16[704,1024]{1,0:T(8,128)(2,1)S(1)}, bf16[704,1024]{1,0:T(8,128)(2,1)S(1)}, u32[]{:S(2)}, u32[]{:S(2)}) collective-permute-start(bf16[704,1024]{1,0:T(8,128)(2,1)S(1)} %copy-done.131), channel_id=1, source_target_pairs={{0,4},{12,8},{1,5},{13,9},{2,6},{14,10},{3,7},{15,11},{16,20},{28,... | collective-permute-start | bytes 4325384 | tf_op jit(solution)/shard_map/ppermute | solution.py:1102
  255.8 11.0 %collective-permute-start.40 = (bf16[256,2048]{1,0:T(8,128)(2,1)}, bf16[256,2048]{1,0:T(8,128)(2,1)S(1)}, u32[]{:S(2)}, u32[]{:S(2)}) collective-permute-start(bf16[256,2048]{1,0:T(8,128)(2,1)} %broadcast_select_fusion.1.refs_0_.refs_4_), channel_id=1, source_target_pairs={{0,8},{8,0},{1,9},{9,1},{2,10},{10,2},{3,11},{11,3},{4,12},{12,4},... | collective-permute-start | bytes 3145736 | tf_op jit(solution)/shard_map/ppermute | solution.py:934
  266.9 8.0 %shard_map.305 = (bf16[2,704,2048]{2,1,0:T(8,128)(2,1)S(1)}, f32[2,1,704]{2,1,0:T(1,128)S(1)}) custom-call(s32[2]{0:T(128)S(1)} %get-tuple-element.453.flags, bf16[2,704,2048]{2,1,0:T(8,128)(2,1)S(1)} %bitcast.68, bf16[1,704,1024]{2,1,0:T(8,128)(2,1)} %collective-permute-done.32.refs_0_, bf16[1,704,1024]{2,1,0:T(8,128)(2,1)S(1)} %collective-permute-done.33.refs_1_, ...), custom_call_target="tpu_custom_call" | custom-call | flops 1476 | bytes 23 | tf_op jit(solution)/shard_map/pallas_call | solution.py:281
  275.5 11.4 %collective-permute-done.36 = bf16[256,2048]{1,0:T(8,128)(2,1)S(1)} collective-permute-done((bf16[256,2048]{1,0:T(8,128)(2,1)S(1)}, bf16[256,2048]{1,0:T(8,128)(2,1)S(1)}, u32[]{:S(2)}, u32[]{:S(2)}) %collective-permute-start.36) | collective-permute-done | bytes 1048608 | tf_op jit(solution)/shard_map/ppermute | solution.py:952
  288.3 4.9 collective-permute-done.41.refs_0_
  298.4 17.5 %collective-permute-done.43.refs_0_.refs_10_ = bf16[256,2048]{1,0:T(8,128)(2,1)S(1)} collective-permute-done((bf16[256,2048]{1,0:T(8,128)(2,1)}, bf16[256,2048]{1,0:T(8,128)(2,1)S(1)}, u32[]{:S(2)}, u32[]{:S(2)}) %collective-permute-start.43) | collective-permute-done | bytes 1048608 | tf_op jit(solution)/shard_map/ppermute | solution.py:952
  331.9 9.6 %collective-permute-done.50.refs_0_.refs_2_ = bf16[256,2048]{1,0:T(8,128)(2,1)S(1)} collective-permute-done((bf16[256,2048]{1,0:T(8,128)(2,1)S(1)}, bf16[256,2048]{1,0:T(8,128)(2,1)S(1)}, u32[]{:S(2)}, u32[]{:S(2)}) %collective-permute-start.50) | collective-permute-done | bytes 1048608 | tf_op jit(solution)/shard_map/ppermute | solution.py:952
  343.8 8.0 %shard_map.311 = (bf16[512,704]{1,0:T(8,128)(2,1)S(1)}, bf16[2,512,704]{2,1,0:T(8,128)(2,1)S(1)}, bf16[256,2048]{1,0:T(8,128)(2,1)S(1)}, bf16[256,2048]{1,0:T(8,128)(2,1)S(1)}, f32[2,1,704]{2,1,0:T(1,128)S(1)}) custom-call(bf16[256,2048]{1,0:T(8,128)(2,1)S(1)} %multiply_convert_fusion.1.refs_0_, bf16[256,2048]{1,0:T(8,128)(2,1)S(1)} %collective-permute-done.39.refs_1_, ...), custom_call_target="tpu_custom_call" | custom-call | flops 5905 | bytes 9 | tf_op jit(solution)/shard_map/pallas_call | solution.py:699
  351.9 8.6 %shard_map.312 = (bf16[512,704]{1,0:T(8,128)(2,1)S(1)}, bf16[2,512,704]{2,1,0:T(8,128)(2,1)S(1)}, bf16[256,2048]{1,0:T(8,128)(2,1)S(1)}, bf16[256,2048]{1,0:T(8,128)(2,1)}, f32[2,1,704]{2,1,0:T(1,128)S(1)}) custom-call(bf16[256,2048]{1,0:T(8,128)(2,1)S(1)} %collective-permute-done.50.refs_0_.refs_2_, ...), custom_call_target="tpu_custom_call" | custom-call | flops 5905 | bytes 9 | tf_op jit(solution)/shard_map/pallas_call | solution.py:699
  360.4 7.8 %shard_map.313 = (bf16[512,704]{1,0:T(8,128)(2,1)S(1)}, bf16[2,512,704]{2,1,0:T(8,128)(2,1)S(1)}, bf16[256,2048]{1,0:T(8,128)(2,1)S(1)}, bf16[256,2048]{1,0:T(8,128)(2,1)S(1)}, f32[2,1,704]{2,1,0:T(1,128)S(1)}) custom-call(bf16[256,2048]{1,0:T(8,128)(2,1)S(1)} %collective-permute-done.47.refs_0_.refs_4_, ...), custom_call_target="tpu_custom_call" | custom-call | flops 5905 | bytes 9 | tf_op jit(solution)/shard_map/pallas_call | solution.py:699
  371.9 11.2 %shard_map.314 = (bf16[512,704]{1,0:T(8,128)(2,1)S(1)}, bf16[2,512,704]{2,1,0:T(8,128)(2,1)S(1)}, bf16[256,2048]{1,0:T(8,128)(2,1)S(1)}, bf16[256,2048]{1,0:T(8,128)(2,1)S(1)}, f32[2,1,704]{2,1,0:T(1,128)S(1)}) custom-call(bf16[128,2048]{1,0:T(8,128)(2,1)S(1)} %collective-permute-done.48.refs_0_.refs_6_, ...), custom_call_target="tpu_custom_call" | custom-call | flops 5905 | bytes 9 | tf_op jit(solution)/shard_map/pallas_call | solution.py:699
  413.1 11.1 %shard_map.319 = (f32[32,2048]{1,0:T(8,128)S(1)}, f32[32,704]{1,0:T(8,128)S(1)}) custom-call(bf16[256,2048]{1,0:T(8,128)(2,1)S(1)} %multiply_convert_fusion.1.refs_0_, bf16[256,2048]{1,0:T(8,128)(2,1)S(1)} %collective-permute-done.39.refs_1_, bf16[256,2048]{1,0:T(8,128)(2,1)S(1)} %collective-permute-done.50.refs_0_.refs_2_, ...), custom_call_target="tpu_custom_call" | custom-call | flops 7247 | bytes 19 | tf_op jit(solution)/shard_map/pallas_call | solution.py:766
  424.4 14.1 %collective-permute-done.59 = bf16[256,2048]{1,0:T(8,128)(2,1)} collective-permute-done((bf16[256,2048]{1,0:T(8,128)(2,1)}, bf16[256,2048]{1,0:T(8,128)(2,1)}, u32[]{:S(2)}, u32[]{:S(2)}) %collective-permute-start.59) | collective-permute-done | bytes 1048608 | tf_op jit(solution)/shard_map/ppermute | solution.py:952
  450.9 21.4 %collective-permute-done.65.refs_0_.refs_3_ = bf16[272,2048]{1,0:T(8,128)(2,1)S(1)} collective-permute-done((bf16[272,2048]{1,0:T(8,128)(2,1)S(1)}, bf16[272,2048]{1,0:T(8,128)(2,1)S(1)}, u32[]{:S(2)}, u32[]{:S(2)}) %collective-permute-start.65) | collective-permute-done | bytes 1114144 | tf_op jit(solution)/shard_map/ppermute | solution.py:952
  479.9 9.0 %collective-permute-done.70.refs_1_.refs_8_ = bf16[144,2048]{1,0:T(8,128)(2,1)S(1)} collective-permute-done((bf16[144,2048]{1,0:T(8,128)(2,1)S(1)}, bf16[144,2048]{1,0:T(8,128)(2,1)S(1)}, u32[]{:S(2)}, u32[]{:S(2)}) %collective-permute-start.70) | collective-permute-done | bytes 589856 | tf_op jit(solution)/shard_map/ppermute | solution.py:952
  504.0 25.4 %shard_map.324 = (bf16[2048,768]{1,0:T(8,128)(2,1)S(1)}, f32[1,768]{1,0:T(1,128)S(1)}) custom-call(s32[13]{0:T(128)S(1)} %pad_add_fusion.1.info, bf16[2048,768]{1,0:T(8,128)(2,1)} %copy-done.49, bf16[512,256]{1,0:T(8,128)(2,1)S(1)} %shard_map.320.refs_0_, bf16[512,256]{1,0:T(8,128)(2,1)S(1)} %shard_map.321.refs_1_, bf16[512,256]{1,0:T(8,128)(2,1)S(1)} %shard_map.322.refs_2_, ...), custom_call_target="tpu_custom_call" | custom-call | flops 10737 | bytes 12 | tf_op jit(solution)/shard_map/pallas_call | solution.py:635
  538.2 6.1 collective-permute-done.75
  563.2 9.0 %shard_map.329 = (f32[48,2048]{1,0:T(8,128)S(1)}, f32[48,768]{1,0:T(8,128)S(1)}) custom-call(bf16[256,2048]{1,0:T(8,128)(2,1)} %fusion.5.refs_0_, bf16[256,2048]{1,0:T(8,128)(2,1)S(1)} %copy-done.40, bf16[256,2048]{1,0:T(8,128)(2,1)S(1)} %copy-done.26, bf16[256,2048]{1,0:T(8,128)(2,1)S(1)} %copy-done.43, bf16[256,2048]{1,0:T(8,128)(2,1)S(1)} %copy-done.29, ...), custom_call_target="tpu_custom_call" | custom-call | flops 5905 | bytes 14 | tf_op jit(solution)/shard_map/pallas_call | solution.py:766
  572.5 5.6 shard_map.330
  578.2 9.8 %shard_map.331 = (f32[16,704]{1,0:T(8,128)S(1)}, f32[16,2048]{1,0:T(8,128)S(1)}) custom-call(bf16[512,704]{1,0:T(8,128)(2,1)S(1)} %copy-done.51, bf16[512,704]{1,0:T(8,128)(2,1)S(1)} %copy-done.53, bf16[512,704]{1,0:T(8,128)(2,1)S(1)} %copy-done.55, bf16[512,704]{1,0:T(8,128)(2,1)S(1)} %copy-done.57, ...), custom_call_target="tpu_custom_call" | custom-call | flops 5771 | bytes 14 | tf_op jit(solution)/shard_map/pallas_call | solution.py:766
  596.4 22.2 %collective-permute-done.83 = bf16[256,2048]{1,0:T(8,128)(2,1)} collective-permute-done((bf16[256,2048]{1,0:T(8,128)(2,1)}, bf16[256,2048]{1,0:T(8,128)(2,1)}, u32[]{:S(2)}, u32[]{:S(2)}) %collective-permute-start.83) | collective-permute-done | bytes 1048608 | tf_op jit(solution)/shard_map/ppermute | solution.py:952
  637.7 37.7 %all-to-all-done = bf16[16,17,1280]{2,1,0:T(8,128)(2,1)S(1)} async-done(((bf16[16,17,1280]{2,1,0:T(8,128)(2,1)}), bf16[16,17,1280]{2,1,0:T(8,128)(2,1)S(1)}, u32[]{:S(2)}, u32[]{:S(2)}) %all-to-all-start) | async-done | bytes 696352 | tf_op jit(solution)/shard_map/all_to_all | solution.py:1383
  (616 shorter events, 269.9 us)
Async XLA Ops:
  7.8 43.8 %collective-permute-start = (bf16[256,2048]{1,0:T(8,128)(2,1)}, bf16[256,2048]{1,0:T(8,128)(2,1)}, u32[]{:S(2)}, u32[]{:S(2)}) collective-permute-start(bf16[256,2048]{1,0:T(8,128)(2,1)} %param.21), channel_id=1, source_target_pairs={{4,8},{8,4},{5,9},{9,5},{6,10},{10,6},{7,11},{11,7},{20,24},{24,20... | collective-permute-start | bytes 3145736 | tf_op jit(solution)/shard_map/ppermute | solution.py:955
  22.7 40.2 %collective-permute-start.9 = (bf16[3,1024,256]{2,1,0:T(8,128)(2,1)}, bf16[3,1024,256]{2,1,0:T(8,128)(2,1)S(1)}, u32[]{:S(2)}, u32[]{:S(2)}) collective-permute-start(bf16[3,1024,256]{2,1,0:T(8,128)(2,1)} %constant_dynamic-slice_fusion.2), channel_id=1, source_target_pairs={{0,4},{12,8},{1,5},{13,9},{2,6},{14,10},{3,7},{15,11},{16,20},{28,... | collective-permute-start | bytes 4718600 | tf_op jit(solution)/shard_map/ppermute | solution.py:1102
  64.8 42.5 %collective-permute-start.8 = (bf16[256,2048]{1,0:T(8,128)(2,1)}, bf16[256,2048]{1,0:T(8,128)(2,1)S(1)}, u32[]{:S(2)}, u32[]{:S(2)}) collective-permute-start(bf16[256,2048]{1,0:T(8,128)(2,1)} %fusion.5.refs_0_), channel_id=1, source_target_pairs={{0,8},{8,0},{1,9},{9,1},{2,10},{10,2},{3,11},{11,3},{4,12},{12,4},... | collective-permute-start | bytes 3145736 | tf_op jit(solution)/shard_map/ppermute | solution.py:934
  78.2 42.0 %collective-permute-start.11 = (bf16[256,2048]{1,0:T(8,128)(2,1)}, bf16[256,2048]{1,0:T(8,128)(2,1)S(1)}, u32[]{:S(2)}, u32[]{:S(2)}) collective-permute-start(bf16[256,2048]{1,0:T(8,128)(2,1)} %fusion.5.refs_0_), channel_id=1, source_target_pairs={{0,1},{1,0},{2,3},{3,2},{4,5},{5,4},{6,7},{7,6},{8,9},{9,8},{10,11... | collective-permute-start | bytes 3145736 | tf_op jit(solution)/shard_map/ppermute | solution.py:952
  79.7 40.5 %collective-permute-start.13 = (bf16[256,2048]{1,0:T(8,128)(2,1)}, bf16[256,2048]{1,0:T(8,128)(2,1)S(1)}, u32[]{:S(2)}, u32[]{:S(2)}) collective-permute-start(bf16[256,2048]{1,0:T(8,128)(2,1)} %fusion.5.refs_0_), channel_id=1, source_target_pairs={{0,2},{1,3},{2,0},{3,1},{4,6},{5,7},{6,4},{7,5},{8,10},{9,11},{10,... | collective-permute-start | bytes 3145736 | tf_op jit(solution)/shard_map/ppermute | solution.py:952
  120.2 35.3 %collective-permute-start.12 = (bf16[256,2048]{1,0:T(8,128)(2,1)S(1)}, bf16[256,2048]{1,0:T(8,128)(2,1)S(1)}, u32[]{:S(2)}, u32[]{:S(2)}) collective-permute-start(bf16[256,2048]{1,0:T(8,128)(2,1)S(1)} %collective-permute-done.11.refs_0_.refs_2_), channel_id=1, source_target_pairs={{0,8},{8,0},{1,9},{9,1},{2,10},{10,2},{3,11},{11,3},{4,12},{12,4},... | collective-permute-start | bytes 3145736 | tf_op jit(solution)/shard_map/ppermute | solution.py:934
  120.2 37.1 %collective-permute-start.14 = (bf16[256,2048]{1,0:T(8,128)(2,1)S(1)}, bf16[256,2048]{1,0:T(8,128)(2,1)S(1)}, u32[]{:S(2)}, u32[]{:S(2)}) collective-permute-start(bf16[256,2048]{1,0:T(8,128)(2,1)S(1)} %collective-permute-done.13.refs_0_.refs_4_), channel_id=1, source_target_pairs={{0,8},{8,0},{1,9},{9,1},{2,10},{10,2},{3,11},{11,3},{4,12},{12,4},... | collective-permute-start | bytes 3145736 | tf_op jit(solution)/shard_map/ppermute | solution.py:934
  120.9 30.7 %collective-permute-start.16 = (bf16[128,2048]{1,0:T(8,128)(2,1)S(1)}, bf16[128,2048]{1,0:T(8,128)(2,1)S(1)}, u32[]{:S(2)}, u32[]{:S(2)}) collective-permute-start(bf16[128,2048]{1,0:T(8,128)(2,1)S(1)} %slice.146), channel_id=1, source_target_pairs={{0,2},{1,3},{2,0},{3,1},{4,6},{5,7},{6,4},{7,5},{8,10},{9,11},{10,... | collective-permute-start | bytes 1572872 | tf_op jit(solution)/shard_map/ppermute | solution.py:952
  121.3 30.2 %collective-permute-start.15 = (bf16[128,2048]{1,0:T(8,128)(2,1)S(1)}, bf16[128,2048]{1,0:T(8,128)(2,1)S(1)}, u32[]{:S(2)}, u32[]{:S(2)}) collective-permute-start(bf16[128,2048]{1,0:T(8,128)(2,1)S(1)} %slice.145), channel_id=1, source_target_pairs={{0,1},{1,0},{2,3},{3,2},{4,5},{5,4},{6,7},{7,6},{8,9},{9,8},{10,11... | collective-permute-start | bytes 1572872 | tf_op jit(solution)/shard_map/ppermute | solution.py:952
  131.7 75.4 %collective-permute-start.27 = (bf16[256,2048]{1,0:T(8,128)(2,1)}, bf16[256,2048]{1,0:T(8,128)(2,1)}, u32[]{:S(2)}, u32[]{:S(2)}) collective-permute-start(bf16[256,2048]{1,0:T(8,128)(2,1)} %broadcast_select_fusion.1.refs_0_.refs_4_), channel_id=1, source_target_pairs={{0,1},{1,0},{2,3},{3,2},{4,5},{5,4},{6,7},{7,6},{8,9},{9,8},{10,11... | collective-permute-start | bytes 3145736 | tf_op jit(solution)/shard_map/ppermute | solution.py:952
  151.5 55.6 %collective-permute-start.26 = (bf16[256,2048]{1,0:T(8,128)(2,1)}, bf16[256,2048]{1,0:T(8,128)(2,1)}, u32[]{:S(2)}, u32[]{:S(2)}) collective-permute-start(bf16[256,2048]{1,0:T(8,128)(2,1)} %broadcast_select_fusion.1.refs_0_.refs_4_), channel_id=1, source_target_pairs={{0,2},{1,3},{2,0},{3,1},{4,6},{5,7},{6,4},{7,5},{8,10},{9,11},{10,... | collective-permute-start | bytes 3145736 | tf_op jit(solution)/shard_map/ppermute | solution.py:952
  158.4 48.8 %collective-permute-start.25 = (bf16[256,1024]{1,0:T(8,128)(2,1)}, bf16[256,1024]{1,0:T(8,128)(2,1)}, u32[]{:S(2)}, u32[]{:S(2)}) collective-permute-start(bf16[256,1024]{1,0:T(8,128)(2,1)} %collective-permute-done.24.refs_0_), channel_id=1, source_target_pairs={{4,20},{8,24},{20,4},{24,8},{5,21},{9,25},{21,5},{25,9},{6,22},{10... | collective-permute-start | bytes 1572872 | tf_op jit(solution)/shard_map/ppermute | solution.py:1112
  160.6 54.8 %collective-permute-start.32 = (bf16[1,704,1024]{2,1,0:T(8,128)(2,1)}, bf16[1,704,1024]{2,1,0:T(8,128)(2,1)}, u32[]{:S(2)}, u32[]{:S(2)}) collective-permute-start(bf16[1,704,1024]{2,1,0:T(8,128)(2,1)} %get-tuple-element.264), channel_id=1, source_target_pairs={{0,4},{12,8},{1,5},{13,9},{2,6},{14,10},{3,7},{15,11},{16,20},{28,... | collective-permute-start | bytes 4325384 | tf_op jit(solution)/shard_map/ppermute | solution.py:1102
  171.9 44.0 %collective-permute-start.34 = (bf16[1,704,1024]{2,1,0:T(8,128)(2,1)}, bf16[1,704,1024]{2,1,0:T(8,128)(2,1)}, u32[]{:S(2)}, u32[]{:S(2)}) collective-permute-start(bf16[1,704,1024]{2,1,0:T(8,128)(2,1)} %get-tuple-element.266), channel_id=1, source_target_pairs={{0,4},{12,8},{1,5},{13,9},{2,6},{14,10},{3,7},{15,11},{16,20},{28,... | collective-permute-start | bytes 4325384 | tf_op jit(solution)/shard_map/ppermute | solution.py:1102
  216.6 39.2 %collective-permute-start.35 = (bf16[1,704,1024]{2,1,0:T(8,128)(2,1)}, bf16[1,704,1024]{2,1,0:T(8,128)(2,1)S(1)}, u32[]{:S(2)}, u32[]{:S(2)}) collective-permute-start(bf16[1,704,1024]{2,1,0:T(8,128)(2,1)} %collective-permute-done.34.refs_2_), channel_id=1, source_target_pairs={{4,20},{8,24},{20,4},{24,8},{5,21},{9,25},{21,5},{25,9},{6,22},{10... | collective-permute-start | bytes 4325384 | tf_op jit(solution)/shard_map/ppermute | solution.py:1112
  218.3 57.3 %collective-permute-start.37 = (bf16[256,2048]{1,0:T(8,128)(2,1)S(1)}, bf16[256,2048]{1,0:T(8,128)(2,1)S(1)}, u32[]{:S(2)}, u32[]{:S(2)}) collective-permute-start(bf16[256,2048]{1,0:T(8,128)(2,1)S(1)} %add_convert_fusion.11), channel_id=1, source_target_pairs={{0,2},{1,3},{2,0},{3,1},{4,6},{5,7},{6,4},{7,5},{8,10},{9,11},{10,... | collective-permute-start | bytes 3145736 | tf_op jit(solution)/shard_map/ppermute | solution.py:952
  231.7 55.2 %collective-permute-start.36 = (bf16[256,2048]{1,0:T(8,128)(2,1)S(1)}, bf16[256,2048]{1,0:T(8,128)(2,1)S(1)}, u32[]{:S(2)}, u32[]{:S(2)}) collective-permute-start(bf16[256,2048]{1,0:T(8,128)(2,1)S(1)} %add_convert_fusion.12), channel_id=1, source_target_pairs={{0,3},{1,2},{2,1},{3,0},{4,7},{5,6},{6,5},{7,4},{8,11},{9,10},{10,... | collective-permute-start | bytes 3145736 | tf_op jit(solution)/shard_map/ppermute | solution.py:952
  232.1 42.8 %collective-permute-start.38 = (bf16[256,2048]{1,0:T(8,128)(2,1)S(1)}, bf16[256,2048]{1,0:T(8,128)(2,1)S(1)}, u32[]{:S(2)}, u32[]{:S(2)}) collective-permute-start(bf16[256,2048]{1,0:T(8,128)(2,1)S(1)} %add_convert_fusion.10), channel_id=1, source_target_pairs={{0,1},{1,0},{2,3},{3,2},{4,5},{5,4},{6,7},{7,6},{8,9},{9,8},{10,11... | collective-permute-start | bytes 3145736 | tf_op jit(solution)/shard_map/ppermute | solution.py:952
  233.8 59.4 %collective-permute-start.41 = (bf16[704,1024]{1,0:T(8,128)(2,1)S(1)}, bf16[704,1024]{1,0:T(8,128)(2,1)S(1)}, u32[]{:S(2)}, u32[]{:S(2)}) collective-permute-start(bf16[704,1024]{1,0:T(8,128)(2,1)S(1)} %copy-done.131), channel_id=1, source_target_pairs={{0,4},{12,8},{1,5},{13,9},{2,6},{14,10},{3,7},{15,11},{16,20},{28,... | collective-permute-start | bytes 4325384 | tf_op jit(solution)/shard_map/ppermute | solution.py:1102
  255.8 60.1 %collective-permute-start.40 = (bf16[256,2048]{1,0:T(8,128)(2,1)}, bf16[256,2048]{1,0:T(8,128)(2,1)S(1)}, u32[]{:S(2)}, u32[]{:S(2)}) collective-permute-start(bf16[256,2048]{1,0:T(8,128)(2,1)} %broadcast_select_fusion.1.refs_0_.refs_4_), channel_id=1, source_target_pairs={{0,8},{8,0},{1,9},{9,1},{2,10},{10,2},{3,11},{11,3},{4,12},{12,4},... | collective-permute-start | bytes 3145736 | tf_op jit(solution)/shard_map/ppermute | solution.py:934
  274.9 41.0 %collective-permute-start.43 = (bf16[256,2048]{1,0:T(8,128)(2,1)}, bf16[256,2048]{1,0:T(8,128)(2,1)S(1)}, u32[]{:S(2)}, u32[]{:S(2)}) collective-permute-start(bf16[256,2048]{1,0:T(8,128)(2,1)} %collective-permute-done.26.refs_0_.refs_8_), channel_id=1, source_target_pairs={{0,1},{1,0},{2,3},{3,2},{4,5},{5,4},{6,7},{7,6},{8,9},{9,8},{10,11... | collective-permute-start | bytes 3145736 | tf_op jit(solution)/shard_map/ppermute | solution.py:952
  386.1 38.2 %collective-permute-start.61 = (bf16[256,2048]{1,0:T(8,128)(2,1)}, bf16[256,2048]{1,0:T(8,128)(2,1)}, u32[]{:S(2)}, u32[]{:S(2)}) collective-permute-start(bf16[256,2048]{1,0:T(8,128)(2,1)} %add_convert_fusion.9), channel_id=1, source_target_pairs={{0,1},{1,0},{2,3},{3,2},{4,5},{5,4},{6,7},{7,6},{8,9},{9,8},{10,11... | collective-permute-start | bytes 3145736 | tf_op jit(solution)/shard_map/ppermute | solution.py:952
  390.2 34.1 %collective-permute-start.60 = (bf16[256,2048]{1,0:T(8,128)(2,1)}, bf16[256,2048]{1,0:T(8,128)(2,1)}, u32[]{:S(2)}, u32[]{:S(2)}) collective-permute-start(bf16[256,2048]{1,0:T(8,128)(2,1)} %add_convert_fusion.8), channel_id=1, source_target_pairs={{0,2},{1,3},{2,0},{3,1},{4,6},{5,7},{6,4},{7,5},{8,10},{9,11},{10,... | collective-permute-start | bytes 3145736 | tf_op jit(solution)/shard_map/ppermute | solution.py:952
  394.6 43.9 %collective-permute-start.59 = (bf16[256,2048]{1,0:T(8,128)(2,1)}, bf16[256,2048]{1,0:T(8,128)(2,1)}, u32[]{:S(2)}, u32[]{:S(2)}) collective-permute-start(bf16[256,2048]{1,0:T(8,128)(2,1)} %add_convert_fusion.7), channel_id=1, source_target_pairs={{0,3},{1,2},{2,1},{3,0},{4,7},{5,6},{6,5},{7,4},{8,11},{9,10},{10,... | collective-permute-start | bytes 3145736 | tf_op jit(solution)/shard_map/ppermute | solution.py:952
  495.8 42.4 %collective-permute-start.73 = (bf16[256,2048]{1,0:T(8,128)(2,1)}, bf16[256,2048]{1,0:T(8,128)(2,1)}, u32[]{:S(2)}, u32[]{:S(2)}) collective-permute-start(bf16[256,2048]{1,0:T(8,128)(2,1)} %add_convert_fusion.6), channel_id=1, source_target_pairs={{0,3},{1,2},{2,1},{3,0},{4,7},{5,6},{6,5},{7,4},{8,11},{9,10},{10,... | collective-permute-start | bytes 3145736 | tf_op jit(solution)/shard_map/ppermute | solution.py:952
  496.6 47.7 %collective-permute-start.75 = (bf16[256,2048]{1,0:T(8,128)(2,1)}, bf16[256,2048]{1,0:T(8,128)(2,1)}, u32[]{:S(2)}, u32[]{:S(2)}) collective-permute-start(bf16[256,2048]{1,0:T(8,128)(2,1)} %add_convert_fusion.5), channel_id=1, source_target_pairs={{0,2},{1,3},{2,0},{3,1},{4,6},{5,7},{6,4},{7,5},{8,10},{9,11},{10,... | collective-permute-start | bytes 3145736 | tf_op jit(solution)/shard_map/ppermute | solution.py:952
  498.3 46.4 %collective-permute-start.77 = (bf16[256,2048]{1,0:T(8,128)(2,1)}, bf16[256,2048]{1,0:T(8,128)(2,1)}, u32[]{:S(2)}, u32[]{:S(2)}) collective-permute-start(bf16[256,2048]{1,0:T(8,128)(2,1)} %add_convert_fusion.4), channel_id=1, source_target_pairs={{0,1},{1,0},{2,3},{3,2},{4,5},{5,4},{6,7},{7,6},{8,9},{9,8},{10,11... | collective-permute-start | bytes 3145736 | tf_op jit(solution)/shard_map/ppermute | solution.py:952
  550.0 42.5 %collective-permute-start.78 = (bf16[256,2048]{1,0:T(8,128)(2,1)}, bf16[256,2048]{1,0:T(8,128)(2,1)}, u32[]{:S(2)}, u32[]{:S(2)}) collective-permute-start(bf16[256,2048]{1,0:T(8,128)(2,1)} %add_convert_fusion.3), channel_id=1, source_target_pairs={{4,8},{8,4},{5,9},{9,5},{6,10},{10,6},{7,11},{11,7},{20,24},{24,20... | collective-permute-start | bytes 3145736 | tf_op jit(solution)/shard_map/ppermute | solution.py:955
  557.8 37.1 %collective-permute-start.85 = (bf16[256,2048]{1,0:T(8,128)(2,1)}, bf16[256,2048]{1,0:T(8,128)(2,1)}, u32[]{:S(2)}, u32[]{:S(2)}) collective-permute-start(bf16[256,2048]{1,0:T(8,128)(2,1)} %add_convert_fusion), channel_id=1, source_target_pairs={{0,1},{1,0},{2,3},{3,2},{4,5},{5,4},{6,7},{7,6},{8,9},{9,8},{10,11... | collective-permute-start | bytes 3145736 | tf_op jit(solution)/shard_map/ppermute | solution.py:952
  558.9 37.5 %collective-permute-start.84 = (bf16[256,2048]{1,0:T(8,128)(2,1)}, bf16[256,2048]{1,0:T(8,128)(2,1)}, u32[]{:S(2)}, u32[]{:S(2)}) collective-permute-start(bf16[256,2048]{1,0:T(8,128)(2,1)} %add_convert_fusion.1), channel_id=1, source_target_pairs={{0,2},{1,3},{2,0},{3,1},{4,6},{5,7},{6,4},{7,5},{8,10},{9,11},{10,... | collective-permute-start | bytes 3145736 | tf_op jit(solution)/shard_map/ppermute | solution.py:952
  560.6 57.9 %collective-permute-start.83 = (bf16[256,2048]{1,0:T(8,128)(2,1)}, bf16[256,2048]{1,0:T(8,128)(2,1)}, u32[]{:S(2)}, u32[]{:S(2)}) collective-permute-start(bf16[256,2048]{1,0:T(8,128)(2,1)} %add_convert_fusion.2), channel_id=1, source_target_pairs={{0,3},{1,2},{2,1},{3,0},{4,7},{5,6},{6,5},{7,4},{8,11},{9,10},{10,... | collective-permute-start | bytes 3145736 | tf_op jit(solution)/shard_map/ppermute | solution.py:952
  630.3 45.1 %all-to-all-start = ((bf16[16,17,1280]{2,1,0:T(8,128)(2,1)}), bf16[16,17,1280]{2,1,0:T(8,128)(2,1)S(1)}, u32[]{:S(2)}, u32[]{:S(2)}) async-start(bf16[16,17,1280]{2,1,0:T(8,128)(2,1)} %add_convert_fusion.13), calls=%async_computation | async-start | bytes 1966080 | tf_op jit(solution)/shard_map/all_to_all | solution.py:1383
  (219 other events, 3412.9 us)

commit v4 on v3

--- a/solution.py
+++ b/solution.py
@@ -38,8 +38,7 @@
     return pltpu.CompilerParams(vmem_limit_bytes=mib * 1024 * 1024)
 
 
-def cost(flops, nbytes, trans=0):
-    scale = 10**6
+def cost(flops, nbytes, trans=0, scale=10**6):
     return pl.CostEstimate(
         flops=int(flops) // scale,
         bytes_accessed=int(nbytes) // scale,
@@ -523,7 +522,7 @@
         ],
         compiler_params=params(40),
         cost_estimate=cost(
-            4 * heads * seq * seq * HD, 2 * seq * width * 3, heads * seq * seq // 2
+            4 * heads * seq * seq * HD, 2 * seq * width * 3, heads * seq * seq // 2, 1
         ),
     )(info, *chunks, low)
 
@@ -1184,7 +1183,6 @@
         return sum((from_offset(a, axis, k) for k in range(1, sizes[axis])), a)
 
     one = gather_next(one)
-    column = over_z(squares)
     parts_qkv = fetch_rest(mine_qkv)
     mine_o = fetch(cuts[0], parts_qkv[0])
     moved_cot = swap_rows(after(cotangent, parts_qkv[0]))
@@ -1198,19 +1196,20 @@
     qkv = []
     for o in range(n_chips):
         qkv.append(mark(qkv_chunk(blk, o, one[o], v_qkv, seq(scale_qkv), cos, sin)))
-        if o == 0:
-            squares = add_over(sum(column, seq(squares)), "y")
-    mark(squares)
+        if o == 1:
+            mine_o = mark(seq(mine_o))
+            parts_o = fetch_rest(mine_o)
     local_cot = mark(jnp.where(stay, cotangent, seq(moved_cot)))
     grad_output = local_cot.astype(F32)
-    parts_o = fetch_rest(mine_o)
     rest_gate = fetch_rest(mine_gate)
     down = [[local_cot, mate(local_cot)]] + [[chips(local_cot, o, -1)] for o in offsets[1 : Y + 1]]
     mine_up = fetch(cuts[2], local_cot)
+    column = over_z(squares)
     qkv_abs, att_abs, att_slot, lse = attn_fwd(info, qkv, seq(low), tokens, bq)
     mark(lse)
     for i in range(1, Y + 1):
         down[i] = [mark(seq(down[i][0]))]
+    squares = add_over(mark(sum(column, seq(squares))), "y")
     v_o = mark(merge_rows(flags, base_attn_out, parts_o, seq(at_o), b_o))
     rest_up = fetch_rest(mine_up)
     blocks = product_blocks(

time: 688 us -> 695 us (1.010)
  starting transfers between devices: 156 us -> 175 us
    ppermute x41, starting transfers between devices: 45 us -> 65.7 us  [from_offset(): return lax.ppermute(a, axis, [(s, (s - k) % n) for s in range(n)])]
    ppermute x27, waiting for transfers between devices: 135 us -> 152 us  [chips(): return lax.ppermute(a, ('zl', 'y'), perm)]
    ppermute x6, waiting for transfers between devices: 14.6 us -> 0.02 us  [over_z(): found.append(lax.ppermute(a, ('zh', 'zl'), perm))]
    unnamed x327 -> x319, local copies, waits for them, and re-layouts: 24.8 us -> 18.7 us
  transfers between devices with their start and end apart: 89 -> 89, of which waited for: 25 -> 28; matrix products, arithmetic and copies ran while one was open for 11% -> 11% of each run, Pallas kernels for 28% -> 28%
where the time goes in v4:
time: 695 us; the launch traced here: 685 us
  waiting for transfers between devices  212 us (31%)
  Pallas kernels  193 us (28%)
  starting transfers between devices  175 us (25%)
  other arithmetic  61.6 us (9%)
  local copies, waits for them, and re-layouts  35 us (5%)
    ppermute x27, waiting for transfers between devices, chips(): return lax.ppermute(a, ('zl', 'y'), perm)  152 us
    ppermute x41, starting transfers between devices, from_offset(): return lax.ppermute(a, axis, [(s, (s - k) % n) for s in range(n)])  65.7 us
    ppermute x27, starting transfers between devices, chips(): return lax.ppermute(a, ('zl', 'y'), perm)  46.6 us
    all_to_all x1, waiting for transfers between devices, on_device(): lax.all_to_all(grads.astype(BF16), ('x', 'zh', 'zl', 'y'), split_axis=0,...  37.3 us
    ppermute x5, starting transfers between devices, fetch(): return lax.ppermute(mine, ('c', 'zh'), [(0, 1), (3, 2)])  37.2 us
    pallas_call x4, Pallas kernels, mlp_chunk(): pl.pallas_call(functools.partial(mlp_kernel, rows), in_specs=[VM] * (len(...  35.6 us
    pallas_call x4, Pallas kernels, rank_grads(): pl.pallas_call(functools.partial(rank_kernel, len(xs), len(ds), groups, t...  35.4 us
    pallas_call x16, Pallas kernels, product(): pl.pallas_call(functools.partial(product_kernel, len(xs), turned, tuple(s...  28.4 us
  transfers between devices with their start and end apart: 89, of which 28 were waited for; matrix products, arithmetic and copies ran while one was open for 11% of the time, Pallas kernels for 28%

profile of v4, /device:TPU:0, one launch (start us, length us, event | category | flops | bytes accessed | tf_op | source)
XLA Modules:
  0.0 685.3 jit_solution(8437424031605387373)
XLA Ops:
  35.7 7.8 %collective-permute-done.5 = bf16[8,17,1280]{2,1,0:T(8,128)(2,1)S(1)} collective-permute-done((bf16[8,17,1280]{2,1,0:T(8,128)(2,1)}, bf16[8,17,1280]{2,1,0:T(8,128)(2,1)S(1)}, u32[]{:S(2)}, u32[]{:S(2)}) %collective-permute-start.5) | collective-permute-done | bytes 348192 | tf_op jit(solution)/shard_map/ppermute | solution.py:933
  66.3 13.4 %collective-permute-start.8 = (bf16[256,2048]{1,0:T(8,128)(2,1)S(1)}, bf16[256,2048]{1,0:T(8,128)(2,1)S(1)}, u32[]{:S(2)}, u32[]{:S(2)}) collective-permute-start(bf16[256,2048]{1,0:T(8,128)(2,1)S(1)} %fusion.5.refs_0_), channel_id=1, source_target_pairs={{0,8},{8,0},{1,9},{9,1},{2,10},{10,2},{3,11},{11,3},{4,12},{12,4},... | collective-permute-start | bytes 3145736 | tf_op jit(solution)/shard_map/ppermute | solution.py:933
  81.2 11.5 %collective-permute-done.13.refs_0_.refs_4_ = bf16[256,2048]{1,0:T(8,128)(2,1)} collective-permute-done((bf16[256,2048]{1,0:T(8,128)(2,1)S(1)}, bf16[256,2048]{1,0:T(8,128)(2,1)}, u32[]{:S(2)}, u32[]{:S(2)}) %collective-permute-start.13) | collective-permute-done | bytes 1048608 | tf_op jit(solution)/shard_map/ppermute | solution.py:951
  95.4 8.5 %collective-permute-done.17.refs_1_.refs_7_ = bf16[128,2048]{1,0:T(8,128)(2,1)S(1)} collective-permute-done((bf16[128,2048]{1,0:T(8,128)(2,1)S(1)}, bf16[128,2048]{1,0:T(8,128)(2,1)S(1)}, u32[]{:S(2)}, u32[]{:S(2)}) %collective-permute-start.17) | collective-permute-done | bytes 524320 | tf_op jit(solution)/shard_map/ppermute | solution.py:951
  140.4 12.9 %collective-permute-start.22 = (bf16[256,2048]{1,0:T(8,128)(2,1)}, bf16[256,2048]{1,0:T(8,128)(2,1)}, u32[]{:S(2)}, u32[]{:S(2)}) collective-permute-start(bf16[256,2048]{1,0:T(8,128)(2,1)} %broadcast_select_fusion.1.refs_0_.refs_4_), channel_id=1, source_target_pairs={{0,2},{1,3},{2,0},{3,1},{4,6},{5,7},{6,4},{7,5},{8,10},{9,11},{10,... | collective-permute-start | bytes 3145736 | tf_op jit(solution)/shard_map/ppermute | solution.py:951
  159.1 12.0 %collective-permute-start.31 = (bf16[1,704,1024]{2,1,0:T(8,128)(2,1)}, bf16[1,704,1024]{2,1,0:T(8,128)(2,1)S(1)}, u32[]{:S(2)}, u32[]{:S(2)}) collective-permute-start(bf16[1,704,1024]{2,1,0:T(8,128)(2,1)} %get-tuple-element.266), channel_id=1, source_target_pairs={{0,4},{12,8},{1,5},{13,9},{2,6},{14,10},{3,7},{15,11},{16,20},{28,... | collective-permute-start | bytes 4325384 | tf_op jit(solution)/shard_map/ppermute | solution.py:1101
  182.0 15.1 %shard_map.299 = (bf16[2048,768]{1,0:T(8,128)(2,1)S(1)}, bf16[2048,256]{1,0:T(8,128)(2,1)S(1)}, bf16[2048,256]{1,0:T(8,128)(2,1)S(1)}, f32[2,1,2048]{2,1,0:T(1,128)S(1)}) custom-call(s32[13]{0:T(128)S(1)} %pad_add_fusion.1.info, bf16[512,768]{1,0:T(8,128)(2,1)S(1)} %copy-done.74, bf16[512,768]{1,0:T(8,128)(2,1)S(1)} %copy-done.76, ...), custom_call_target="tpu_custom_call" | custom-call | flops 4294967296 | bytes 9437184 | tf_op jit(solution)/shard_map/pallas_call | solution.py:498
  198.0 10.5 %collective-permute-start.33 = (bf16[1,704,1024]{2,1,0:T(8,128)(2,1)S(1)}, bf16[1,704,1024]{2,1,0:T(8,128)(2,1)S(1)}, u32[]{:S(2)}, u32[]{:S(2)}) collective-permute-start(bf16[1,704,1024]{2,1,0:T(8,128)(2,1)S(1)} %copy-done.127), channel_id=1, source_target_pairs={{0,4},{12,8},{1,5},{13,9},{2,6},{14,10},{3,7},{15,11},{16,20},{28,... | collective-permute-start | bytes 4325384 | tf_op jit(solution)/shard_map/ppermute | solution.py:1101
  217.6 7.2 %collective-permute-done.33.refs_2_ = bf16[1,704,1024]{2,1,0:T(8,128)(2,1)S(1)} collective-permute-done((bf16[1,704,1024]{2,1,0:T(8,128)(2,1)S(1)}, bf16[1,704,1024]{2,1,0:T(8,128)(2,1)S(1)}, u32[]{:S(2)}, u32[]{:S(2)}) %collective-permute-start.33) | collective-permute-done | bytes 1441824 | tf_op jit(solution)/shard_map/ppermute | solution.py:1101
  224.8 15.7 %collective-permute-start.30 = (bf16[256,2048]{1,0:T(8,128)(2,1)S(1)}, bf16[256,2048]{1,0:T(8,128)(2,1)S(1)}, u32[]{:S(2)}, u32[]{:S(2)}) collective-permute-start(bf16[256,2048]{1,0:T(8,128)(2,1)S(1)} %get-tuple-element.264), channel_id=1, source_target_pairs={{0,8},{8,0},{1,9},{9,1},{2,10},{10,2},{3,11},{11,3},{4,12},{12,4},... | collective-permute-start | bytes 3145736 | tf_op jit(solution)/shard_map/ppermute | solution.py:933
  246.2 6.4 collective-permute-start.41
  253.0 7.6 %collective-permute-start.40 = (bf16[256,2048]{1,0:T(8,128)(2,1)}, bf16[256,2048]{1,0:T(8,128)(2,1)S(1)}, u32[]{:S(2)}, u32[]{:S(2)}) collective-permute-start(bf16[256,2048]{1,0:T(8,128)(2,1)} %broadcast_select_fusion.1.refs_0_.refs_4_), channel_id=1, source_target_pairs={{0,8},{8,0},{1,9},{9,1},{2,10},{10,2},{3,11},{11,3},{4,12},{12,4},... | collective-permute-start | bytes 3145736 | tf_op jit(solution)/shard_map/ppermute | solution.py:933
  260.6 6.3 shard_map.305
  272.1 11.2 %collective-permute-done.36 = bf16[256,2048]{1,0:T(8,128)(2,1)S(1)} collective-permute-done((bf16[256,2048]{1,0:T(8,128)(2,1)S(1)}, bf16[256,2048]{1,0:T(8,128)(2,1)S(1)}, u32[]{:S(2)}, u32[]{:S(2)}) %collective-permute-start.36) | collective-permute-done | bytes 1048608 | tf_op jit(solution)/shard_map/ppermute | solution.py:951
  283.3 20.6 %collective-permute-done.35 = bf16[256,2048]{1,0:T(8,128)(2,1)S(1)} collective-permute-done((bf16[256,2048]{1,0:T(8,128)(2,1)S(1)}, bf16[256,2048]{1,0:T(8,128)(2,1)S(1)}, u32[]{:S(2)}, u32[]{:S(2)}) %collective-permute-start.35) | collective-permute-done | bytes 1048608 | tf_op jit(solution)/shard_map/ppermute | solution.py:951
  310.9 7.1 %collective-permute-done.43.refs_0_.refs_10_ = bf16[256,2048]{1,0:T(8,128)(2,1)S(1)} collective-permute-done((bf16[256,2048]{1,0:T(8,128)(2,1)}, bf16[256,2048]{1,0:T(8,128)(2,1)S(1)}, u32[]{:S(2)}, u32[]{:S(2)}) %collective-permute-start.43) | collective-permute-done | bytes 1048608 | tf_op jit(solution)/shard_map/ppermute | solution.py:951
  327.6 7.2 %collective-permute-start.39 = (bf16[256,2048]{1,0:T(8,128)(2,1)S(1)}, bf16[256,2048]{1,0:T(8,128)(2,1)S(1)}, u32[]{:S(2)}, u32[]{:S(2)}) collective-permute-start(bf16[256,2048]{1,0:T(8,128)(2,1)S(1)} %multiply_convert_fusion.1.refs_0_), channel_id=1, source_target_pairs={{0,8},{8,0},{1,9},{9,1},{2,10},{10,2},{3,11},{11,3},{4,12},{12,4},... | collective-permute-start | bytes 3145736 | tf_op jit(solution)/shard_map/ppermute | solution.py:933
  347.7 7.8 %shard_map.311 = (bf16[512,704]{1,0:T(8,128)(2,1)S(1)}, bf16[2,512,704]{2,1,0:T(8,128)(2,1)S(1)}, bf16[256,2048]{1,0:T(8,128)(2,1)S(1)}, bf16[256,2048]{1,0:T(8,128)(2,1)S(1)}, f32[2,1,704]{2,1,0:T(1,128)S(1)}) custom-call(bf16[256,2048]{1,0:T(8,128)(2,1)S(1)} %multiply_convert_fusion.1.refs_0_, bf16[256,2048]{1,0:T(8,128)(2,1)S(1)} %collective-permute-done.39.refs_1_, ...), custom_call_target="tpu_custom_call" | custom-call | flops 5905 | bytes 9 | tf_op jit(solution)/shard_map/pallas_call | solution.py:698
  355.5 7.6 %shard_map.312 = (bf16[512,704]{1,0:T(8,128)(2,1)S(1)}, bf16[2,512,704]{2,1,0:T(8,128)(2,1)S(1)}, bf16[256,2048]{1,0:T(8,128)(2,1)S(1)}, bf16[256,2048]{1,0:T(8,128)(2,1)S(1)}, f32[2,1,704]{2,1,0:T(1,128)S(1)}) custom-call(bf16[256,2048]{1,0:T(8,128)(2,1)S(1)} %collective-permute-done.50.refs_0_.refs_2_, ...), custom_call_target="tpu_custom_call" | custom-call | flops 5905 | bytes 9 | tf_op jit(solution)/shard_map/pallas_call | solution.py:698
  363.2 9.0 %shard_map.313 = (bf16[512,704]{1,0:T(8,128)(2,1)S(1)}, bf16[2,512,704]{2,1,0:T(8,128)(2,1)S(1)}, bf16[256,2048]{1,0:T(8,128)(2,1)S(1)}, bf16[256,2048]{1,0:T(8,128)(2,1)}, f32[2,1,704]{2,1,0:T(1,128)S(1)}) custom-call(bf16[256,2048]{1,0:T(8,128)(2,1)S(1)} %collective-permute-done.47.refs_0_.refs_4_, ...), custom_call_target="tpu_custom_call" | custom-call | flops 5905 | bytes 9 | tf_op jit(solution)/shard_map/pallas_call | solution.py:698
  376.5 11.2 %shard_map.314 = (bf16[512,704]{1,0:T(8,128)(2,1)S(1)}, bf16[2,512,704]{2,1,0:T(8,128)(2,1)S(1)}, bf16[256,2048]{1,0:T(8,128)(2,1)S(1)}, bf16[256,2048]{1,0:T(8,128)(2,1)S(1)}, f32[2,1,704]{2,1,0:T(1,128)S(1)}) custom-call(bf16[128,2048]{1,0:T(8,128)(2,1)S(1)} %collective-permute-done.48.refs_0_.refs_6_, ...), custom_call_target="tpu_custom_call" | custom-call | flops 5905 | bytes 9 | tf_op jit(solution)/shard_map/pallas_call | solution.py:698
  416.5 11.1 %shard_map.319 = (f32[32,2048]{1,0:T(8,128)S(1)}, f32[32,704]{1,0:T(8,128)S(1)}) custom-call(bf16[256,2048]{1,0:T(8,128)(2,1)S(1)} %multiply_convert_fusion.1.refs_0_, bf16[256,2048]{1,0:T(8,128)(2,1)S(1)} %collective-permute-done.39.refs_1_, bf16[256,2048]{1,0:T(8,128)(2,1)S(1)} %collective-permute-done.50.refs_0_.refs_2_, ...), custom_call_target="tpu_custom_call" | custom-call | flops 7247 | bytes 19 | tf_op jit(solution)/shard_map/pallas_call | solution.py:765
  427.7 15.1 %collective-permute-done.59 = bf16[256,2048]{1,0:T(8,128)(2,1)} collective-permute-done((bf16[256,2048]{1,0:T(8,128)(2,1)S(1)}, bf16[256,2048]{1,0:T(8,128)(2,1)}, u32[]{:S(2)}, u32[]{:S(2)}) %collective-permute-start.59) | collective-permute-done | bytes 1048608 | tf_op jit(solution)/shard_map/ppermute | solution.py:951
  455.3 21.9 %collective-permute-done.65.refs_0_.refs_3_ = bf16[272,2048]{1,0:T(8,128)(2,1)S(1)} collective-permute-done((bf16[272,2048]{1,0:T(8,128)(2,1)S(1)}, bf16[272,2048]{1,0:T(8,128)(2,1)S(1)}, u32[]{:S(2)}, u32[]{:S(2)}) %collective-permute-start.65) | collective-permute-done | bytes 1114144 | tf_op jit(solution)/shard_map/ppermute | solution.py:951
  484.0 10.2 %collective-permute-done.70.refs_1_.refs_8_ = bf16[144,2048]{1,0:T(8,128)(2,1)S(1)} collective-permute-done((bf16[144,2048]{1,0:T(8,128)(2,1)S(1)}, bf16[144,2048]{1,0:T(8,128)(2,1)S(1)}, u32[]{:S(2)}, u32[]{:S(2)}) %collective-permute-start.70) | collective-permute-done | bytes 589856 | tf_op jit(solution)/shard_map/ppermute | solution.py:951
  508.0 25.4 %shard_map.324 = (bf16[2048,768]{1,0:T(8,128)(2,1)S(1)}, f32[1,768]{1,0:T(1,128)S(1)}) custom-call(s32[13]{0:T(128)S(1)} %pad_add_fusion.1.info, bf16[2048,768]{1,0:T(8,128)(2,1)} %copy-done.42, bf16[512,256]{1,0:T(8,128)(2,1)S(1)} %shard_map.320.refs_0_, bf16[512,256]{1,0:T(8,128)(2,1)S(1)} %shard_map.321.refs_1_, bf16[512,256]{1,0:T(8,128)(2,1)S(1)} %shard_map.322.refs_2_, ...), custom_call_target="tpu_custom_call" | custom-call | flops 10737 | bytes 12 | tf_op jit(solution)/shard_map/pallas_call | solution.py:634
  542.2 6.2 collective-permute-done.75
  570.6 9.0 %shard_map.329 = (f32[48,2048]{1,0:T(8,128)S(1)}, f32[48,768]{1,0:T(8,128)S(1)}) custom-call(bf16[256,2048]{1,0:T(8,128)(2,1)S(1)} %copy-done.8, bf16[256,2048]{1,0:T(8,128)(2,1)S(1)} %copy-done.37, bf16[256,2048]{1,0:T(8,128)(2,1)S(1)} %copy-done.27, bf16[256,2048]{1,0:T(8,128)(2,1)S(1)} %copy-done.39, ...), custom_call_target="tpu_custom_call" | custom-call | flops 5905 | bytes 14 | tf_op jit(solution)/shard_map/pallas_call | solution.py:765
  579.9 5.6 shard_map.330
  585.6 9.7 %shard_map.331 = (f32[16,704]{1,0:T(8,128)S(1)}, f32[16,2048]{1,0:T(8,128)S(1)}) custom-call(bf16[512,704]{1,0:T(8,128)(2,1)S(1)} %copy-done.44, bf16[512,704]{1,0:T(8,128)(2,1)S(1)} %copy-done.46, bf16[512,704]{1,0:T(8,128)(2,1)S(1)} %copy-done.48, bf16[512,704]{1,0:T(8,128)(2,1)S(1)} %copy-done.50, ...), custom_call_target="tpu_custom_call" | custom-call | flops 5771 | bytes 14 | tf_op jit(solution)/shard_map/pallas_call | solution.py:765
  603.5 22.2 %collective-permute-done.83 = bf16[256,2048]{1,0:T(8,128)(2,1)} collective-permute-done((bf16[256,2048]{1,0:T(8,128)(2,1)}, bf16[256,2048]{1,0:T(8,128)(2,1)}, u32[]{:S(2)}, u32[]{:S(2)}) %collective-permute-start.83) | collective-permute-done | bytes 1048608 | tf_op jit(solution)/shard_map/ppermute | solution.py:951
  645.3 37.3 %all-to-all-done = bf16[16,17,1280]{2,1,0:T(8,128)(2,1)S(1)} async-done(((bf16[16,17,1280]{2,1,0:T(8,128)(2,1)}), bf16[16,17,1280]{2,1,0:T(8,128)(2,1)S(1)}, u32[]{:S(2)}, u32[]{:S(2)}) %all-to-all-start) | async-done | bytes 696352 | tf_op jit(solution)/shard_map/all_to_all | solution.py:1382
  (608 shorter events, 290.9 us)
Async XLA Ops:
  7.8 41.5 %collective-permute-start = (bf16[256,2048]{1,0:T(8,128)(2,1)}, bf16[256,2048]{1,0:T(8,128)(2,1)}, u32[]{:S(2)}, u32[]{:S(2)}) collective-permute-start(bf16[256,2048]{1,0:T(8,128)(2,1)} %param.21), channel_id=1, source_target_pairs={{4,8},{8,4},{5,9},{9,5},{6,10},{10,6},{7,11},{11,7},{20,24},{24,20... | collective-permute-start | bytes 3145736 | tf_op jit(solution)/shard_map/ppermute | solution.py:954
  22.8 42.6 %collective-permute-start.9 = (bf16[3,1024,256]{2,1,0:T(8,128)(2,1)}, bf16[3,1024,256]{2,1,0:T(8,128)(2,1)}, u32[]{:S(2)}, u32[]{:S(2)}) collective-permute-start(bf16[3,1024,256]{2,1,0:T(8,128)(2,1)} %constant_dynamic-slice_fusion.2), channel_id=1, source_target_pairs={{0,4},{12,8},{1,5},{13,9},{2,6},{14,10},{3,7},{15,11},{16,20},{28,... | collective-permute-start | bytes 4718600 | tf_op jit(solution)/shard_map/ppermute | solution.py:1101
  50.2 29.5 %collective-permute-start.11 = (bf16[256,2048]{1,0:T(8,128)(2,1)S(1)}, bf16[256,2048]{1,0:T(8,128)(2,1)S(1)}, u32[]{:S(2)}, u32[]{:S(2)}) collective-permute-start(bf16[256,2048]{1,0:T(8,128)(2,1)S(1)} %fusion.5.refs_0_), channel_id=1, source_target_pairs={{0,1},{1,0},{2,3},{3,2},{4,5},{5,4},{6,7},{7,6},{8,9},{9,8},{10,11... | collective-permute-start | bytes 3145736 | tf_op jit(solution)/shard_map/ppermute | solution.py:951
  51.8 40.9 %collective-permute-start.13 = (bf16[256,2048]{1,0:T(8,128)(2,1)S(1)}, bf16[256,2048]{1,0:T(8,128)(2,1)}, u32[]{:S(2)}, u32[]{:S(2)}) collective-permute-start(bf16[256,2048]{1,0:T(8,128)(2,1)S(1)} %fusion.5.refs_0_), channel_id=1, source_target_pairs={{0,2},{1,3},{2,0},{3,1},{4,6},{5,7},{6,4},{7,5},{8,10},{9,11},{10,... | collective-permute-start | bytes 3145736 | tf_op jit(solution)/shard_map/ppermute | solution.py:951
  65.4 48.5 %collective-permute-start.10 = (bf16[3,1024,256]{2,1,0:T(8,128)(2,1)}, bf16[3,1024,256]{2,1,0:T(8,128)(2,1)S(1)}, u32[]{:S(2)}, u32[]{:S(2)}) collective-permute-start(bf16[3,1024,256]{2,1,0:T(8,128)(2,1)} %collective-permute-done.9.refs_0_), channel_id=1, source_target_pairs={{4,20},{8,24},{20,4},{24,8},{5,21},{9,25},{21,5},{25,9},{6,22},{10... | collective-permute-start | bytes 4718600 | tf_op jit(solution)/shard_map/ppermute | solution.py:1111
  66.3 42.3 %collective-permute-start.8 = (bf16[256,2048]{1,0:T(8,128)(2,1)S(1)}, bf16[256,2048]{1,0:T(8,128)(2,1)S(1)}, u32[]{:S(2)}, u32[]{:S(2)}) collective-permute-start(bf16[256,2048]{1,0:T(8,128)(2,1)S(1)} %fusion.5.refs_0_), channel_id=1, source_target_pairs={{0,8},{8,0},{1,9},{9,1},{2,10},{10,2},{3,11},{11,3},{4,12},{12,4},... | collective-permute-start | bytes 3145736 | tf_op jit(solution)/shard_map/ppermute | solution.py:933
  79.7 34.2 %collective-permute-start.12 = (bf16[256,2048]{1,0:T(8,128)(2,1)S(1)}, bf16[256,2048]{1,0:T(8,128)(2,1)S(1)}, u32[]{:S(2)}, u32[]{:S(2)}) collective-permute-start(bf16[256,2048]{1,0:T(8,128)(2,1)S(1)} %collective-permute-done.11.refs_0_.refs_2_), channel_id=1, source_target_pairs={{0,8},{8,0},{1,9},{9,1},{2,10},{10,2},{3,11},{11,3},{4,12},{12,4},... | collective-permute-start | bytes 3145736 | tf_op jit(solution)/shard_map/ppermute | solution.py:933
  107.9 30.0 %collective-permute-start.20 = (bf16[256,2048]{1,0:T(8,128)(2,1)S(1)}, bf16[256,2048]{1,0:T(8,128)(2,1)S(1)}, u32[]{:S(2)}, u32[]{:S(2)}) collective-permute-start(bf16[256,2048]{1,0:T(8,128)(2,1)S(1)} %copy-done.129), channel_id=1, source_target_pairs={{4,8},{8,4},{5,9},{9,5},{6,10},{10,6},{7,11},{11,7},{20,24},{24,20... | collective-permute-start | bytes 3145736 | tf_op jit(solution)/shard_map/ppermute | solution.py:954
  140.4 36.3 %collective-permute-start.22 = (bf16[256,2048]{1,0:T(8,128)(2,1)}, bf16[256,2048]{1,0:T(8,128)(2,1)}, u32[]{:S(2)}, u32[]{:S(2)}) collective-permute-start(bf16[256,2048]{1,0:T(8,128)(2,1)} %broadcast_select_fusion.1.refs_0_.refs_4_), channel_id=1, source_target_pairs={{0,2},{1,3},{2,0},{3,1},{4,6},{5,7},{6,4},{7,5},{8,10},{9,11},{10,... | collective-permute-start | bytes 3145736 | tf_op jit(solution)/shard_map/ppermute | solution.py:951
  154.2 43.8 %collective-permute-start.24 = (f32[2,2048]{1,0:T(2,128)S(1)}, f32[2,2048]{1,0:T(2,128)S(1)}, u32[]{:S(2)}, u32[]{:S(2)}) collective-permute-start(f32[2,2048]{1,0:T(2,128)S(1)} %pad_maximum_fusion.1), channel_id=1, source_target_pairs={{0,4},{2,6},{4,0},{6,2},{1,5},{3,7},{5,1},{7,3},{8,12},{10,14},{12... | collective-permute-start | bytes 49160 | tf_op jit(solution)/shard_map/ppermute | solution.py:1078
  157.5 51.0 %collective-permute-start.25 = (f32[2,2048]{1,0:T(2,128)S(1)}, f32[2,2048]{1,0:T(2,128)S(1)}, u32[]{:S(2)}, u32[]{:S(2)}) collective-permute-start(f32[2,2048]{1,0:T(2,128)S(1)} %pad_maximum_fusion.1), channel_id=1, source_target_pairs={{0,2},{2,0},{4,6},{6,4},{1,3},{3,1},{5,7},{7,5},{8,10},{10,8},{12,... | collective-permute-start | bytes 49160 | tf_op jit(solution)/shard_map/ppermute | solution.py:1078
  157.6 51.0 %collective-permute-start.26 = (f32[2,2048]{1,0:T(2,128)S(1)}, f32[2,2048]{1,0:T(2,128)S(1)}, u32[]{:S(2)}, u32[]{:S(2)}) collective-permute-start(f32[2,2048]{1,0:T(2,128)S(1)} %pad_maximum_fusion.1), channel_id=1, source_target_pairs={{0,6},{2,4},{4,2},{6,0},{1,7},{3,5},{5,3},{7,1},{8,14},{10,12},{12... | collective-permute-start | bytes 49160 | tf_op jit(solution)/shard_map/ppermute | solution.py:1078
  159.1 53.9 %collective-permute-start.31 = (bf16[1,704,1024]{2,1,0:T(8,128)(2,1)}, bf16[1,704,1024]{2,1,0:T(8,128)(2,1)S(1)}, u32[]{:S(2)}, u32[]{:S(2)}) collective-permute-start(bf16[1,704,1024]{2,1,0:T(8,128)(2,1)} %get-tuple-element.266), channel_id=1, source_target_pairs={{0,4},{12,8},{1,5},{13,9},{2,6},{14,10},{3,7},{15,11},{16,20},{28,... | collective-permute-start | bytes 4325384 | tf_op jit(solution)/shard_map/ppermute | solution.py:1101
  176.7 31.9 %collective-permute-start.21 = (bf16[256,1024]{1,0:T(8,128)(2,1)}, bf16[256,1024]{1,0:T(8,128)(2,1)S(1)}, u32[]{:S(2)}, u32[]{:S(2)}) collective-permute-start(bf16[256,1024]{1,0:T(8,128)(2,1)} %copy-done.82), channel_id=1, source_target_pairs={{4,20},{8,24},{20,4},{24,8},{5,21},{9,25},{21,5},{25,9},{6,22},{10... | collective-permute-start | bytes 1572872 | tf_op jit(solution)/shard_map/ppermute | solution.py:1111
  211.2 29.3 %collective-permute-start.27 = (bf16[256,2048]{1,0:T(8,128)(2,1)S(1)}, bf16[256,2048]{1,0:T(8,128)(2,1)S(1)}, u32[]{:S(2)}, u32[]{:S(2)}) collective-permute-start(bf16[256,2048]{1,0:T(8,128)(2,1)S(1)} %get-tuple-element.258), channel_id=1, source_target_pairs={{0,8},{8,0},{1,9},{9,1},{2,10},{10,2},{3,11},{11,3},{4,12},{12,4},... | collective-permute-start | bytes 3145736 | tf_op jit(solution)/shard_map/ppermute | solution.py:933
  213.0 33.2 %collective-permute-start.32 = (bf16[1,704,1024]{2,1,0:T(8,128)(2,1)S(1)}, bf16[1,704,1024]{2,1,0:T(8,128)(2,1)S(1)}, u32[]{:S(2)}, u32[]{:S(2)}) collective-permute-start(bf16[1,704,1024]{2,1,0:T(8,128)(2,1)S(1)} %collective-permute-done.31.refs_0_), channel_id=1, source_target_pairs={{4,20},{8,24},{20,4},{24,8},{5,21},{9,25},{21,5},{25,9},{6,22},{10... | collective-permute-start | bytes 4325384 | tf_op jit(solution)/shard_map/ppermute | solution.py:1111
  242.1 41.2 %collective-permute-start.36 = (bf16[256,2048]{1,0:T(8,128)(2,1)S(1)}, bf16[256,2048]{1,0:T(8,128)(2,1)S(1)}, u32[]{:S(2)}, u32[]{:S(2)}) collective-permute-start(bf16[256,2048]{1,0:T(8,128)(2,1)S(1)} %add_convert_fusion.11), channel_id=1, source_target_pairs={{0,2},{1,3},{2,0},{3,1},{4,6},{5,7},{6,4},{7,5},{8,10},{9,11},{10,... | collective-permute-start | bytes 3145736 | tf_op jit(solution)/shard_map/ppermute | solution.py:951
  243.3 60.5 %collective-permute-start.35 = (bf16[256,2048]{1,0:T(8,128)(2,1)S(1)}, bf16[256,2048]{1,0:T(8,128)(2,1)S(1)}, u32[]{:S(2)}, u32[]{:S(2)}) collective-permute-start(bf16[256,2048]{1,0:T(8,128)(2,1)S(1)} %add_convert_fusion.12), channel_id=1, source_target_pairs={{0,3},{1,2},{2,1},{3,0},{4,7},{5,6},{6,5},{7,4},{8,11},{9,10},{10,... | collective-permute-start | bytes 3145736 | tf_op jit(solution)/shard_map/ppermute | solution.py:951
  246.2 60.0 %collective-permute-start.41 = (bf16[704,1024]{1,0:T(8,128)(2,1)S(1)}, bf16[704,1024]{1,0:T(8,128)(2,1)S(1)}, u32[]{:S(2)}, u32[]{:S(2)}) collective-permute-start(bf16[704,1024]{1,0:T(8,128)(2,1)S(1)} %copy-done.126), channel_id=1, source_target_pairs={{0,4},{12,8},{1,5},{13,9},{2,6},{14,10},{3,7},{15,11},{16,20},{28,... | collective-permute-start | bytes 4325384 | tf_op jit(solution)/shard_map/ppermute | solution.py:1101
  253.0 65.1 %collective-permute-start.40 = (bf16[256,2048]{1,0:T(8,128)(2,1)}, bf16[256,2048]{1,0:T(8,128)(2,1)S(1)}, u32[]{:S(2)}, u32[]{:S(2)}) collective-permute-start(bf16[256,2048]{1,0:T(8,128)(2,1)} %broadcast_select_fusion.1.refs_0_.refs_4_), channel_id=1, source_target_pairs={{0,8},{8,0},{1,9},{9,1},{2,10},{10,2},{3,11},{11,3},{4,12},{12,4},... | collective-permute-start | bytes 3145736 | tf_op jit(solution)/shard_map/ppermute | solution.py:933
  269.7 48.3 %collective-permute-start.43 = (bf16[256,2048]{1,0:T(8,128)(2,1)}, bf16[256,2048]{1,0:T(8,128)(2,1)S(1)}, u32[]{:S(2)}, u32[]{:S(2)}) collective-permute-start(bf16[256,2048]{1,0:T(8,128)(2,1)} %collective-permute-done.22.refs_0_.refs_8_), channel_id=1, source_target_pairs={{0,1},{1,0},{2,3},{3,2},{4,5},{5,4},{6,7},{7,6},{8,9},{9,8},{10,11... | collective-permute-start | bytes 3145736 | tf_op jit(solution)/shard_map/ppermute | solution.py:951
  390.8 36.9 %collective-permute-start.61 = (bf16[256,2048]{1,0:T(8,128)(2,1)}, bf16[256,2048]{1,0:T(8,128)(2,1)}, u32[]{:S(2)}, u32[]{:S(2)}) collective-permute-start(bf16[256,2048]{1,0:T(8,128)(2,1)} %add_convert_fusion.9), channel_id=1, source_target_pairs={{0,1},{1,0},{2,3},{3,2},{4,5},{5,4},{6,7},{7,6},{8,9},{9,8},{10,11... | collective-permute-start | bytes 3145736 | tf_op jit(solution)/shard_map/ppermute | solution.py:951
  394.9 32.8 %collective-permute-start.60 = (bf16[256,2048]{1,0:T(8,128)(2,1)}, bf16[256,2048]{1,0:T(8,128)(2,1)}, u32[]{:S(2)}, u32[]{:S(2)}) collective-permute-start(bf16[256,2048]{1,0:T(8,128)(2,1)} %add_convert_fusion.8), channel_id=1, source_target_pairs={{0,2},{1,3},{2,0},{3,1},{4,6},{5,7},{6,4},{7,5},{8,10},{9,11},{10,... | collective-permute-start | bytes 3145736 | tf_op jit(solution)/shard_map/ppermute | solution.py:951
  397.5 45.3 %collective-permute-start.59 = (bf16[256,2048]{1,0:T(8,128)(2,1)S(1)}, bf16[256,2048]{1,0:T(8,128)(2,1)}, u32[]{:S(2)}, u32[]{:S(2)}) collective-permute-start(bf16[256,2048]{1,0:T(8,128)(2,1)S(1)} %add_convert_fusion.7), channel_id=1, source_target_pairs={{0,3},{1,2},{2,1},{3,0},{4,7},{5,6},{6,5},{7,4},{8,11},{9,10},{10,... | collective-permute-start | bytes 3145736 | tf_op jit(solution)/shard_map/ppermute | solution.py:951
  500.5 41.7 %collective-permute-start.73 = (bf16[256,2048]{1,0:T(8,128)(2,1)}, bf16[256,2048]{1,0:T(8,128)(2,1)}, u32[]{:S(2)}, u32[]{:S(2)}) collective-permute-start(bf16[256,2048]{1,0:T(8,128)(2,1)} %add_convert_fusion.6), channel_id=1, source_target_pairs={{0,3},{1,2},{2,1},{3,0},{4,7},{5,6},{6,5},{7,4},{8,11},{9,10},{10,... | collective-permute-start | bytes 3145736 | tf_op jit(solution)/shard_map/ppermute | solution.py:951
  501.8 46.6 %collective-permute-start.75 = (bf16[256,2048]{1,0:T(8,128)(2,1)}, bf16[256,2048]{1,0:T(8,128)(2,1)}, u32[]{:S(2)}, u32[]{:S(2)}) collective-permute-start(bf16[256,2048]{1,0:T(8,128)(2,1)} %add_convert_fusion.5), channel_id=1, source_target_pairs={{0,2},{1,3},{2,0},{3,1},{4,6},{5,7},{6,4},{7,5},{8,10},{9,11},{10,... | collective-permute-start | bytes 3145736 | tf_op jit(solution)/shard_map/ppermute | solution.py:951
  502.4 47.1 %collective-permute-start.77 = (bf16[256,2048]{1,0:T(8,128)(2,1)}, bf16[256,2048]{1,0:T(8,128)(2,1)}, u32[]{:S(2)}, u32[]{:S(2)}) collective-permute-start(bf16[256,2048]{1,0:T(8,128)(2,1)} %add_convert_fusion.4), channel_id=1, source_target_pairs={{0,1},{1,0},{2,3},{3,2},{4,5},{5,4},{6,7},{7,6},{8,9},{9,8},{10,11... | collective-permute-start | bytes 3145736 | tf_op jit(solution)/shard_map/ppermute | solution.py:951
  554.6 45.2 %collective-permute-start.78 = (bf16[256,2048]{1,0:T(8,128)(2,1)}, bf16[256,2048]{1,0:T(8,128)(2,1)}, u32[]{:S(2)}, u32[]{:S(2)}) collective-permute-start(bf16[256,2048]{1,0:T(8,128)(2,1)} %add_convert_fusion.3), channel_id=1, source_target_pairs={{4,8},{8,4},{5,9},{9,5},{6,10},{10,6},{7,11},{11,7},{20,24},{24,20... | collective-permute-start | bytes 3145736 | tf_op jit(solution)/shard_map/ppermute | solution.py:954
  565.2 37.1 %collective-permute-start.85 = (bf16[256,2048]{1,0:T(8,128)(2,1)}, bf16[256,2048]{1,0:T(8,128)(2,1)}, u32[]{:S(2)}, u32[]{:S(2)}) collective-permute-start(bf16[256,2048]{1,0:T(8,128)(2,1)} %add_convert_fusion), channel_id=1, source_target_pairs={{0,1},{1,0},{2,3},{3,2},{4,5},{5,4},{6,7},{7,6},{8,9},{9,8},{10,11... | collective-permute-start | bytes 3145736 | tf_op jit(solution)/shard_map/ppermute | solution.py:951
  566.7 36.8 %collective-permute-start.84 = (bf16[256,2048]{1,0:T(8,128)(2,1)}, bf16[256,2048]{1,0:T(8,128)(2,1)}, u32[]{:S(2)}, u32[]{:S(2)}) collective-permute-start(bf16[256,2048]{1,0:T(8,128)(2,1)} %add_convert_fusion.1), channel_id=1, source_target_pairs={{0,2},{1,3},{2,0},{3,1},{4,6},{5,7},{6,4},{7,5},{8,10},{9,11},{10,... | collective-permute-start | bytes 3145736 | tf_op jit(solution)/shard_map/ppermute | solution.py:951
  567.3 58.4 %collective-permute-start.83 = (bf16[256,2048]{1,0:T(8,128)(2,1)}, bf16[256,2048]{1,0:T(8,128)(2,1)}, u32[]{:S(2)}, u32[]{:S(2)}) collective-permute-start(bf16[256,2048]{1,0:T(8,128)(2,1)} %add_convert_fusion.2), channel_id=1, source_target_pairs={{0,3},{1,2},{2,1},{3,0},{4,7},{5,6},{6,5},{7,4},{8,11},{9,10},{10,... | collective-permute-start | bytes 3145736 | tf_op jit(solution)/shard_map/ppermute | solution.py:951
  637.4 45.1 %all-to-all-start = ((bf16[16,17,1280]{2,1,0:T(8,128)(2,1)}), bf16[16,17,1280]{2,1,0:T(8,128)(2,1)S(1)}, u32[]{:S(2)}, u32[]{:S(2)}) async-start(bf16[16,17,1280]{2,1,0:T(8,128)(2,1)} %add_convert_fusion.13), calls=%async_computation | async-start | bytes 1966080 | tf_op jit(solution)/shard_map/all_to_all | solution.py:1382
  (215 other events, 3972.2 us)
